TPU v7x, 128 devices: a whole 4x4x4 slice. The times are simulated.
128 devices in a mesh: row: 8 (over x_hi, y), col: 16 (over x_lo, z, core).
Axes of the slice: x: 4 (x_hi: 2, x_lo: 2; x = x_hi * 2 + x_lo), y: 4, z: 4, core: 2. Of those that a mesh axis runs over, the one named last changes fastest.
Arguments:
- matrix: float32 [32768, 8192], P('row', 'col'), may hold values from -6 to 6
- pivots: int32 [1024], replicated, may hold values from 0 to 32767, as said below
- lower_panel: float32 [1024, 32768], P('col', 'row'), as said below
Outputs:
- updated: float32 [32768, 8192], P('row', 'col')
Inputs may be any that keep to these rules, and one draw needn't show every extreme that they name: `pivots`: the 1024 entries are distinct rows of the trailing matrix. For column index r < 1024: lower_panel[r, r] = 1 and lower_panel[k, r] = 0 for k > r.
All inputs are finite; a program needn't handle non-finite values.
Results may differ from a plain program's by a relative error of at most 0.000059.
Values sent between devices are 32-bit elements; how exact they have to be, the bound alone decides.
No kernel may reach another device: no remote copies, remote signals or barrier semaphores. Data moves between devices by JAX's collectives and lax.ppermute only.
A program may use at most 128 MiB of HBM per device.

v0:
```python
import jax
import jax.numpy as jnp
from jax import lax
from jax.sharding import PartitionSpec as P


def spread(value, axis, source):
    kept = jnp.where(lax.axis_index(axis) == source, value, 0).astype(value.dtype)
    return lax.psum(kept, axis)


def displaced_rows(pivots, top):
    whole = jnp.arange(top, dtype=jnp.int32)
    chosen_top = jnp.any(pivots[None, :] == whole[:, None], axis=1)
    spare_rows = jnp.sort(jnp.where(chosen_top, jnp.int32(2**30), whole))
    vacated = jnp.sort(jnp.where(pivots >= top, pivots, jnp.int32(2**30)))
    return (spare_rows, vacated)


def contract(left_block, right_block):
    return lax.dot_general(
        left_block,
        right_block,
        (((0,), (0,)), ((), ())),
        precision=lax.Precision.HIGHEST,
        preferred_element_type=jnp.float32,
    )


def per_device(matrix, pivots, lower_panel):
    top = pivots.shape[0]
    local_rows, local_cols = matrix.shape
    first_row = lax.axis_index("row") * local_rows
    spare_rows, vacated = displaced_rows(pivots, top)
    initial_top = spread(matrix[:top], "row", 0)
    inside = (vacated >= first_row) & (vacated < first_row + local_rows)
    local_target = jnp.where(inside, vacated - first_row, local_rows)
    swapped = matrix.at[local_target].set(
        initial_top[jnp.minimum(spare_rows, top - 1)], mode="drop"
    )
    owned_mask = (pivots >= first_row) & (pivots < first_row + local_rows)
    local_index = jnp.clip(pivots - first_row, 0, local_rows - 1)
    picked = jnp.where(owned_mask[:, None], jnp.take(matrix, local_index, axis=0), 0.0)
    pivot_block = lax.psum(picked, "row")
    product = contract(lax.all_gather(lower_panel, "col", axis=0, tiled=True), pivot_block)
    global_rows = first_row + jnp.arange(local_rows, dtype=jnp.int32)[:, None]
    return jnp.where(global_rows < top, product, swapped - product)


def solution(mesh):
    in_specs = (P("row", "col"), P(), P("col", "row"))
    out_specs = P("row", "col")
    return jax.shard_map(
        per_device, mesh=mesh, in_specs=in_specs, out_specs=out_specs, check_vma=False
    )
```

profile of v0, /device:TPU:1, one launch (start us, length us, event | category | flops | bytes accessed | tf_op | source)
XLA Modules:
  0.0 292.7 jit_solution(3470179886124595553)
XLA Ops:
  7.4 0.0 all-reduce.3.cloned.1.call-start
  7.4 0.0 copy-start.1
  7.4 7.8 %copy.12 = f32[4096,512]{1,0:T(8,128)} copy(f32[4096,512]{1,0:T(8,128)} %param.3) | data formatting | bytes 16777216
  15.1 0.0 copy-done.1
  15.2 7.4 %gather_fusion = f32[1024,512]{1,0:T(8,128)S(1)} fusion(f32[4096,512]{1,0:T(8,128)} %copy.12, s32[1024]{0:T(1024)S(1)} %get-tuple-element.15), kind=kCustom, calls=%fused_computation | custom fusion | bytes 4198400 | tf_op jit(solution)/shard_map/jit(_take)/gather | solution.py:43
  22.6 3.1 %slice_select_fusion = f32[1024,512]{1,0:T(8,128)} fusion(f32[4096,512]{1,0:T(8,128)} %copy.12, pred[]{:T(512)S(6)} %eq.16), kind=kLoop, calls=%fused_computation.8 | loop fusion | flops 524288 | bytes 4194305 | tf_op jit(solution)/shard_map/jit(_where)/select_n | solution.py:8
  25.7 2.0 select_select_fusion
  27.7 0.0 all-reduce.3.cloned.1.call-update
  27.7 0.0 all-gather.2.cloned.1.call-start
  27.7 0.5 all-gather.2.cloned.1.call-update
  28.3 4.4 %sort.21 = (s32[1024]{0:T(1024)S(1)}, s32[1024]{0:T(1024)}) sort(s32[1024]{0:T(1024)S(1)} %get-tuple-element.16, s32[1024]{0:T(1024)S(1)} %iota.18), dimensions={0}, to_apply=%region_1.2 | sort | flops 10240 | bytes 16384 | tf_op jit(solution)/shard_map/jit(sort)/sort | solution.py:16
  32.6 0.6 fusion
  33.2 4.4 %sort.28 = (s32[1024]{0:T(1024)S(1)}, s32[1024]{0:T(1024)}) sort(s32[1024]{0:T(1024)S(1)} %iota_select_fusion, s32[1024]{0:T(1024)S(1)} %iota.20), dimensions={0}, to_apply=%region_4.5 | sort | flops 10240 | bytes 16384 | tf_op jit(solution)/shard_map/jit(sort)/sort | solution.py:15
  37.6 178.3 %all-reduce.3.cloned.1.call-done = (f32[1024,512]{1,0:T(8,128)}, f32[1024,512]{1,0:T(8,128)}) async-done(((f32[1024,512]{1,0:T(8,128)}, f32[1024,512]{1,0:T(8,128)}), (f32[1024,512]{1,0:T(8,128)}, f32[1024,512]{1,0:T(8,128)})) %all-reduce.3.cloned.1.call-update) | async-done | bytes 4194320 | tf_op jit(solution)/shard_map/psum | solution.py:9
  215.9 20.0 %scatter_custom_fusion = f32[4096,512]{1,0:T(8,128)} fusion(f32[4096,512]{1,0:T(8,128)} %copy.12, s32[1024]{0:T(1024)S(1)} %get-tuple-element.17, f32[1024,512]{1,0:T(8,128)} %get-tuple-element.11, s32[1024]{0:T(1024)S(1)} %get-tuple-element.18), kind=kCustom, calls=%fused_computation.6 | custom fusion | bytes 8388608 | tf_op jit(solution)/shard_map/scatter | solution.py:38
  235.8 0.0 copy-start
  235.8 9.1 %copy.6 = f32[4096,512]{0,1:T(8,128)} copy(f32[4096,512]{1,0:T(8,128)} %scatter_custom_fusion) | data formatting | bytes 16777216 | tf_op jit(solution)/shard_map/scatter | solution.py:38
  244.9 0.0 all-gather.2.cloned.1.call-done
  244.9 0.0 copy-done
  244.9 31.4 %subtract_select_fusion = f32[4096,512]{0,1:T(8,128)} fusion(f32[4096,512]{0,1:T(8,128)} %copy.6, f32[1024,512]{1,0:T(8,128)S(1)} %copy-done, f32[1024,4096]{1,0:T(8,128)} %all-gather.2.cloned.1.call-done, pred[4096]{0:T(1024)(128)(4,1)S(1)} %add_compare_fusion), kind=kOutput, calls=%fused_computation.3 | convolution fusion | flops 25773998080 | bytes 35655680 | tf_op jit(solution)/shard_map/dot_general | solution.py:21
  276.3 8.9 %copy.7 = f32[4096,512]{1,0:T(8,128)} copy(f32[4096,512]{0,1:T(8,128)} %subtract_select_fusion) | data formatting | bytes 16777216 | tf_op jit(solution)/shard_map/jit(_where)/select_n | solution.py:47
  (7 shorter events, 0.1 us)
Async XLA Ops:
  7.4 208.5 %all-reduce.3.cloned.1.call-start = ((), (), s32[]{:S(2)}) async-start(), calls=%async_computation.1 | async-start | bytes 8388608 | tf_op jit(solution)/shard_map/psum | solution.py:9
  7.4 7.8 %copy-start.1 = (s32[1024]{0:T(1024)S(1)}, s32[1024]{0:T(1024)}, u32[]{:S(2)}) copy-start(s32[1024]{0:T(1024)} %param.4) | copy-start | bytes 12292
  27.7 217.2 %all-gather.2.cloned.1.call-start = ((), (), s32[]{:S(2)}) async-start(), calls=%async_computation | async-start | bytes 17825792 | tf_op jit(solution)/shard_map/all_gather | solution.py:45
  235.8 9.1 %copy-start = (f32[1024,512]{1,0:T(8,128)S(1)}, f32[1024,512]{1,0:T(8,128)}, u32[]{:S(2)}) copy-start(f32[1024,512]{1,0:T(8,128)} %get-tuple-element.12) | copy-start | bytes 6291460
Sparse Core Ops, SparseCore 0:
  27.8 187.9 all-reduce.2
Sparse Core Ops, SparseCore 1:
  29.9 131.6 all-gather.1
where the time goes:
time: 293 us
  waiting for transfers between devices  179 us (61%)
  local copies, waits for them, and re-layouts  53.2 us (18%)
  matrix products  31.4 us (11%)
  between operations  14.9 us (5%)
  other arithmetic  14.4 us (5%)
    psum x1, waiting for transfers between devices, spread(): return lax.psum(kept, axis)  178 us
    dot_general x1, matrix products, contract(): lax.dot_general(left_block, right_block, (((0,), (0,)), ((), ())), precis...  31.4 us
    scatter x2, local copies, waits for them, and re-layouts, per_device(): matrix.at[local_target]  29 us
    select_n x1, local copies, waits for them, and re-layouts, per_device(): return jnp.where(global_rows < top, product, swapped - product)  8.94 us
    unnamed x5, local copies, waits for them, and re-layouts  7.78 us
    gather x1, local copies, waits for them, and re-layouts, per_device(): jnp.take(matrix, local_index, axis=0)  7.4 us
  transfers between devices with their start and end apart: 2, of which 1 were waited for; matrix products, arithmetic and copies ran while one was open for 13% of the time, Pallas kernels for 0%

commit v1 on v0

v1 whole, which is shorter than its diff:
```python
import functools

import jax
import jax.numpy as jnp
from jax import lax
from jax.experimental import pallas as pl
from jax.experimental.pallas import tpu as pltpu
from jax.sharding import PartitionSpec as P


NZ, NY, NX, NC = 4, 4, 2, 2


def col_shift(dx, dz, dc):
    pairs = []
    for i in range(NX * NZ * NC):
        x, z, c = i // 8, (i // 2) % 4, i % 2
        pairs.append((i, ((x + dx) % 2) * 8 + ((z + dz) % 4) * 2 + (c + dc) % 2))
    return pairs


def row_shift(dx, dy, keep=lambda x: True):
    pairs = []
    for i in range(NX * NY):
        x, y = i // 4, i % 4
        if keep(x):
            pairs.append((i, ((x + dx) % 2) * 4 + (y + dy) % 4))
    return pairs


def send_col(value, dx, dz, dc=0):
    return lax.ppermute(value, "col", col_shift(dx, dz, dc))


def send_row(value, dx, dy, keep=lambda x: True):
    return lax.ppermute(value, "row", row_shift(dx, dy, keep))


FIRST = [(0, 0), (1, 0), (0, -1), (0, 1)]
SECOND = [(0, 2), (1, -1), (1, 1), (1, 2)]
KP = 64
MB = 512


def split(value):
    hi = value.astype(jnp.bfloat16)
    return hi, (value - hi.astype(jnp.float32)).astype(jnp.bfloat16)


def prep_body(order_ref, *refs):
    slices, (b1h, b1l, b2h, b2l), full = refs[:8], refs[8:12], refs[12]
    y = order_ref[16]
    for d in range(4):
        t = lax.rem(y + d, 4)
        for h in range(2):
            full[pl.ds(pl.multiple_of(t * 256 + h * 128, 128), 128), :] = slices[2 * d + h][...]
    n1 = 2 * len(FIRST)
    for j in range(16):
        rows = full[pl.ds(pl.multiple_of(order_ref[j] * KP, KP), KP), :]
        hi, lo = split(rows)
        bh, bl, k = (b1h, b1l, j) if j < n1 else (b2h, b2l, j - n1)
        bh[k * KP : (k + 1) * KP, :] = hi
        bl[k * KP : (k + 1) * KP, :] = lo


def prep(order, slices):
    n = slices[0].shape[1]
    k1, k2 = 2 * len(FIRST) * KP, 2 * len(SECOND) * KP
    out = [jax.ShapeDtypeStruct((k, n), jnp.bfloat16) for k in (k1, k1, k2, k2)]
    vm = pl.BlockSpec(memory_space=pltpu.VMEM)
    return pl.pallas_call(
        prep_body,
        in_specs=[pl.BlockSpec(memory_space=pltpu.SMEM)] + [vm] * len(slices),
        out_specs=[vm] * 4,
        out_shape=out,
        scratch_shapes=[pltpu.VMEM((1024, n), jnp.float32)],
        cost_estimate=pl.CostEstimate(flops=0, bytes_accessed=4 << 20, transcendentals=0),
        name="prep",
    )(order, *slices)


def product(bh, bl, ah, al):
    dot = functools.partial(
        lax.dot_general,
        dimension_numbers=(((0,), (0,)), ((), ())),
        preferred_element_type=jnp.float32,
    )
    return dot(ah[...], bh[...]) + dot(ah[...], bl[...]) + dot(al[...], bh[...])


def load_pieces(pieces, ah, al):
    for j, piece in enumerate(pieces):
        hi, lo = split(piece[...])
        ah[j * KP : (j + 1) * KP, :] = hi
        al[j * KP : (j + 1) * KP, :] = lo


def first_body(info, starts, keys, spares, *refs):
    pieces, (bh, bl, mat, top, out, ah, al) = refs[:8], refs[8:]
    block = pl.program_id(0)
    root = info[0]
    in_top = (root == 1) & (block < 1024 // MB)
    load_pieces(pieces, ah, al)
    out[...] = jnp.where(in_top, 0.0, mat[...])
    lo, hi = starts[block], starts[block + 1]

    @pl.when(root == 1)
    def _():
        def patch(k, carry):
            out[pl.ds(keys[k] - block * MB, 1), :] = top[pl.ds(spares[k], 1), :]
            return carry

        lax.fori_loop(lo, hi, patch, 0)

    @pl.when(root == 0)
    def _():
        def patch(k, carry):
            out[pl.ds(keys[k] - block * MB, 1), :] = jnp.zeros((1, out.shape[1]), jnp.float32)
            return carry

        lax.fori_loop(lo, hi, patch, 0)

    out[...] += jnp.where(in_top, 1.0, -1.0) * product(bh, bl, ah, al)


def second_body(nblk, info, starts, keys, slots, *refs):
    left, right, rest = refs[:8], refs[8:16], refs[16:]
    (bh, bl, prev), parts, (out, ah, al, disp) = rest[:3], rest[3:-4], rest[-4:]
    block = pl.program_id(0)
    root = info[0]
    in_top = (root == 1) & (block < 1024 // MB)

    @pl.when(block == 0)
    def _():
        at = 0
        for part in parts:
            disp[at : at + part.shape[0], :] = part[...]
            at += part.shape[0]

    @pl.when(block < nblk // 2)
    def _():
        load_pieces(left, ah, al)

    @pl.when(block >= nblk // 2)
    def _():
        load_pieces(right, ah, al)

    out[...] = prev[...] + jnp.where(in_top, 1.0, -1.0) * product(bh, bl, ah, al)

    @pl.when(root == 0)
    def _():
        def patch(k, carry):
            out[pl.ds(keys[k] - block * MB, 1), :] += disp[pl.ds(slots[k], 1), :]
            return carry

        lax.fori_loop(starts[block], starts[block + 1], patch, 0)


def const(shape):
    return pl.BlockSpec(shape, lambda i, *_: (0, 0), pipeline_mode=pl.Buffered(1))


def run(body, scalars, pieces, piece_specs, bh, bl, base, extra, scratch, aliases):
    rows, n = base.shape
    k = bh.shape[0]
    return pl.pallas_call(
        body,
        grid_spec=pltpu.PrefetchScalarGridSpec(
            num_scalar_prefetch=4,
            grid=(rows // MB,),
            in_specs=[
                *piece_specs,
                const(bh.shape),
                const(bl.shape),
                pl.BlockSpec((MB, n), lambda i, *_: (i, 0)),
                *[const(e[1]) for e in extra],
            ],
            out_specs=pl.BlockSpec((MB, n), lambda i, *_: (i, 0)),
            scratch_shapes=[pltpu.VMEM((k, MB), jnp.bfloat16)] * 2 + scratch,
        ),
        out_shape=jax.ShapeDtypeStruct(base.shape, jnp.float32),
        input_output_aliases=aliases,
        cost_estimate=pl.CostEstimate(
            flops=6 * rows * n * k, bytes_accessed=4 * (rows * k + 2 * rows * n), transcendentals=0
        ),
    )(*scalars, *pieces, bh, bl, base, *[e[0] for e in extra])


def step(matrix, pivots, lower_panel):
    top = pivots.shape[0]
    local_rows, n = matrix.shape
    row, col = lax.axis_index("row"), lax.axis_index("col")
    x_hi, y = row // 4, row % 4
    x_lo, z, core = col // 8, (col // 2) % 4, col % 2
    first_row = row * local_rows
    root = row == 0
    half = local_rows // 2

    xs = send_col(lower_panel, 1, 0)
    zm = send_col(lower_panel, 0, 1)
    zp = send_col(lower_panel, 0, -1)

    tops = jnp.arange(top, dtype=jnp.int32)
    chosen = jnp.any(pivots[None, :] == tops[:, None], axis=1)
    away = pivots >= top
    rank = jnp.sum((away & (pivots[None, :] < pivots[:, None])).astype(jnp.int32), axis=1)
    before = jnp.sum((~chosen[None, :] & (tops[None, :] < tops[:, None])).astype(jnp.int32), axis=1)
    hit = ~chosen[None, :] & (before[None, :] == rank[:, None])
    spare = jnp.sum(jnp.where(hit, tops[None, :], 0), axis=1)
    owned = (pivots >= first_row) & (pivots < first_row + local_rows)
    index = jnp.where(owned, pivots - first_row, jnp.where(root, spare, 0))
    live = owned | root

    quarter, eighth = top // 4, top // 8

    def gathered(h):
        at = [((y + d) % 4) * quarter + h * eighth for d in (2, 1, 3, 0)]
        idx = jnp.concatenate([lax.dynamic_slice(index, (s,), (eighth,)) for s in at])
        msk = jnp.concatenate([lax.dynamic_slice(live, (s,), (eighth,)) for s in at])
        got = jnp.take(matrix, idx, axis=0, mode="clip")
        got = [jnp.where(msk[i * eighth : (i + 1) * eighth, None], got[i * eighth : (i + 1) * eighth], 0.0) for i in range(4)]
        s = at[3]
        root_owned = (lax.dynamic_slice(pivots, (s,), (eighth,)) < local_rows)[:, None]
        return got, root_owned

    def exchange(got, root_owned):
        m2 = send_row(got[0], 0, 2)
        m1 = send_row(got[1], 0, 1)
        m3 = send_row(got[2], 0, -1)
        pivot_sum, disp = 0.0, 0.0
        for message, source in ((got[3], y), (m1, (y + 3) % 4), (m2, (y + 2) % 4), (m3, (y + 1) % 4)):
            from_root = (x_hi == 0) & (source == 0)
            is_disp = from_root & ~root_owned
            pivot_sum = pivot_sum + jnp.where(is_disp, 0.0, message)
            disp = disp + jnp.where(is_disp, message, 0.0)
        return pivot_sum, disp

    got_a, owned_a = gathered(0)
    got_b, owned_b = gathered(1)
    part_a, disp_a = exchange(got_a, owned_a)
    part_b, disp_b = exchange(got_b, owned_b)
    full_a = part_a + send_row(part_a, 1, 0)
    full_b = part_b + send_row(part_b, 1, 0)
    disp = jnp.concatenate([disp_a, disp_b], axis=0)
    cross = send_row(disp, 1, 0, lambda x: x == 0)
    disp = jnp.where(x_hi == 0, disp, cross)
    lo_a, hi_a = send_row(full_a, 0, 1), send_row(full_a, 0, -1)
    lo_b, hi_b = send_row(full_b, 0, 1), send_row(full_b, 0, -1)
    far_a = send_row(lo_a, 0, 1)
    far_b = send_row(hi_b, 0, -1)
    lo_d, hi_d = send_row(disp, 0, 1), send_row(disp, 0, -1)
    far_da = send_row(lo_d[:eighth], 0, 1)
    far_db = send_row(hi_d[eighth:], 0, -1)
    pivot_slices = [full_a, full_b, hi_a, hi_b, far_a, far_b, lo_a, lo_b]
    disp_parts = [disp, hi_d, far_da, far_db, lo_d]

    up2 = send_col(jnp.concatenate([zm[:, :half], xs[:, :half]], axis=0), 0, 1)
    dn2 = send_col(jnp.concatenate([zp[:, half:], xs[:, half:]], axis=0), 0, -1)
    x2 = send_col(jnp.concatenate([zp[:, :half], zm[:, half:]], axis=0), 1, 0)
    up3 = send_col(up2[KP:], 0, 1)
    dn3 = send_col(dn2[KP:], 0, -1)
    own_o = send_col(lower_panel, 0, 0, 1)
    xs_o, zm_o, zp_o = (send_col(v, 0, 0, 1) for v in (xs, zm, zp))
    x2_o, up2_o, dn2_o = (send_col(v, 0, 0, 1) for v in (x2, up2, dn2))
    up3_o, dn3_o = (send_col(v, 0, 0, 1) for v in (up3, dn3))

    offsets = [(dx, dz, dc) for dx, dz in FIRST + SECOND for dc in (0, 1)]
    order = [((x_lo + dx) % 2) * 8 + ((z + dz) % 4) * 2 + (core + dc) % 2 for dx, dz, dc in offsets]
    order = jnp.stack(order + [y]).astype(jnp.int32)

    mine = owned & away
    key = jnp.where(mine, pivots - first_row, jnp.int32(2**30))
    slot_row = ((tops // quarter - y) % 4) * quarter + tops % quarter
    keys, slots, spares = lax.sort((key, slot_row, spare), num_keys=1)
    edges = jnp.arange(local_rows // MB + 1, dtype=jnp.int32) * MB
    starts = jnp.sum((key[None, :] < edges[:, None]).astype(jnp.int32), axis=1)
    info = root.astype(jnp.int32).reshape(1)

    b1h, b1l, b2h, b2l = prep(order, pivot_slices)
    nblk = local_rows // MB
    hb = nblk // 2
    whole = pl.BlockSpec((KP, MB), lambda i, *_: (0, i))
    out = run(
        first_body, (info, starts, keys, spares),
        [lower_panel, own_o, xs, xs_o, zm, zm_o, zp, zp_o], [whole] * 8,
        b1h, b1l, matrix, [(matrix, (top, n))], [], {},
    )

    def left(r):
        return pl.BlockSpec((KP, MB), lambda i, *_: (r, jnp.minimum(i, hb - 1)))

    def right(r):
        return pl.BlockSpec((KP, MB), lambda i, *_: (r, jnp.maximum(i - hb, 0)))

    pieces = [up2, up2_o, up2, up2_o, x2, x2_o, up3, up3_o]
    specs = [left(r) for r in (0, 0, 1, 1, 0, 0, 0, 0)]
    pieces += [dn2, dn2_o, x2, x2_o, dn2, dn2_o, dn3, dn3_o]
    specs += [right(r) for r in (0, 0, 1, 1, 1, 1, 0, 0)]
    return run(
        functools.partial(second_body, nblk), (info, starts, keys, slots),
        pieces, specs, b2h, b2l, out, [(d, d.shape) for d in disp_parts],
        [pltpu.VMEM((top, n), jnp.float32)], {4 + 16 + 2: 0},
    )


def solution(mesh):
    in_specs = (P("row", "col"), P(), P("col", "row"))
    out_specs = P("row", "col")
    return jax.shard_map(step, mesh=mesh, in_specs=in_specs, out_specs=out_specs, check_vma=False)
```

time: 293 us -> 207 us (0.71)
  waiting for transfers between devices: 179 us -> 81 us
  starting transfers between devices: 0.05 us -> 55 us
  local copies, waits for them, and re-layouts: 53.2 us -> 13.9 us
  Pallas kernels: 0 us -> 38.1 us
  matrix products: 31.4 us -> 0 us
  between operations: 14.9 us -> 0.66 us
    psum x1 -> x0, waiting for transfers between devices: 178 us -> none  [spread(): return lax.psum(kept, axis)]
    ppermute x0 -> x36, waiting for transfers between devices: none -> 81 us  [the longest x19 69.2 us: send_row(): return lax.ppermute(value, 'row', row_shift(dx, dy, keep))]
    ppermute x0 -> x36, starting transfers between devices: none -> 55 us  [the longest x17 31.3 us: send_col(): return lax.ppermute(value, 'col', col_shift(dx, dz, dc))]
    pallas_call x0 -> x3, Pallas kernels: none -> 38.1 us  [the longest x2 35 us: run(): pl.pallas_call(body, grid_spec=pltpu.PrefetchScalarGridSpec(num_scalar_pr...]
    dot_general x1 -> x0, matrix products: 31.4 us -> none  [contract(): lax.dot_general(left_block, right_block, (((0,), (0,)), ((), ())), precis...]
    scatter x2 -> x0, local copies, waits for them, and re-layouts: 29 us -> none  [per_device(): matrix.at[local_target]]
    select_n x1 -> x0, local copies, waits for them, and re-layouts: 8.94 us -> none  [per_device(): return jnp.where(global_rows < top, product, swapped - product)]
    unnamed x5 -> x48, local copies, waits for them, and re-layouts: 7.78 us -> 0.09 us
  transfers between devices with their start and end apart: 2 -> 36, of which waited for: 1 -> 14; matrix products, arithmetic and copies ran while one was open for 13% -> 9% of each run, Pallas kernels for 0% -> 10%
where the time goes in v1:
time: 207 us; the launch traced here: 205 us
  waiting for transfers between devices  81 us (39%)
  starting transfers between devices  55 us (27%)
  Pallas kernels  38.1 us (18%)
  other arithmetic  16.4 us (8%)
  local copies, waits for them, and re-layouts  13.9 us (7%)
    ppermute x19, waiting for transfers between devices, send_row(): return lax.ppermute(value, 'row', row_shift(dx, dy, keep))  69.2 us
    pallas_call x2, Pallas kernels, run(): pl.pallas_call(body, grid_spec=pltpu.PrefetchScalarGridSpec(num_scalar_pr...  35 us
    ppermute x17, starting transfers between devices, send_col(): return lax.ppermute(value, 'col', col_shift(dx, dz, dc))  31.3 us
    ppermute x19, starting transfers between devices, send_row(): return lax.ppermute(value, 'row', row_shift(dx, dy, keep))  23.7 us
    ppermute x17, waiting for transfers between devices, send_col(): return lax.ppermute(value, 'col', col_shift(dx, dz, dc))  11.8 us
    gather x2, local copies, waits for them, and re-layouts, gathered(): got = jnp.take(matrix, idx, axis=0, mode='clip')  10.9 us
    sort x1, other arithmetic, step(): keys, slots, spares = lax.sort((key, slot_row, spare), num_keys=1)  4.44 us
  transfers between devices with their start and end apart: 36, of which 14 were waited for; matrix products, arithmetic and copies ran while one was open for 9% of the time, Pallas kernels for 10%

profile of v1, /device:TPU:1, one launch (start us, length us, event | category | flops | bytes accessed | tf_op | source)
XLA Modules:
  0.0 205.1 jit_solution(16448709410751347054)
XLA Ops:
  5.6 5.4 %gather_fusion.1 = f32[512,512]{1,0:T(8,128)S(1)} fusion(f32[4096,512]{1,0:T(8,128)} %refs_11_.1, s32[1024]{0:T(1024)S(1)} %pad_clamp_fusion), kind=kCustom, calls=%fused_computation.1 | custom fusion | bytes 2099200 | tf_op jit(solution)/shard_map/jit(_take)/gather | solution.py:220
  12.0 2.1 %collective-permute-start.17 = (f32[128,512]{1,0:T(8,128)}, f32[128,512]{1,0:T(8,128)}, u32[]{:S(2)}, u32[]{:S(2)}) collective-permute-start(f32[128,512]{1,0:T(8,128)} %get-tuple-element.30), channel_id=1, source_target_pairs={{0,16},{16,32},{32,48},{48,0},{64,80},{80,96},{96,112},{112,64},{1... | collective-permute-start | bytes 786440 | tf_op jit(solution)/shard_map/ppermute | solution.py:36
  14.1 2.6 %collective-permute-start.18 = (f32[128,512]{1,0:T(8,128)}, f32[128,512]{1,0:T(8,128)}, u32[]{:S(2)}, u32[]{:S(2)}) collective-permute-start(f32[128,512]{1,0:T(8,128)} %get-tuple-element.31), channel_id=1, source_target_pairs={{0,32},{16,48},{32,0},{48,16},{64,96},{80,112},{96,64},{112,80},{1... | collective-permute-start | bytes 786440 | tf_op jit(solution)/shard_map/ppermute | solution.py:36
  17.8 5.5 %gather_fusion = f32[512,512]{1,0:T(8,128)S(1)} fusion(f32[4096,512]{1,0:T(8,128)} %refs_11_.1, s32[1024]{0:T(1024)S(1)} %pad_clamp_fusion.1), kind=kCustom, calls=%fused_computation | custom fusion | bytes 2099200 | tf_op jit(solution)/shard_map/jit(_take)/gather | solution.py:220
  26.4 1.7 collective-permute-start.15
  28.4 3.8 %collective-permute-start.4 = (f32[64,4096]{1,0:T(8,128)S(1)}, f32[64,4096]{1,0:T(8,128)S(1)}, u32[]{:S(2)}, u32[]{:S(2)}) collective-permute-start(f32[64,4096]{1,0:T(8,128)S(1)} %copy-done.9), channel_id=1, source_target_pairs={{0,6},{1,7},{2,0},{3,1},{4,2},{5,3},{6,4},{7,5},{8,14},{9,15},{10,... | collective-permute-start | bytes 3145736 | tf_op jit(solution)/shard_map/ppermute | solution.py:32
  34.4 5.2 %collective-permute-done.14 = f32[128,512]{1,0:T(8,128)} collective-permute-done((f32[128,512]{1,0:T(8,128)}, f32[128,512]{1,0:T(8,128)}, u32[]{:S(2)}, u32[]{:S(2)}) %collective-permute-start.14) | collective-permute-done | bytes 262176 | tf_op jit(solution)/shard_map/ppermute | solution.py:36
  40.9 4.7 %collective-permute-start.31 = (f32[256,512]{1,0:T(8,128)S(1)}, f32[256,512]{1,0:T(8,128)S(1)}, u32[]{:S(2)}, u32[]{:S(2)}) collective-permute-start(f32[256,512]{1,0:T(8,128)S(1)} %pad_maximum_fusion.3), channel_id=1, source_target_pairs={{0,64},{16,80},{32,96},{48,112},{1,65},{17,81},{33,97},{49,113},{2... | collective-permute-start | bytes 1572872 | tf_op jit(solution)/shard_map/ppermute | solution.py:36
  46.0 3.0 %collective-permute-start.16 = (f32[128,512]{1,0:T(8,128)S(1)}, f32[128,512]{1,0:T(8,128)S(1)}, u32[]{:S(2)}, u32[]{:S(2)}) collective-permute-start(f32[128,512]{1,0:T(8,128)S(1)} %get-tuple-element.27), channel_id=1, source_target_pairs={{0,64},{16,80},{32,96},{48,112},{64,0},{80,16},{96,32},{112,48},{1... | collective-permute-start | bytes 786440 | tf_op jit(solution)/shard_map/ppermute | solution.py:36
  49.0 34.4 %collective-permute-done.20 = f32[128,512]{1,0:T(8,128)S(1)} collective-permute-done((f32[128,512]{1,0:T(8,128)S(1)}, f32[128,512]{1,0:T(8,128)S(1)}, u32[]{:S(2)}, u32[]{:S(2)}) %collective-permute-start.20) | collective-permute-done | bytes 262176 | tf_op jit(solution)/shard_map/ppermute | solution.py:36
  83.3 1.6 collective-permute-start
  85.0 3.9 %collective-permute-done.16 = f32[128,512]{1,0:T(8,128)S(1)} collective-permute-done((f32[128,512]{1,0:T(8,128)S(1)}, f32[128,512]{1,0:T(8,128)S(1)}, u32[]{:S(2)}, u32[]{:S(2)}) %collective-permute-start.16) | collective-permute-done | bytes 262176 | tf_op jit(solution)/shard_map/ppermute | solution.py:36
  89.0 2.4 %collective-permute-start.27 = (f32[64,4096]{1,0:T(8,128)S(1)}, f32[64,4096]{1,0:T(8,128)S(1)}, u32[]{:S(2)}, u32[]{:S(2)}) collective-permute-start(f32[64,4096]{1,0:T(8,128)S(1)} %copy-done.9), channel_id=1, source_target_pairs={{0,1},{1,0},{2,3},{3,2},{4,5},{5,4},{6,7},{7,6},{8,9},{9,8},{10,11... | collective-permute-start | bytes 3145736 | tf_op jit(solution)/shard_map/ppermute | solution.py:32
  91.5 3.0 %collective-permute-start.22 = (f32[128,512]{1,0:T(8,128)S(1)}, f32[128,512]{1,0:T(8,128)S(1)}, u32[]{:S(2)}, u32[]{:S(2)}) collective-permute-start(f32[128,512]{1,0:T(8,128)S(1)} %add.418.refs_1_), channel_id=1, source_target_pairs={{0,48},{16,0},{32,16},{48,32},{64,112},{80,64},{96,80},{112,96},{1... | collective-permute-start | bytes 786440 | tf_op jit(solution)/shard_map/ppermute | solution.py:36
  95.1 5.0 %collective-permute-done.22.refs_3_ = f32[128,512]{1,0:T(8,128)S(1)} collective-permute-done((f32[128,512]{1,0:T(8,128)S(1)}, f32[128,512]{1,0:T(8,128)S(1)}, u32[]{:S(2)}, u32[]{:S(2)}) %collective-permute-start.22) | collective-permute-done | bytes 262176 | tf_op jit(solution)/shard_map/ppermute | solution.py:36
  100.1 3.4 %collective-permute-start.21 = (f32[128,512]{1,0:T(8,128)S(1)}, f32[128,512]{1,0:T(8,128)S(1)}, u32[]{:S(2)}, u32[]{:S(2)}) collective-permute-start(f32[128,512]{1,0:T(8,128)S(1)} %add.406.refs_0_), channel_id=1, source_target_pairs={{0,48},{16,0},{32,16},{48,32},{64,112},{80,64},{96,80},{112,96},{1... | collective-permute-start | bytes 786440 | tf_op jit(solution)/shard_map/ppermute | solution.py:36
  103.5 5.5 %collective-permute-done.23.refs_6_ = f32[128,512]{1,0:T(8,128)S(1)} collective-permute-done((f32[128,512]{1,0:T(8,128)S(1)}, f32[128,512]{1,0:T(8,128)S(1)}, u32[]{:S(2)}, u32[]{:S(2)}) %collective-permute-start.23) | collective-permute-done | bytes 262176 | tf_op jit(solution)/shard_map/ppermute | solution.py:36
  109.0 3.8 %collective-permute-start.9 = (f32[128,2048]{1,0:T(8,128)S(1)}, f32[128,2048]{1,0:T(8,128)S(1)}, u32[]{:S(2)}, u32[]{:S(2)}) collective-permute-start(f32[128,2048]{1,0:T(8,128)S(1)} %pad_maximum_fusion.2), channel_id=1, source_target_pairs={{0,6},{1,7},{2,0},{3,1},{4,2},{5,3},{6,4},{7,5},{8,14},{9,15},{10,... | collective-permute-start | bytes 3145736 | tf_op jit(solution)/shard_map/ppermute | solution.py:32
  115.1 5.1 %collective-permute-done.33.refs_23_ = f32[256,512]{1,0:T(8,128)S(1)} collective-permute-done((f32[256,512]{1,0:T(8,128)S(1)}, f32[256,512]{1,0:T(8,128)S(1)}, u32[]{:S(2)}, u32[]{:S(2)}) %collective-permute-start.33) | collective-permute-done | bytes 524320 | tf_op jit(solution)/shard_map/ppermute | solution.py:36
  121.9 2.0 collective-permute-done.24.refs_4_
  124.0 3.2 %collective-permute-start.28 = (f32[64,4096]{1,0:T(8,128)S(1)}, f32[64,4096]{1,0:T(8,128)S(1)}, u32[]{:S(2)}, u32[]{:S(2)}) collective-permute-start(f32[64,4096]{1,0:T(8,128)S(1)} %collective-permute-done.1.refs_2_), channel_id=1, source_target_pairs={{0,1},{1,0},{2,3},{3,2},{4,5},{5,4},{6,7},{7,6},{8,9},{9,8},{10,11... | collective-permute-start | bytes 3145736 | tf_op jit(solution)/shard_map/ppermute | solution.py:32
  127.3 1.7 collective-permute-start.29
  129.0 1.7 collective-permute-done.34.refs_21_
  130.7 3.9 %collective-permute-start.30 = (f32[64,4096]{1,0:T(8,128)S(1)}, f32[64,4096]{1,0:T(8,128)S(1)}, u32[]{:S(2)}, u32[]{:S(2)}) collective-permute-start(f32[64,4096]{1,0:T(8,128)S(1)} %collective-permute-done.4.refs_6_), channel_id=1, source_target_pairs={{0,1},{1,0},{2,3},{3,2},{4,5},{5,4},{6,7},{7,6},{8,9},{9,8},{10,11... | collective-permute-start | bytes 3145736 | tf_op jit(solution)/shard_map/ppermute | solution.py:32
  134.9 10.7 %collective-permute-done.2.refs_0_.refs_2_ = f32[128,2048]{1,0:T(8,128)S(1)} collective-permute-done((f32[128,2048]{1,0:T(8,128)S(1)}, f32[128,2048]{1,0:T(8,128)S(1)}, u32[]{:S(2)}, u32[]{:S(2)}) %collective-permute-start.2) | collective-permute-done | bytes 1048608 | tf_op jit(solution)/shard_map/ppermute | solution.py:32
  147.4 3.8 %collective-permute-done.35.refs_22_ = f32[128,512]{1,0:T(8,128)S(1)} collective-permute-done((f32[128,512]{1,0:T(8,128)S(1)}, f32[128,512]{1,0:T(8,128)S(1)}, u32[]{:S(2)}, u32[]{:S(2)}) %collective-permute-start.35) | collective-permute-done | bytes 262176 | tf_op jit(solution)/shard_map/ppermute | solution.py:36
  152.7 3.9 %collective-permute-start.10 = (f32[128,2048]{1,0:T(8,128)S(1)}, f32[128,2048]{1,0:T(8,128)}, u32[]{:S(2)}, u32[]{:S(2)}) collective-permute-start(f32[128,2048]{1,0:T(8,128)S(1)} %collective-permute-done.9.refs_8_.refs_12_), channel_id=1, source_target_pairs={{0,1},{1,0},{2,3},{3,2},{4,5},{5,4},{6,7},{7,6},{8,9},{9,8},{10,11... | collective-permute-start | bytes 3145736 | tf_op jit(solution)/shard_map/ppermute | solution.py:32
  157.8 2.6 %collective-permute-start.6 = (f32[128,2048]{1,0:T(8,128)S(1)}, f32[128,2048]{1,0:T(8,128)}, u32[]{:S(2)}, u32[]{:S(2)}) collective-permute-start(f32[128,2048]{1,0:T(8,128)S(1)} %collective-permute-done.5.refs_4_.refs_10_), channel_id=1, source_target_pairs={{0,1},{1,0},{2,3},{3,2},{4,5},{5,4},{6,7},{7,6},{8,9},{9,8},{10,11... | collective-permute-start | bytes 3145736 | tf_op jit(solution)/shard_map/ppermute | solution.py:32
  160.3 4.4 %sort.31 = (s32[1024]{0:T(1024)}, s32[1024]{0:T(1024)}, s32[1024]{0:T(1024)}, s32[1024]{0:T(1024)}) sort(s32[1024]{0:T(1024)S(1)} %get-tuple-element.55, s32[1024]{0:T(1024)S(1)} %fusion.11, s32[1024]{0:T(1024)S(1)} %select_reduce_fusion, s32[1024]{0:T(1024)S(1)} %iota.21), dimensions={0}, to_apply=%region_5.6 | sort | flops 10240 | bytes 32768 | tf_op jit(solution)/shard_map/sort | solution.py:274
  166.2 3.1 %prep.1 = (bf16[512,512]{1,0:T(8,128)(2,1)}, bf16[512,512]{1,0:T(8,128)(2,1)}, bf16[512,512]{1,0:T(8,128)(2,1)}, bf16[512,512]{1,0:T(8,128)(2,1)}) custom-call(s32[17]{0:T(128)} %stack.71.order_ref, f32[128,512]{1,0:T(8,128)} %copy-done.15, f32[128,512]{1,0:T(8,128)} %copy-done.14, f32[128,512]{1,0:T(8,128)} %copy-done.21, f32[128,512]{1,0:T(8,128)} %copy-done.18, ...), custom_call_target="tpu_custom_call" | custom-call | bytes 4194304 | tf_op jit(solution)/shard_map/prep/pallas_call | solution.py:71
  169.8 18.2 %shard_map.37.refs_18_ = f32[4096,512]{1,0:T(8,128)} custom-call(s32[1]{0:T(128)} %bitcast.info, s32[9]{0:T(128)} %convert_reduce_fusion.2.starts, s32[1024]{0:T(1024)} %get-tuple-element.15.keys, s32[1024]{0:T(1024)} %get-tuple-element.19.spares, f32[64,4096]{1,0:T(8,128)} %refs_0_.1, f32[64,4096]{1,0:T(8,128)} %copy-done.10, f32[64,4096]{1,0:T(8,128)} %copy-done.4, ...), custom_call_target="tpu_custom_call" | custom-call | flops 6442450944 | bytes 25165824 | tf_op jit(solution)/shard_map/pallas_call | solution.py:166
  188.1 16.8 %shard_map.38 = f32[4096,512]{1,0:T(8,128)} custom-call(s32[1]{0:T(128)} %bitcast.info, s32[9]{0:T(128)} %convert_reduce_fusion.2.starts, s32[1024]{0:T(1024)} %get-tuple-element.15.keys, s32[1024]{0:T(1024)} %get-tuple-element.16.slots, f32[128,2048]{1,0:T(8,128)} %copy-done.1, ...), custom_call_target="tpu_custom_call", output_to_operand_aliasing={{}: (22, {})} | custom-call | flops 6442450944 | bytes 25165824 | tf_op jit(solution)/shard_map/pallas_call | solution.py:166
  (132 shorter events, 26.3 us)
Async XLA Ops:
  12.0 14.4 %collective-permute-start.17 = (f32[128,512]{1,0:T(8,128)}, f32[128,512]{1,0:T(8,128)}, u32[]{:S(2)}, u32[]{:S(2)}) collective-permute-start(f32[128,512]{1,0:T(8,128)} %get-tuple-element.30), channel_id=1, source_target_pairs={{0,16},{16,32},{32,48},{48,0},{64,80},{80,96},{96,112},{112,64},{1... | collective-permute-start | bytes 786440 | tf_op jit(solution)/shard_map/ppermute | solution.py:36
  14.1 14.3 %collective-permute-start.18 = (f32[128,512]{1,0:T(8,128)}, f32[128,512]{1,0:T(8,128)}, u32[]{:S(2)}, u32[]{:S(2)}) collective-permute-start(f32[128,512]{1,0:T(8,128)} %get-tuple-element.31), channel_id=1, source_target_pairs={{0,32},{16,48},{32,0},{48,16},{64,96},{80,112},{96,64},{112,80},{1... | collective-permute-start | bytes 786440 | tf_op jit(solution)/shard_map/ppermute | solution.py:36
  16.7 15.4 %collective-permute-start.19 = (f32[128,512]{1,0:T(8,128)S(1)}, f32[128,512]{1,0:T(8,128)}, u32[]{:S(2)}, u32[]{:S(2)}) collective-permute-start(f32[128,512]{1,0:T(8,128)S(1)} %get-tuple-element.32), channel_id=1, source_target_pairs={{0,48},{16,0},{32,16},{48,32},{64,112},{80,64},{96,80},{112,96},{1... | collective-permute-start | bytes 786440 | tf_op jit(solution)/shard_map/ppermute | solution.py:36
  24.3 10.1 %collective-permute-start.13 = (f32[128,512]{1,0:T(8,128)}, f32[128,512]{1,0:T(8,128)}, u32[]{:S(2)}, u32[]{:S(2)}) collective-permute-start(f32[128,512]{1,0:T(8,128)} %get-tuple-element.33), channel_id=1, source_target_pairs={{0,16},{16,32},{32,48},{48,0},{64,80},{80,96},{96,112},{112,64},{1... | collective-permute-start | bytes 786440 | tf_op jit(solution)/shard_map/ppermute | solution.py:36
  24.7 14.9 %collective-permute-start.14 = (f32[128,512]{1,0:T(8,128)}, f32[128,512]{1,0:T(8,128)}, u32[]{:S(2)}, u32[]{:S(2)}) collective-permute-start(f32[128,512]{1,0:T(8,128)} %get-tuple-element.34), channel_id=1, source_target_pairs={{0,32},{16,48},{32,0},{48,16},{64,96},{80,112},{96,64},{112,80},{1... | collective-permute-start | bytes 786440 | tf_op jit(solution)/shard_map/ppermute | solution.py:36
  26.4 13.3 %collective-permute-start.15 = (f32[128,512]{1,0:T(8,128)}, f32[128,512]{1,0:T(8,128)S(1)}, u32[]{:S(2)}, u32[]{:S(2)}) collective-permute-start(f32[128,512]{1,0:T(8,128)} %get-tuple-element.35), channel_id=1, source_target_pairs={{0,48},{16,0},{32,16},{48,32},{64,112},{80,64},{96,80},{112,96},{1... | collective-permute-start | bytes 786440 | tf_op jit(solution)/shard_map/ppermute | solution.py:36
  28.4 66.2 %collective-permute-start.4 = (f32[64,4096]{1,0:T(8,128)S(1)}, f32[64,4096]{1,0:T(8,128)S(1)}, u32[]{:S(2)}, u32[]{:S(2)}) collective-permute-start(f32[64,4096]{1,0:T(8,128)S(1)} %copy-done.9), channel_id=1, source_target_pairs={{0,6},{1,7},{2,0},{3,1},{4,2},{5,3},{6,4},{7,5},{8,14},{9,15},{10,... | collective-permute-start | bytes 3145736 | tf_op jit(solution)/shard_map/ppermute | solution.py:32
  40.9 50.5 %collective-permute-start.31 = (f32[256,512]{1,0:T(8,128)S(1)}, f32[256,512]{1,0:T(8,128)S(1)}, u32[]{:S(2)}, u32[]{:S(2)}) collective-permute-start(f32[256,512]{1,0:T(8,128)S(1)} %pad_maximum_fusion.3), channel_id=1, source_target_pairs={{0,64},{16,80},{32,96},{48,112},{1,65},{17,81},{33,97},{49,113},{2... | collective-permute-start | bytes 1572872 | tf_op jit(solution)/shard_map/ppermute | solution.py:36
  45.6 49.1 %collective-permute-start.1 = (f32[64,4096]{1,0:T(8,128)S(1)}, f32[64,4096]{1,0:T(8,128)S(1)}, u32[]{:S(2)}, u32[]{:S(2)}) collective-permute-start(f32[64,4096]{1,0:T(8,128)S(1)} %copy-done.9), channel_id=1, source_target_pairs={{0,8},{1,9},{2,10},{3,11},{4,12},{5,13},{6,14},{7,15},{8,0},{9,1},... | collective-permute-start | bytes 3145736 | tf_op jit(solution)/shard_map/ppermute | solution.py:32
  46.0 37.3 %collective-permute-start.20 = (f32[128,512]{1,0:T(8,128)S(1)}, f32[128,512]{1,0:T(8,128)S(1)}, u32[]{:S(2)}, u32[]{:S(2)}) collective-permute-start(f32[128,512]{1,0:T(8,128)S(1)} %get-tuple-element.29), channel_id=1, source_target_pairs={{0,64},{16,80},{32,96},{48,112},{64,0},{80,16},{96,32},{112,48},{1... | collective-permute-start | bytes 786440 | tf_op jit(solution)/shard_map/ppermute | solution.py:36
  46.0 43.0 %collective-permute-start.16 = (f32[128,512]{1,0:T(8,128)S(1)}, f32[128,512]{1,0:T(8,128)S(1)}, u32[]{:S(2)}, u32[]{:S(2)}) collective-permute-start(f32[128,512]{1,0:T(8,128)S(1)} %get-tuple-element.27), channel_id=1, source_target_pairs={{0,64},{16,80},{32,96},{48,112},{64,0},{80,16},{96,32},{112,48},{1... | collective-permute-start | bytes 786440 | tf_op jit(solution)/shard_map/ppermute | solution.py:36
  83.3 25.7 %collective-permute-start = (f32[64,4096]{1,0:T(8,128)S(1)}, f32[64,4096]{1,0:T(8,128)S(1)}, u32[]{:S(2)}, u32[]{:S(2)}) collective-permute-start(f32[64,4096]{1,0:T(8,128)S(1)} %copy-done.9), channel_id=1, source_target_pairs={{0,2},{1,3},{2,4},{3,5},{4,6},{5,7},{6,0},{7,1},{8,10},{9,11},{10,... | collective-permute-start | bytes 3145736 | tf_op jit(solution)/shard_map/ppermute | solution.py:32
  89.0 35.0 %collective-permute-start.27 = (f32[64,4096]{1,0:T(8,128)S(1)}, f32[64,4096]{1,0:T(8,128)S(1)}, u32[]{:S(2)}, u32[]{:S(2)}) collective-permute-start(f32[64,4096]{1,0:T(8,128)S(1)} %copy-done.9), channel_id=1, source_target_pairs={{0,1},{1,0},{2,3},{3,2},{4,5},{5,4},{6,7},{7,6},{8,9},{9,8},{10,11... | collective-permute-start | bytes 3145736 | tf_op jit(solution)/shard_map/ppermute | solution.py:32
  94.5 9.0 %collective-permute-start.26 = (f32[128,512]{1,0:T(8,128)S(1)}, f32[128,512]{1,0:T(8,128)S(1)}, u32[]{:S(2)}, u32[]{:S(2)}) collective-permute-start(f32[128,512]{1,0:T(8,128)S(1)} %add.418.refs_1_), channel_id=1, source_target_pairs={{0,16},{16,32},{32,48},{48,0},{64,80},{80,96},{96,112},{112,64},{1... | collective-permute-start | bytes 786440 | tf_op jit(solution)/shard_map/ppermute | solution.py:36
  94.7 14.3 %collective-permute-start.23 = (f32[128,512]{1,0:T(8,128)S(1)}, f32[128,512]{1,0:T(8,128)S(1)}, u32[]{:S(2)}, u32[]{:S(2)}) collective-permute-start(f32[128,512]{1,0:T(8,128)S(1)} %add.406.refs_0_), channel_id=1, source_target_pairs={{0,16},{16,32},{32,48},{48,0},{64,80},{80,96},{96,112},{112,64},{1... | collective-permute-start | bytes 786440 | tf_op jit(solution)/shard_map/ppermute | solution.py:36
  100.1 12.9 %collective-permute-start.21 = (f32[128,512]{1,0:T(8,128)S(1)}, f32[128,512]{1,0:T(8,128)S(1)}, u32[]{:S(2)}, u32[]{:S(2)}) collective-permute-start(f32[128,512]{1,0:T(8,128)S(1)} %add.406.refs_0_), channel_id=1, source_target_pairs={{0,48},{16,0},{32,16},{48,32},{64,112},{80,64},{96,80},{112,96},{1... | collective-permute-start | bytes 786440 | tf_op jit(solution)/shard_map/ppermute | solution.py:36
  103.5 16.7 %collective-permute-start.33 = (f32[256,512]{1,0:T(8,128)S(1)}, f32[256,512]{1,0:T(8,128)S(1)}, u32[]{:S(2)}, u32[]{:S(2)}) collective-permute-start(f32[256,512]{1,0:T(8,128)S(1)} %broadcast_select_fusion.refs_19_), channel_id=1, source_target_pairs={{0,16},{16,32},{32,48},{48,0},{64,80},{80,96},{96,112},{112,64},{1... | collective-permute-start | bytes 1572872 | tf_op jit(solution)/shard_map/ppermute | solution.py:36
  109.0 25.6 %collective-permute-start.9 = (f32[128,2048]{1,0:T(8,128)S(1)}, f32[128,2048]{1,0:T(8,128)S(1)}, u32[]{:S(2)}, u32[]{:S(2)}) collective-permute-start(f32[128,2048]{1,0:T(8,128)S(1)} %pad_maximum_fusion.2), channel_id=1, source_target_pairs={{0,6},{1,7},{2,0},{3,1},{4,2},{5,3},{6,4},{7,5},{8,14},{9,15},{10,... | collective-permute-start | bytes 3145736 | tf_op jit(solution)/shard_map/ppermute | solution.py:32
  113.0 14.3 %collective-permute-start.32 = (f32[256,512]{1,0:T(8,128)S(1)}, f32[256,512]{1,0:T(8,128)S(1)}, u32[]{:S(2)}, u32[]{:S(2)}) collective-permute-start(f32[256,512]{1,0:T(8,128)S(1)} %broadcast_select_fusion.refs_19_), channel_id=1, source_target_pairs={{0,48},{16,0},{32,16},{48,32},{64,112},{80,64},{96,80},{112,96},{1... | collective-permute-start | bytes 1572872 | tf_op jit(solution)/shard_map/ppermute | solution.py:36
  115.0 8.9 %collective-permute-start.24 = (f32[128,512]{1,0:T(8,128)S(1)}, f32[128,512]{1,0:T(8,128)S(1)}, u32[]{:S(2)}, u32[]{:S(2)}) collective-permute-start(f32[128,512]{1,0:T(8,128)S(1)} %collective-permute-done.23.refs_6_), channel_id=1, source_target_pairs={{0,16},{16,32},{32,48},{48,0},{64,80},{80,96},{96,112},{112,64},{1... | collective-permute-start | bytes 786440 | tf_op jit(solution)/shard_map/ppermute | solution.py:36
  120.3 25.4 %collective-permute-start.2 = (f32[128,2048]{1,0:T(8,128)S(1)}, f32[128,2048]{1,0:T(8,128)S(1)}, u32[]{:S(2)}, u32[]{:S(2)}) collective-permute-start(f32[128,2048]{1,0:T(8,128)S(1)} %pad_maximum_fusion), channel_id=1, source_target_pairs={{0,2},{1,3},{2,4},{3,5},{4,6},{5,7},{6,0},{7,1},{8,10},{9,11},{10,... | collective-permute-start | bytes 3145736 | tf_op jit(solution)/shard_map/ppermute | solution.py:32
  124.0 28.4 %collective-permute-start.28 = (f32[64,4096]{1,0:T(8,128)S(1)}, f32[64,4096]{1,0:T(8,128)S(1)}, u32[]{:S(2)}, u32[]{:S(2)}) collective-permute-start(f32[64,4096]{1,0:T(8,128)S(1)} %collective-permute-done.1.refs_2_), channel_id=1, source_target_pairs={{0,1},{1,0},{2,3},{3,2},{4,5},{5,4},{6,7},{7,6},{8,9},{9,8},{10,11... | collective-permute-start | bytes 3145736 | tf_op jit(solution)/shard_map/ppermute | solution.py:32
  127.3 25.4 %collective-permute-start.29 = (f32[64,4096]{1,0:T(8,128)S(1)}, f32[64,4096]{1,0:T(8,128)S(1)}, u32[]{:S(2)}, u32[]{:S(2)}) collective-permute-start(f32[64,4096]{1,0:T(8,128)S(1)} %collective-permute-done.refs_4_), channel_id=1, source_target_pairs={{0,1},{1,0},{2,3},{3,2},{4,5},{5,4},{6,7},{7,6},{8,9},{9,8},{10,11... | collective-permute-start | bytes 3145736 | tf_op jit(solution)/shard_map/ppermute | solution.py:32
  130.7 25.9 %collective-permute-start.30 = (f32[64,4096]{1,0:T(8,128)S(1)}, f32[64,4096]{1,0:T(8,128)S(1)}, u32[]{:S(2)}, u32[]{:S(2)}) collective-permute-start(f32[64,4096]{1,0:T(8,128)S(1)} %collective-permute-done.4.refs_6_), channel_id=1, source_target_pairs={{0,1},{1,0},{2,3},{3,2},{4,5},{5,4},{6,7},{7,6},{8,9},{9,8},{10,11... | collective-permute-start | bytes 3145736 | tf_op jit(solution)/shard_map/ppermute | solution.py:32
  134.6 23.1 %collective-permute-start.5 = (f32[128,2048]{1,0:T(8,128)S(1)}, f32[128,2048]{1,0:T(8,128)S(1)}, u32[]{:S(2)}, u32[]{:S(2)}) collective-permute-start(f32[128,2048]{1,0:T(8,128)S(1)} %pad_maximum_fusion.1), channel_id=1, source_target_pairs={{0,8},{1,9},{2,10},{3,11},{4,12},{5,13},{6,14},{7,15},{8,0},{9,1},... | collective-permute-start | bytes 3145736 | tf_op jit(solution)/shard_map/ppermute | solution.py:32
  151.2 18.1 %collective-permute-start.11 = (f32[64,2048]{1,0:T(8,128)}, f32[64,2048]{1,0:T(8,128)}, u32[]{:S(2)}, u32[]{:S(2)}) collective-permute-start(f32[64,2048]{1,0:T(8,128)} %slice.83), channel_id=1, source_target_pairs={{0,6},{1,7},{2,0},{3,1},{4,2},{5,3},{6,4},{7,5},{8,14},{9,15},{10,... | collective-permute-start | bytes 1572872 | tf_op jit(solution)/shard_map/ppermute | solution.py:32
  152.4 17.1 %collective-permute-start.7 = (f32[64,2048]{1,0:T(8,128)}, f32[64,2048]{1,0:T(8,128)}, u32[]{:S(2)}, u32[]{:S(2)}) collective-permute-start(f32[64,2048]{1,0:T(8,128)} %slice.80), channel_id=1, source_target_pairs={{0,2},{1,3},{2,4},{3,5},{4,6},{5,7},{6,0},{7,1},{8,10},{9,11},{10,... | collective-permute-start | bytes 1572872 | tf_op jit(solution)/shard_map/ppermute | solution.py:32
  152.7 35.4 %collective-permute-start.10 = (f32[128,2048]{1,0:T(8,128)S(1)}, f32[128,2048]{1,0:T(8,128)}, u32[]{:S(2)}, u32[]{:S(2)}) collective-permute-start(f32[128,2048]{1,0:T(8,128)S(1)} %collective-permute-done.9.refs_8_.refs_12_), channel_id=1, source_target_pairs={{0,1},{1,0},{2,3},{3,2},{4,5},{5,4},{6,7},{7,6},{8,9},{9,8},{10,11... | collective-permute-start | bytes 3145736 | tf_op jit(solution)/shard_map/ppermute | solution.py:32
  156.5 31.5 %collective-permute-start.3 = (f32[128,2048]{1,0:T(8,128)S(1)}, f32[128,2048]{1,0:T(8,128)}, u32[]{:S(2)}, u32[]{:S(2)}) collective-permute-start(f32[128,2048]{1,0:T(8,128)S(1)} %collective-permute-done.2.refs_0_.refs_2_), channel_id=1, source_target_pairs={{0,1},{1,0},{2,3},{3,2},{4,5},{5,4},{6,7},{7,6},{8,9},{9,8},{10,11... | collective-permute-start | bytes 3145736 | tf_op jit(solution)/shard_map/ppermute | solution.py:32
  157.8 30.3 %collective-permute-start.6 = (f32[128,2048]{1,0:T(8,128)S(1)}, f32[128,2048]{1,0:T(8,128)}, u32[]{:S(2)}, u32[]{:S(2)}) collective-permute-start(f32[128,2048]{1,0:T(8,128)S(1)} %collective-permute-done.5.refs_4_.refs_10_), channel_id=1, source_target_pairs={{0,1},{1,0},{2,3},{3,2},{4,5},{5,4},{6,7},{7,6},{8,9},{9,8},{10,11... | collective-permute-start | bytes 3145736 | tf_op jit(solution)/shard_map/ppermute | solution.py:32
  169.3 18.8 %collective-permute-start.12 = (f32[64,2048]{1,0:T(8,128)}, f32[64,2048]{1,0:T(8,128)}, u32[]{:S(2)}, u32[]{:S(2)}) collective-permute-start(f32[64,2048]{1,0:T(8,128)} %collective-permute-done.11.refs_14_), channel_id=1, source_target_pairs={{0,1},{1,0},{2,3},{3,2},{4,5},{5,4},{6,7},{7,6},{8,9},{9,8},{10,11... | collective-permute-start | bytes 1572872 | tf_op jit(solution)/shard_map/ppermute | solution.py:32
  169.5 18.6 %collective-permute-start.8 = (f32[64,2048]{1,0:T(8,128)}, f32[64,2048]{1,0:T(8,128)}, u32[]{:S(2)}, u32[]{:S(2)}) collective-permute-start(f32[64,2048]{1,0:T(8,128)} %collective-permute-done.7.refs_6_), channel_id=1, source_target_pairs={{0,1},{1,0},{2,3},{3,2},{4,5},{5,4},{6,7},{7,6},{8,9},{9,8},{10,11... | collective-permute-start | bytes 1572872 | tf_op jit(solution)/shard_map/ppermute | solution.py:32
  (28 other events, 565.0 us)

commit v2 on v0

v2 whole, which is shorter than its diff:
```python
import functools

import jax
import jax.numpy as jnp
from jax import lax
from jax.experimental import pallas as pl
from jax.experimental.pallas import tpu as pltpu
from jax.sharding import PartitionSpec as P


NZ, NY, NX, NC = 4, 4, 2, 2


def col_shift(dx, dz, dc):
    pairs = []
    for i in range(NX * NZ * NC):
        x, z, c = i // 8, (i // 2) % 4, i % 2
        pairs.append((i, ((x + dx) % 2) * 8 + ((z + dz) % 4) * 2 + (c + dc) % 2))
    return pairs


def row_shift(dx, dy, keep=lambda x: True):
    pairs = []
    for i in range(NX * NY):
        x, y = i // 4, i % 4
        if keep(x):
            pairs.append((i, ((x + dx) % 2) * 4 + (y + dy) % 4))
    return pairs


def send_col(value, dx, dz, dc=0):
    return lax.ppermute(value, "col", col_shift(dx, dz, dc))


def send_row(value, dx, dy, keep=lambda x: True):
    return lax.ppermute(value, "row", row_shift(dx, dy, keep))


PIECES = [(0, 0), (1, 0), (0, -1), (0, 1), (0, 2), (1, -1), (1, 1), (1, 2)]
KP = 64
MB = 512
VMEM = pl.BlockSpec(memory_space=pltpu.VMEM)
ANY = pl.BlockSpec(memory_space=pl.ANY)
SMEM = pl.BlockSpec(memory_space=pltpu.SMEM)


def params(mib):
    return pltpu.CompilerParams(vmem_limit_bytes=mib << 20)


def split(value):
    hi = value.astype(jnp.bfloat16)
    return hi, (value - hi.astype(jnp.float32)).astype(jnp.bfloat16)


def gather_body(h, index, where, matrix, *outs):
    y = where[0]
    for out, d in zip(outs, (2, 1, 3, 0)):
        start = lax.rem(y + d, 4) * 256 + h * 128

        def group(g, carry, out=out, start=start):
            rows = []
            for u in range(8):
                i = index[start + g * 8 + u]
                row = matrix[pl.ds(jnp.maximum(i, 0), 1), :]
                rows.append(jnp.where(i >= 0, row, 0.0))
            out[pl.ds(pl.multiple_of(g * 8, 8), 8), :] = jnp.concatenate(rows, axis=0)
            return carry

        lax.fori_loop(0, 16, group, 0)


def gather_rows(h, index, where, matrix):
    n = matrix.shape[1]
    return pl.pallas_call(
        functools.partial(gather_body, h),
        in_specs=[SMEM, SMEM, VMEM],
        out_specs=[VMEM] * 4,
        out_shape=[jax.ShapeDtypeStruct((128, n), jnp.float32)] * 4,
        compiler_params=params(4),
        cost_estimate=pl.CostEstimate(flops=0, bytes_accessed=6 << 20, transcendentals=0),
        name="gather_rows",
    )(index, where, matrix)


def dots(bh, bl, ah, al):
    dot = functools.partial(
        lax.dot_general,
        dimension_numbers=(((0,), (0,)), ((), ())),
        preferred_element_type=jnp.float32,
    )
    return dot(ah, bh) + dot(ah, bl) + dot(al, bh)


def prep_body(order, *refs):
    slices, (bh, bl), full = refs[:8], refs[8:10], refs[10]
    y = order[16]
    for d in range(4):
        t = lax.rem(y + d, 4)
        for h in range(2):
            full[pl.ds(pl.multiple_of(t * 256 + h * 128, 128), 128), :] = slices[2 * d + h][...]
    for j in range(16):
        rows = full[pl.ds(pl.multiple_of(order[j] * KP, KP), KP), :]
        bh[j * KP : (j + 1) * KP, :], bl[j * KP : (j + 1) * KP, :] = split(rows)


def prep(order, slices):
    n = slices[0].shape[1]
    return pl.pallas_call(
        prep_body,
        in_specs=[SMEM] + [VMEM] * len(slices),
        out_specs=[VMEM] * 2,
        out_shape=[jax.ShapeDtypeStruct((1024, n), jnp.bfloat16)] * 2,
        scratch_shapes=[pltpu.VMEM((1024, n), jnp.float32)],
        compiler_params=params(8),
        cost_estimate=pl.CostEstimate(flops=0, bytes_accessed=4 << 20, transcendentals=0),
        name="prep",
    )(order, *slices)


def update_body(nblk, order, starts, keys, spares, slots, *refs):
    common, left, right = refs[:8], refs[8:16], refs[16:24]
    (bh, bl, base, whole), parts, (out, ah, al, disp, top) = refs[24:28], refs[28:-5], refs[-5:]
    block = pl.program_id(0)
    root = order[17]

    @pl.when(block == 0)
    def _():
        at = 0
        for part in parts:
            disp[at : at + part.shape[0], :] = part[...]
            at += part.shape[0]

    @pl.when((block == 0) & (root == 1))
    def _():
        pltpu.sync_copy(whole.at[pl.ds(0, 1024), :], top)

    def load(first, pieces):
        for j, piece in enumerate(pieces, first):
            ah[j * KP : (j + 1) * KP, :], al[j * KP : (j + 1) * KP, :] = split(piece[...])

    load(0, common)

    @pl.when(block < nblk // 2)
    def _():
        load(8, left)

    @pl.when(block >= nblk // 2)
    def _():
        load(8, right)

    in_top = (root == 1) & (block < 1024 // MB)
    acc = dots(bh[...], bl[...], ah[...], al[...])
    out[...] = jnp.where(in_top, 0.0, base[...]) + jnp.where(in_top, 1.0, -1.0) * acc

    def patch(source, rows):
        def one(k, carry):
            r = pl.ds(keys[k] - block * MB, 1)
            out[r, :] += source[pl.ds(rows[k], 1), :] - base[r, :]
            return carry

        lax.fori_loop(starts[block], starts[block + 1], one, 0)

    @pl.when(root == 1)
    def _():
        patch(top, spares)

    @pl.when(root == 0)
    def _():
        patch(disp, slots)


def update(scalars, common, left, right, cuts_l, cuts_r, bh, bl, matrix, parts):
    rows, n = matrix.shape
    nblk = rows // MB
    hb = nblk // 2

    def const(shape):
        return pl.BlockSpec(shape, lambda i, *_: (0, 0), pipeline_mode=pl.Buffered(1))

    specs = [pl.BlockSpec((KP, MB), lambda i, *_: (0, i))] * 8
    specs += [pl.BlockSpec((KP, MB), lambda i, *_, r=r: (r // KP, jnp.minimum(i, hb - 1))) for r in cuts_l]
    specs += [pl.BlockSpec((KP, MB), lambda i, *_, r=r: (r // KP, jnp.maximum(i - hb, 0))) for r in cuts_r]
    specs += [const(bh.shape), const(bl.shape), pl.BlockSpec((MB, n), lambda i, *_: (i, 0)), ANY]
    specs += [const(p.shape) for p in parts]
    return pl.pallas_call(
        functools.partial(update_body, nblk),
        grid_spec=pltpu.PrefetchScalarGridSpec(
            num_scalar_prefetch=5,
            grid=(nblk,),
            in_specs=specs,
            out_specs=pl.BlockSpec((MB, n), lambda i, *_: (i, 0)),
            scratch_shapes=[pltpu.VMEM((1024, MB), jnp.bfloat16)] * 2 + [pltpu.VMEM((1024, n), jnp.float32)] * 2,
        ),
        out_shape=jax.ShapeDtypeStruct(matrix.shape, jnp.float32),
        compiler_params=params(40),
        cost_estimate=pl.CostEstimate(flops=6 * rows * n * 1024, bytes_accessed=32 << 20, transcendentals=0),
        name="update",
    )(*scalars, *common, *left, *right, bh, bl, matrix, matrix, *parts)


def cut_body(r0, ref, out):
    out[...] = ref[r0 : r0 + out.shape[0], :]


def cut(value, r0, count):
    return pl.pallas_call(
        functools.partial(cut_body, r0),
        in_specs=[VMEM],
        out_specs=VMEM,
        out_shape=jax.ShapeDtypeStruct((count, value.shape[1]), value.dtype),
        compiler_params=params(2),
        cost_estimate=pl.CostEstimate(flops=0, bytes_accessed=1 << 19, transcendentals=0),
        name="cut",
    )(value)


def step(matrix, pivots, lower_panel):
    top = pivots.shape[0]
    local_rows, _ = matrix.shape
    row, col = lax.axis_index("row"), lax.axis_index("col")
    x_hi, y = row // 4, row % 4
    x_lo, z, core = col // 8, (col // 2) % 4, col % 2
    first_row = row * local_rows
    root = row == 0
    half = local_rows // 2

    xs = send_col(lower_panel, 1, 0)
    zm = send_col(lower_panel, 0, 1)
    zp = send_col(lower_panel, 0, -1)

    tops = jnp.arange(top, dtype=jnp.int32)
    chosen = jnp.any(pivots[None, :] == tops[:, None], axis=1)
    away = pivots >= top
    rank = jnp.sum((away & (pivots[None, :] < pivots[:, None])).astype(jnp.int32), axis=1)
    before = jnp.sum((~chosen[None, :] & (tops[None, :] < tops[:, None])).astype(jnp.int32), axis=1)
    hit = ~chosen[None, :] & (before[None, :] == rank[:, None])
    spare = jnp.sum(jnp.where(hit, tops[None, :], 0), axis=1)
    owned = (pivots >= first_row) & (pivots < first_row + local_rows)
    index = jnp.where(owned, pivots - first_row, jnp.where(root, spare, -1))

    quarter, eighth = top // 4, top // 8
    where = y.astype(jnp.int32).reshape(1)
    got_a = gather_rows(0, index, where, matrix)
    got_b = gather_rows(1, index, where, matrix)

    def exchange(h, got):
        root_owned = (lax.dynamic_slice(pivots, (y * quarter + h * eighth,), (eighth,)) < local_rows)[:, None]
        m2 = send_row(got[0], 0, 2)
        m1 = send_row(got[1], 0, 1)
        m3 = send_row(got[2], 0, -1)
        pivot_sum, disp = 0.0, 0.0
        for message, source in ((got[3], y), (m1, (y + 3) % 4), (m2, (y + 2) % 4), (m3, (y + 1) % 4)):
            from_root = (x_hi == 0) & (source == 0)
            is_disp = from_root & ~root_owned
            pivot_sum = pivot_sum + jnp.where(is_disp, 0.0, message)
            disp = disp + jnp.where(is_disp, message, 0.0)
        return pivot_sum, disp

    part_a, disp_a = exchange(0, got_a)
    part_b, disp_b = exchange(1, got_b)
    full_a = part_a + send_row(part_a, 1, 0)
    full_b = part_b + send_row(part_b, 1, 0)
    disp = jnp.concatenate([disp_a, disp_b], axis=0)
    cross = send_row(disp, 1, 0, lambda x: x == 0)
    disp = jnp.where(x_hi == 0, disp, cross)
    lo_a, hi_a = send_row(full_a, 0, 1), send_row(full_a, 0, -1)
    lo_b, hi_b = send_row(full_b, 0, 1), send_row(full_b, 0, -1)
    far_a = send_row(lo_a, 0, 1)
    far_b = send_row(hi_b, 0, -1)
    lo_d, hi_d = send_row(disp, 0, 1), send_row(disp, 0, -1)
    far_da = send_row(cut(lo_d, 0, eighth), 0, 1)
    far_db = send_row(cut(hi_d, eighth, eighth), 0, -1)
    pivot_slices = [full_a, full_b, hi_a, hi_b, far_a, far_b, lo_a, lo_b]
    disp_parts = [disp, hi_d, far_da, far_db, lo_d]

    up2 = send_col(jnp.concatenate([zm[:, :half], xs[:, :half], xs[:, half:]], axis=0), 0, 1)
    dn2 = send_col(jnp.concatenate([zp[:, half:], xs[:, :half], xs[:, half:]], axis=0), 0, -1)
    up3 = send_col(cut(up2, KP, KP), 0, 1)
    dn3 = send_col(cut(dn2, 2 * KP, KP), 0, -1)

    def other(value):
        return send_col(value, 0, 0, 1)

    pairs = [(lower_panel, other(lower_panel)), (xs, other(xs)), (zm, other(zm)), (zp, other(zp))]
    ups, up3s = (up2, other(up2)), (up3, other(up3))
    dns, dn3s = (dn2, other(dn2)), (dn3, other(dn3))

    offsets = [(dx, dz, dc) for dx, dz in PIECES for dc in (0, 1)]
    order = [((x_lo + dx) % 2) * 8 + ((z + dz) % 4) * 2 + (core + dc) % 2 for dx, dz, dc in offsets]
    order = jnp.stack(order + [y, root.astype(jnp.int32)]).astype(jnp.int32)

    mine = owned & away
    key = jnp.where(mine, pivots - first_row, jnp.int32(2**30))
    slot_row = ((tops // quarter - y) % 4) * quarter + tops % quarter
    keys, slots, spares = lax.sort((key, slot_row, spare), num_keys=1)
    edges = jnp.arange(local_rows // MB + 1, dtype=jnp.int32) * MB
    starts = jnp.sum((key[None, :] < edges[:, None]).astype(jnp.int32), axis=1)

    common = [v for pair in pairs for v in pair]
    left = [*ups, *ups, *dns, *up3s]
    right = [*dns, *ups, *dns, *dn3s]
    cuts_l, cuts_r = (0, 0, KP, KP, KP, KP, 0, 0), (0, 0, 2 * KP, 2 * KP, 2 * KP, 2 * KP, 0, 0)
    bh, bl = prep(order, pivot_slices)
    return update((order, starts, keys, spares, slots), common, left, right, cuts_l, cuts_r, bh, bl, matrix, disp_parts)


def solution(mesh):
    in_specs = (P("row", "col"), P(), P("col", "row"))
    out_specs = P("row", "col")
    return jax.shard_map(step, mesh=mesh, in_specs=in_specs, out_specs=out_specs, check_vma=False)
```

time: 293 us -> 196 us (0.67)
  waiting for transfers between devices: 179 us -> 46.1 us
  starting transfers between devices: 0.05 us -> 67.1 us
  Pallas kernels: 0 us -> 32.2 us
  matrix products: 31.4 us -> 0 us
  local copies, waits for them, and re-layouts: 53.2 us -> 35.6 us
  between operations: 14.9 us -> 0.62 us
    psum x1 -> x0, waiting for transfers between devices: 178 us -> none  [spread(): return lax.psum(kept, axis)]
    ppermute x0 -> x34, starting transfers between devices: none -> 67.1 us  [the longest x15 41.9 us: send_col(): return lax.ppermute(value, 'col', col_shift(dx, dz, dc))]
    ppermute x0 -> x34, waiting for transfers between devices: none -> 46.1 us  [the longest x19 32.3 us: send_row(): return lax.ppermute(value, 'row', row_shift(dx, dy, keep))]
    pallas_call x0 -> x8, Pallas kernels: none -> 32.2 us  [the longest x1 25.7 us: update(): pl.pallas_call(functools.partial(update_body, nblk), grid_spec=pltpu.Pref...]
    dot_general x1 -> x0, matrix products: 31.4 us -> none  [contract(): lax.dot_general(left_block, right_block, (((0,), (0,)), ((), ())), precis...]
    scatter x2 -> x0, local copies, waits for them, and re-layouts: 29 us -> none  [per_device(): matrix.at[local_target]]
    unnamed x5 -> x74, local copies, waits for them, and re-layouts: 7.78 us -> 33.3 us
    select_n x1 -> x0, local copies, waits for them, and re-layouts: 8.94 us -> none  [per_device(): return jnp.where(global_rows < top, product, swapped - product)]
  transfers between devices with their start and end apart: 2 -> 34, of which waited for: 1 -> 10; matrix products, arithmetic and copies ran while one was open for 13% -> 5% of each run, Pallas kernels for 0% -> 2%
where the time goes in v2:
time: 196 us; the launch traced here: 195 us
  starting transfers between devices  67.1 us (34%)
  waiting for transfers between devices  46.1 us (24%)
  local copies, waits for them, and re-layouts  35.6 us (18%)
  Pallas kernels  32.2 us (16%)
  other arithmetic  13 us (7%)
    ppermute x15, starting transfers between devices, send_col(): return lax.ppermute(value, 'col', col_shift(dx, dz, dc))  41.9 us
    unnamed x74, local copies, waits for them, and re-layouts  33.3 us
    ppermute x19, waiting for transfers between devices, send_row(): return lax.ppermute(value, 'row', row_shift(dx, dy, keep))  32.3 us
    pallas_call x1, Pallas kernels, update(): pl.pallas_call(functools.partial(update_body, nblk), grid_spec=pltpu.Pref...  25.7 us
    ppermute x19, starting transfers between devices, send_row(): return lax.ppermute(value, 'row', row_shift(dx, dy, keep))  25.2 us
    ppermute x15, waiting for transfers between devices, send_col(): return lax.ppermute(value, 'col', col_shift(dx, dz, dc))  13.8 us
    pallas_call x2, Pallas kernels, gather_rows(): pl.pallas_call(functools.partial(gather_body, h), in_specs=[SMEM, SMEM, V...  5.46 us
    sort x1, other arithmetic, step(): keys, slots, spares = lax.sort((key, slot_row, spare), num_keys=1)  4.41 us
  transfers between devices with their start and end apart: 34, of which 10 were waited for; matrix products, arithmetic and copies ran while one was open for 5% of the time, Pallas kernels for 2%

profile of v2, /device:TPU:1, one launch (start us, length us, event | category | flops | bytes accessed | tf_op | source)
XLA Modules:
  0.0 194.7 jit_solution(6102720960289947204)
XLA Ops:
  5.4 3.4 %copy-done = f32[4096,512]{1,0:T(8,128)S(1)} copy-done((f32[4096,512]{1,0:T(8,128)S(1)}, f32[4096,512]{1,0:T(8,128)}, u32[]{:S(2)}) %copy-start) | copy-done | bytes 8388632
  8.8 2.7 %gather_rows.3 = (f32[128,512]{1,0:T(8,128)S(1)}, f32[128,512]{1,0:T(8,128)S(1)}, f32[128,512]{1,0:T(8,128)S(1)}, f32[128,512]{1,0:T(8,128)S(1)}) custom-call(s32[1024]{0:T(1024)S(1)} %get-tuple-element.48.index, s32[1]{0:T(128)} %bitcast.16.where, f32[4096,512]{1,0:T(8,128)S(1)} %copy-done), custom_call_target="tpu_custom_call" | custom-call | bytes 6291456 | tf_op jit(solution)/shard_map/gather_rows/pallas_call | solution.py:75
  11.6 2.2 %collective-permute-start.19 = (f32[128,512]{1,0:T(8,128)S(1)}, f32[128,512]{1,0:T(8,128)}, u32[]{:S(2)}, u32[]{:S(2)}) collective-permute-start(f32[128,512]{1,0:T(8,128)S(1)} %get-tuple-element.29), channel_id=1, source_target_pairs={{0,16},{16,32},{32,48},{48,0},{64,80},{80,96},{96,112},{112,64},{1... | collective-permute-start | bytes 786440 | tf_op jit(solution)/shard_map/ppermute | solution.py:36
  13.7 1.6 collective-permute-start.3
  16.6 2.6 %collective-permute-start.20 = (f32[128,512]{1,0:T(8,128)S(1)}, f32[128,512]{1,0:T(8,128)}, u32[]{:S(2)}, u32[]{:S(2)}) collective-permute-start(f32[128,512]{1,0:T(8,128)S(1)} %get-tuple-element.30), channel_id=1, source_target_pairs={{0,32},{16,48},{32,0},{48,16},{64,96},{80,112},{96,64},{112,80},{1... | collective-permute-start | bytes 786440 | tf_op jit(solution)/shard_map/ppermute | solution.py:36
  20.3 3.4 %copy-done.1 = f32[4096,512]{1,0:T(8,128)S(1)} copy-done((f32[4096,512]{1,0:T(8,128)S(1)}, f32[4096,512]{1,0:T(8,128)}, u32[]{:S(2)}) %copy-start.1) | copy-done | bytes 8388632
  23.7 2.7 %gather_rows.2 = (f32[128,512]{1,0:T(8,128)S(1)}, f32[128,512]{1,0:T(8,128)S(1)}, f32[128,512]{1,0:T(8,128)S(1)}, f32[128,512]{1,0:T(8,128)S(1)}) custom-call(s32[1024]{0:T(1024)S(1)} %get-tuple-element.48.index, s32[1]{0:T(128)} %bitcast.16.where, f32[4096,512]{1,0:T(8,128)S(1)} %copy-done.1), custom_call_target="tpu_custom_call" | custom-call | bytes 6291456 | tf_op jit(solution)/shard_map/gather_rows/pallas_call | solution.py:75
  27.8 3.8 %collective-permute-start.5 = (f32[64,4096]{1,0:T(8,128)}, f32[64,4096]{1,0:T(8,128)}, u32[]{:S(2)}, u32[]{:S(2)}) collective-permute-start(f32[64,4096]{1,0:T(8,128)} %refs_0_.1), channel_id=1, source_target_pairs={{0,6},{1,7},{2,0},{3,1},{4,2},{5,3},{6,4},{7,5},{8,14},{9,15},{10,... | collective-permute-start | bytes 3145736 | tf_op jit(solution)/shard_map/ppermute | solution.py:32
  32.1 2.3 %collective-permute-done.15 = f32[128,512]{1,0:T(8,128)S(1)} collective-permute-done((f32[128,512]{1,0:T(8,128)S(1)}, f32[128,512]{1,0:T(8,128)S(1)}, u32[]{:S(2)}, u32[]{:S(2)}) %collective-permute-start.15) | collective-permute-done | bytes 262176 | tf_op jit(solution)/shard_map/ppermute | solution.py:36
  35.8 2.6 %collective-permute-done.16 = f32[128,512]{1,0:T(8,128)S(1)} collective-permute-done((f32[128,512]{1,0:T(8,128)S(1)}, f32[128,512]{1,0:T(8,128)S(1)}, u32[]{:S(2)}, u32[]{:S(2)}) %collective-permute-start.16) | collective-permute-done | bytes 262176 | tf_op jit(solution)/shard_map/ppermute | solution.py:36
  38.4 2.7 %collective-permute-start.22 = (f32[128,512]{1,0:T(8,128)S(1)}, f32[128,512]{1,0:T(8,128)S(1)}, u32[]{:S(2)}, u32[]{:S(2)}) collective-permute-start(f32[128,512]{1,0:T(8,128)S(1)} %get-tuple-element.41), channel_id=1, source_target_pairs={{0,64},{16,80},{32,96},{48,112},{64,0},{80,16},{96,32},{112,48},{1... | collective-permute-start | bytes 786440 | tf_op jit(solution)/shard_map/ppermute | solution.py:36
  41.1 2.7 %collective-permute-done.17 = f32[128,512]{1,0:T(8,128)S(1)} collective-permute-done((f32[128,512]{1,0:T(8,128)S(1)}, f32[128,512]{1,0:T(8,128)S(1)}, u32[]{:S(2)}, u32[]{:S(2)}) %collective-permute-start.17) | collective-permute-done | bytes 262176 | tf_op jit(solution)/shard_map/ppermute | solution.py:36
  44.1 2.5 %collective-permute-start.18 = (f32[128,512]{1,0:T(8,128)S(1)}, f32[128,512]{1,0:T(8,128)S(1)}, u32[]{:S(2)}, u32[]{:S(2)}) collective-permute-start(f32[128,512]{1,0:T(8,128)S(1)} %get-tuple-element.39), channel_id=1, source_target_pairs={{0,64},{16,80},{32,96},{48,112},{64,0},{80,16},{96,32},{112,48},{1... | collective-permute-start | bytes 786440 | tf_op jit(solution)/shard_map/ppermute | solution.py:36
  46.7 7.7 %collective-permute-start = (f32[64,4096]{1,0:T(8,128)}, f32[64,4096]{1,0:T(8,128)S(1)}, u32[]{:S(2)}, u32[]{:S(2)}) collective-permute-start(f32[64,4096]{1,0:T(8,128)} %refs_0_.1), channel_id=1, source_target_pairs={{0,1},{1,0},{2,3},{3,2},{4,5},{5,4},{6,7},{7,6},{8,9},{9,8},{10,11... | collective-permute-start | bytes 3145736 | tf_op jit(solution)/shard_map/ppermute | solution.py:32
  54.4 4.4 %collective-permute-start.29 = (f32[256,512]{1,0:T(8,128)S(1)}, f32[256,512]{1,0:T(8,128)S(1)}, u32[]{:S(2)}, u32[]{:S(2)}) collective-permute-start(f32[256,512]{1,0:T(8,128)S(1)} %pad_maximum_fusion.4), channel_id=1, source_target_pairs={{0,64},{16,80},{32,96},{48,112},{1,65},{17,81},{33,97},{49,113},{2... | collective-permute-start | bytes 1572872 | tf_op jit(solution)/shard_map/ppermute | solution.py:36
  58.9 2.3 %collective-permute-start.28 = (f32[128,512]{1,0:T(8,128)S(1)}, f32[128,512]{1,0:T(8,128)S(1)}, u32[]{:S(2)}, u32[]{:S(2)}) collective-permute-start(f32[128,512]{1,0:T(8,128)S(1)} %add.349.refs_1_), channel_id=1, source_target_pairs={{0,16},{16,32},{32,48},{48,0},{64,80},{80,96},{96,112},{112,64},{1... | collective-permute-start | bytes 786440 | tf_op jit(solution)/shard_map/ppermute | solution.py:36
  66.2 3.0 %collective-permute-start.9 = (f32[192,2048]{1,0:T(8,128)S(1)}, f32[192,2048]{1,0:T(8,128)S(1)}, u32[]{:S(2)}, u32[]{:S(2)}) collective-permute-start(f32[192,2048]{1,0:T(8,128)S(1)} %get-tuple-element.42), channel_id=1, source_target_pairs={{0,6},{1,7},{2,0},{3,1},{4,2},{5,3},{6,4},{7,5},{8,14},{9,15},{10,... | collective-permute-start | bytes 4718600 | tf_op jit(solution)/shard_map/ppermute | solution.py:32
  70.0 2.5 %collective-permute-done.25.refs_6_ = f32[128,512]{1,0:T(8,128)S(1)} collective-permute-done((f32[128,512]{1,0:T(8,128)S(1)}, f32[128,512]{1,0:T(8,128)S(1)}, u32[]{:S(2)}, u32[]{:S(2)}) %collective-permute-start.25) | collective-permute-done | bytes 262176 | tf_op jit(solution)/shard_map/ppermute | solution.py:36
  72.7 5.3 %collective-permute-done.23.refs_2_ = f32[128,512]{1,0:T(8,128)S(1)} collective-permute-done((f32[128,512]{1,0:T(8,128)S(1)}, f32[128,512]{1,0:T(8,128)S(1)}, u32[]{:S(2)}, u32[]{:S(2)}) %collective-permute-start.23) | collective-permute-done | bytes 262176 | tf_op jit(solution)/shard_map/ppermute | solution.py:36
  78.7 4.2 %collective-permute-done.27.refs_5_ = f32[128,512]{1,0:T(8,128)S(1)} collective-permute-done((f32[128,512]{1,0:T(8,128)S(1)}, f32[128,512]{1,0:T(8,128)S(1)}, u32[]{:S(2)}, u32[]{:S(2)}) %collective-permute-start.27) | collective-permute-done | bytes 262176 | tf_op jit(solution)/shard_map/ppermute | solution.py:36
  83.7 9.3 %collective-permute-done.26.refs_4_ = f32[128,512]{1,0:T(8,128)S(1)} collective-permute-done((f32[128,512]{1,0:T(8,128)S(1)}, f32[128,512]{1,0:T(8,128)S(1)}, u32[]{:S(2)}, u32[]{:S(2)}) %collective-permute-start.26) | collective-permute-done | bytes 262176 | tf_op jit(solution)/shard_map/ppermute | solution.py:36
  94.7 6.9 %collective-permute-start.4 = (f32[64,4096]{1,0:T(8,128)}, f32[64,4096]{1,0:T(8,128)S(1)}, u32[]{:S(2)}, u32[]{:S(2)}) collective-permute-start(f32[64,4096]{1,0:T(8,128)} %collective-permute-done.3.refs_4_), channel_id=1, source_target_pairs={{0,1},{1,0},{2,3},{3,2},{4,5},{5,4},{6,7},{7,6},{8,9},{9,8},{10,11... | collective-permute-start | bytes 3145736 | tf_op jit(solution)/shard_map/ppermute | solution.py:32
  102.4 1.7 collective-permute-start.32
  104.2 5.7 %collective-permute-start.10 = (f32[192,2048]{1,0:T(8,128)S(1)}, f32[192,2048]{1,0:T(8,128)}, u32[]{:S(2)}, u32[]{:S(2)}) collective-permute-start(f32[192,2048]{1,0:T(8,128)S(1)} %collective-permute-done.9.ref.refs_12_.refs_16_.refs_20_), channel_id=1, source_target_pairs={{0,1},{1,0},{2,3},{3,2},{4,5},{5,4},{6,7},{7,6},{8,9},{9,8},{10,11... | collective-permute-start | bytes 4718600 | tf_op jit(solution)/shard_map/ppermute | solution.py:32
  111.7 2.9 %collective-permute-start.33 = (f32[128,512]{1,0:T(8,128)S(1)}, f32[128,512]{1,0:T(8,128)S(1)}, u32[]{:S(2)}, u32[]{:S(2)}) collective-permute-start(f32[128,512]{1,0:T(8,128)S(1)} %cut.7), channel_id=1, source_target_pairs={{0,48},{16,0},{32,16},{48,32},{64,112},{80,64},{96,80},{112,96},{1... | collective-permute-start | bytes 786440 | tf_op jit(solution)/shard_map/ppermute | solution.py:36
  114.6 3.2 %collective-permute-done.33.refs_31_ = f32[128,512]{1,0:T(8,128)S(1)} collective-permute-done((f32[128,512]{1,0:T(8,128)S(1)}, f32[128,512]{1,0:T(8,128)S(1)}, u32[]{:S(2)}, u32[]{:S(2)}) %collective-permute-start.33) | collective-permute-done | bytes 262176 | tf_op jit(solution)/shard_map/ppermute | solution.py:36
  118.6 6.6 %collective-permute-start.6 = (f32[64,4096]{1,0:T(8,128)}, f32[64,4096]{1,0:T(8,128)}, u32[]{:S(2)}, u32[]{:S(2)}) collective-permute-start(f32[64,4096]{1,0:T(8,128)} %collective-permute-done.5.refs_6_), channel_id=1, source_target_pairs={{0,1},{1,0},{2,3},{3,2},{4,5},{5,4},{6,7},{7,6},{8,9},{9,8},{10,11... | collective-permute-start | bytes 3145736 | tf_op jit(solution)/shard_map/ppermute | solution.py:32
  126.1 2.7 %collective-permute-start.13 = (f32[64,2048]{1,0:T(8,128)S(1)}, f32[64,2048]{1,0:T(8,128)}, u32[]{:S(2)}, u32[]{:S(2)}) collective-permute-start(f32[64,2048]{1,0:T(8,128)S(1)} %cut.5), channel_id=1, source_target_pairs={{0,6},{1,7},{2,0},{3,1},{4,2},{5,3},{6,4},{7,5},{8,14},{9,15},{10,... | collective-permute-start | bytes 1572872 | tf_op jit(solution)/shard_map/ppermute | solution.py:32
  129.8 10.4 %collective-permute-done.13.refs_22_ = f32[64,2048]{1,0:T(8,128)} collective-permute-done((f32[64,2048]{1,0:T(8,128)S(1)}, f32[64,2048]{1,0:T(8,128)}, u32[]{:S(2)}, u32[]{:S(2)}) %collective-permute-start.13) | collective-permute-done | bytes 524320 | tf_op jit(solution)/shard_map/ppermute | solution.py:32
  140.9 3.4 %collective-permute-done.11.refs_14_ = f32[64,2048]{1,0:T(8,128)} collective-permute-done((f32[64,2048]{1,0:T(8,128)S(1)}, f32[64,2048]{1,0:T(8,128)}, u32[]{:S(2)}, u32[]{:S(2)}) %collective-permute-start.11) | collective-permute-done | bytes 524320 | tf_op jit(solution)/shard_map/ppermute | solution.py:32
  145.5 4.4 %sort.31 = (s32[1024]{0:T(1024)S(1)}, s32[1024]{0:T(1024)S(1)}, s32[1024]{0:T(1024)S(1)}, s32[1024]{0:T(1024)}) sort(s32[1024]{0:T(1024)S(1)} %get-tuple-element.49, s32[1024]{0:T(1024)S(1)} %fusion.11, s32[1024]{0:T(1024)S(1)} %select_reduce_fusion, s32[1024]{0:T(1024)S(1)} %iota.21), dimensions={0}, to_apply=%region_5.6 | sort | flops 10240 | bytes 32768 | tf_op jit(solution)/shard_map/sort | solution.py:296
  168.8 25.7 %update.1 = f32[4096,512]{1,0:T(8,128)} custom-call(s32[18]{0:T(128)S(1)} %stack.79.order, s32[9]{0:T(128)S(1)} %convert_reduce_fusion.2.starts, s32[1024]{0:T(1024)S(1)} %get-tuple-element.21.keys, s32[1024]{0:T(1024)S(1)} %get-tuple-element.22.spares, s32[1024]{0:T(1024)S(1)} %get-tuple-element.23.slots, f32[64,4096]{1,0:T(8,128)} %refs_0_.1, ...), custom_call_target="tpu_custom_call" | custom-call | flops 12884901888 | bytes 33554432 | tf_op jit(solution)/shard_map/update/pallas_call | solution.py:186
  (143 shorter events, 46.3 us)
Async XLA Ops:
  11.6 15.8 %collective-permute-start.19 = (f32[128,512]{1,0:T(8,128)S(1)}, f32[128,512]{1,0:T(8,128)}, u32[]{:S(2)}, u32[]{:S(2)}) collective-permute-start(f32[128,512]{1,0:T(8,128)S(1)} %get-tuple-element.29), channel_id=1, source_target_pairs={{0,16},{16,32},{32,48},{48,0},{64,80},{80,96},{96,112},{112,64},{1... | collective-permute-start | bytes 786440 | tf_op jit(solution)/shard_map/ppermute | solution.py:36
  13.7 45.2 %collective-permute-start.3 = (f32[64,4096]{1,0:T(8,128)}, f32[64,4096]{1,0:T(8,128)}, u32[]{:S(2)}, u32[]{:S(2)}) collective-permute-start(f32[64,4096]{1,0:T(8,128)} %refs_0_.1), channel_id=1, source_target_pairs={{0,2},{1,3},{2,4},{3,5},{4,6},{5,7},{6,0},{7,1},{8,10},{9,11},{10,... | collective-permute-start | bytes 3145736 | tf_op jit(solution)/shard_map/ppermute | solution.py:32
  15.4 46.9 %collective-permute-start.1 = (f32[64,4096]{1,0:T(8,128)}, f32[64,4096]{1,0:T(8,128)S(1)}, u32[]{:S(2)}, u32[]{:S(2)}) collective-permute-start(f32[64,4096]{1,0:T(8,128)} %refs_0_.1), channel_id=1, source_target_pairs={{0,8},{1,9},{2,10},{3,11},{4,12},{5,13},{6,14},{7,15},{8,0},{9,1},... | collective-permute-start | bytes 3145736 | tf_op jit(solution)/shard_map/ppermute | solution.py:32
  16.6 11.2 %collective-permute-start.20 = (f32[128,512]{1,0:T(8,128)S(1)}, f32[128,512]{1,0:T(8,128)}, u32[]{:S(2)}, u32[]{:S(2)}) collective-permute-start(f32[128,512]{1,0:T(8,128)S(1)} %get-tuple-element.30), channel_id=1, source_target_pairs={{0,32},{16,48},{32,0},{48,16},{64,96},{80,112},{96,64},{112,80},{1... | collective-permute-start | bytes 786440 | tf_op jit(solution)/shard_map/ppermute | solution.py:36
  19.2 12.4 %collective-permute-start.21 = (f32[128,512]{1,0:T(8,128)S(1)}, f32[128,512]{1,0:T(8,128)}, u32[]{:S(2)}, u32[]{:S(2)}) collective-permute-start(f32[128,512]{1,0:T(8,128)S(1)} %get-tuple-element.31), channel_id=1, source_target_pairs={{0,48},{16,0},{32,16},{48,32},{64,112},{80,64},{96,80},{112,96},{1... | collective-permute-start | bytes 786440 | tf_op jit(solution)/shard_map/ppermute | solution.py:36
  27.3 7.2 %collective-permute-start.15 = (f32[128,512]{1,0:T(8,128)S(1)}, f32[128,512]{1,0:T(8,128)S(1)}, u32[]{:S(2)}, u32[]{:S(2)}) collective-permute-start(f32[128,512]{1,0:T(8,128)S(1)} %get-tuple-element.25), channel_id=1, source_target_pairs={{0,16},{16,32},{32,48},{48,0},{64,80},{80,96},{96,112},{112,64},{1... | collective-permute-start | bytes 786440 | tf_op jit(solution)/shard_map/ppermute | solution.py:36
  27.8 35.1 %collective-permute-start.5 = (f32[64,4096]{1,0:T(8,128)}, f32[64,4096]{1,0:T(8,128)}, u32[]{:S(2)}, u32[]{:S(2)}) collective-permute-start(f32[64,4096]{1,0:T(8,128)} %refs_0_.1), channel_id=1, source_target_pairs={{0,6},{1,7},{2,0},{3,1},{4,2},{5,3},{6,4},{7,5},{8,14},{9,15},{10,... | collective-permute-start | bytes 3145736 | tf_op jit(solution)/shard_map/ppermute | solution.py:32
  31.6 6.8 %collective-permute-start.16 = (f32[128,512]{1,0:T(8,128)S(1)}, f32[128,512]{1,0:T(8,128)S(1)}, u32[]{:S(2)}, u32[]{:S(2)}) collective-permute-start(f32[128,512]{1,0:T(8,128)S(1)} %get-tuple-element.26), channel_id=1, source_target_pairs={{0,32},{16,48},{32,0},{48,16},{64,96},{80,112},{96,64},{112,80},{1... | collective-permute-start | bytes 786440 | tf_op jit(solution)/shard_map/ppermute | solution.py:36
  34.5 9.4 %collective-permute-start.17 = (f32[128,512]{1,0:T(8,128)S(1)}, f32[128,512]{1,0:T(8,128)S(1)}, u32[]{:S(2)}, u32[]{:S(2)}) collective-permute-start(f32[128,512]{1,0:T(8,128)S(1)} %get-tuple-element.27), channel_id=1, source_target_pairs={{0,48},{16,0},{32,16},{48,32},{64,112},{80,64},{96,80},{112,96},{1... | collective-permute-start | bytes 786440 | tf_op jit(solution)/shard_map/ppermute | solution.py:36
  38.4 8.2 %collective-permute-start.22 = (f32[128,512]{1,0:T(8,128)S(1)}, f32[128,512]{1,0:T(8,128)S(1)}, u32[]{:S(2)}, u32[]{:S(2)}) collective-permute-start(f32[128,512]{1,0:T(8,128)S(1)} %get-tuple-element.41), channel_id=1, source_target_pairs={{0,64},{16,80},{32,96},{48,112},{64,0},{80,16},{96,32},{112,48},{1... | collective-permute-start | bytes 786440 | tf_op jit(solution)/shard_map/ppermute | solution.py:36
  44.1 10.4 %collective-permute-start.18 = (f32[128,512]{1,0:T(8,128)S(1)}, f32[128,512]{1,0:T(8,128)S(1)}, u32[]{:S(2)}, u32[]{:S(2)}) collective-permute-start(f32[128,512]{1,0:T(8,128)S(1)} %get-tuple-element.39), channel_id=1, source_target_pairs={{0,64},{16,80},{32,96},{48,112},{64,0},{80,16},{96,32},{112,48},{1... | collective-permute-start | bytes 786440 | tf_op jit(solution)/shard_map/ppermute | solution.py:36
  46.7 47.1 %collective-permute-start = (f32[64,4096]{1,0:T(8,128)}, f32[64,4096]{1,0:T(8,128)S(1)}, u32[]{:S(2)}, u32[]{:S(2)}) collective-permute-start(f32[64,4096]{1,0:T(8,128)} %refs_0_.1), channel_id=1, source_target_pairs={{0,1},{1,0},{2,3},{3,2},{4,5},{5,4},{6,7},{7,6},{8,9},{9,8},{10,11... | collective-permute-start | bytes 3145736 | tf_op jit(solution)/shard_map/ppermute | solution.py:32
  54.4 18.1 %collective-permute-start.29 = (f32[256,512]{1,0:T(8,128)S(1)}, f32[256,512]{1,0:T(8,128)S(1)}, u32[]{:S(2)}, u32[]{:S(2)}) collective-permute-start(f32[256,512]{1,0:T(8,128)S(1)} %pad_maximum_fusion.4), channel_id=1, source_target_pairs={{0,64},{16,80},{32,96},{48,112},{1,65},{17,81},{33,97},{49,113},{2... | collective-permute-start | bytes 1572872 | tf_op jit(solution)/shard_map/ppermute | solution.py:36
  58.9 6.6 %collective-permute-start.28 = (f32[128,512]{1,0:T(8,128)S(1)}, f32[128,512]{1,0:T(8,128)S(1)}, u32[]{:S(2)}, u32[]{:S(2)}) collective-permute-start(f32[128,512]{1,0:T(8,128)S(1)} %add.349.refs_1_), channel_id=1, source_target_pairs={{0,16},{16,32},{32,48},{48,0},{64,80},{80,96},{96,112},{112,64},{1... | collective-permute-start | bytes 786440 | tf_op jit(solution)/shard_map/ppermute | solution.py:36
  62.3 6.9 %collective-permute-start.24 = (f32[128,512]{1,0:T(8,128)S(1)}, f32[128,512]{1,0:T(8,128)S(1)}, u32[]{:S(2)}, u32[]{:S(2)}) collective-permute-start(f32[128,512]{1,0:T(8,128)S(1)} %add.349.refs_1_), channel_id=1, source_target_pairs={{0,48},{16,0},{32,16},{48,32},{64,112},{80,64},{96,80},{112,96},{1... | collective-permute-start | bytes 786440 | tf_op jit(solution)/shard_map/ppermute | solution.py:36
  62.9 9.6 %collective-permute-start.25 = (f32[128,512]{1,0:T(8,128)S(1)}, f32[128,512]{1,0:T(8,128)S(1)}, u32[]{:S(2)}, u32[]{:S(2)}) collective-permute-start(f32[128,512]{1,0:T(8,128)S(1)} %add.343.refs_0_), channel_id=1, source_target_pairs={{0,16},{16,32},{32,48},{48,0},{64,80},{80,96},{96,112},{112,64},{1... | collective-permute-start | bytes 786440 | tf_op jit(solution)/shard_map/ppermute | solution.py:36
  66.2 38.0 %collective-permute-start.9 = (f32[192,2048]{1,0:T(8,128)S(1)}, f32[192,2048]{1,0:T(8,128)S(1)}, u32[]{:S(2)}, u32[]{:S(2)}) collective-permute-start(f32[192,2048]{1,0:T(8,128)S(1)} %get-tuple-element.42), channel_id=1, source_target_pairs={{0,6},{1,7},{2,0},{3,1},{4,2},{5,3},{6,4},{7,5},{8,14},{9,15},{10,... | collective-permute-start | bytes 4718600 | tf_op jit(solution)/shard_map/ppermute | solution.py:32
  69.3 40.6 %collective-permute-start.7 = (f32[192,2048]{1,0:T(8,128)S(1)}, f32[192,2048]{1,0:T(8,128)S(1)}, u32[]{:S(2)}, u32[]{:S(2)}) collective-permute-start(f32[192,2048]{1,0:T(8,128)S(1)} %get-tuple-element.43), channel_id=1, source_target_pairs={{0,2},{1,3},{2,4},{3,5},{4,6},{5,7},{6,0},{7,1},{8,10},{9,11},{10,... | collective-permute-start | bytes 4718600 | tf_op jit(solution)/shard_map/ppermute | solution.py:32
  72.5 10.5 %collective-permute-start.27 = (f32[128,512]{1,0:T(8,128)S(1)}, f32[128,512]{1,0:T(8,128)S(1)}, u32[]{:S(2)}, u32[]{:S(2)}) collective-permute-start(f32[128,512]{1,0:T(8,128)S(1)} %collective-permute-done.24.refs_3_), channel_id=1, source_target_pairs={{0,48},{16,0},{32,16},{48,32},{64,112},{80,64},{96,80},{112,96},{1... | collective-permute-start | bytes 786440 | tf_op jit(solution)/shard_map/ppermute | solution.py:36
  78.7 22.9 %collective-permute-start.31 = (f32[256,512]{1,0:T(8,128)S(1)}, f32[256,512]{1,0:T(8,128)S(1)}, u32[]{:S(2)}, u32[]{:S(2)}) collective-permute-start(f32[256,512]{1,0:T(8,128)S(1)} %broadcast_select_fusion.refs_28_), channel_id=1, source_target_pairs={{0,16},{16,32},{32,48},{48,0},{64,80},{80,96},{96,112},{112,64},{1... | collective-permute-start | bytes 1572872 | tf_op jit(solution)/shard_map/ppermute | solution.py:36
  83.7 9.3 %collective-permute-start.26 = (f32[128,512]{1,0:T(8,128)S(1)}, f32[128,512]{1,0:T(8,128)S(1)}, u32[]{:S(2)}, u32[]{:S(2)}) collective-permute-start(f32[128,512]{1,0:T(8,128)S(1)} %collective-permute-done.25.refs_6_), channel_id=1, source_target_pairs={{0,16},{16,32},{32,48},{48,0},{64,80},{80,96},{96,112},{112,64},{1... | collective-permute-start | bytes 786440 | tf_op jit(solution)/shard_map/ppermute | solution.py:36
  93.7 8.7 %collective-permute-start.30 = (f32[256,512]{1,0:T(8,128)S(1)}, f32[256,512]{1,0:T(8,128)S(1)}, u32[]{:S(2)}, u32[]{:S(2)}) collective-permute-start(f32[256,512]{1,0:T(8,128)S(1)} %broadcast_select_fusion.refs_28_), channel_id=1, source_target_pairs={{0,48},{16,0},{32,16},{48,32},{64,112},{80,64},{96,80},{112,96},{1... | collective-permute-start | bytes 1572872 | tf_op jit(solution)/shard_map/ppermute | solution.py:36
  94.7 30.4 %collective-permute-start.4 = (f32[64,4096]{1,0:T(8,128)}, f32[64,4096]{1,0:T(8,128)S(1)}, u32[]{:S(2)}, u32[]{:S(2)}) collective-permute-start(f32[64,4096]{1,0:T(8,128)} %collective-permute-done.3.refs_4_), channel_id=1, source_target_pairs={{0,1},{1,0},{2,3},{3,2},{4,5},{5,4},{6,7},{7,6},{8,9},{9,8},{10,11... | collective-permute-start | bytes 3145736 | tf_op jit(solution)/shard_map/ppermute | solution.py:32
  101.6 27.2 %collective-permute-start.2 = (f32[64,4096]{1,0:T(8,128)}, f32[64,4096]{1,0:T(8,128)S(1)}, u32[]{:S(2)}, u32[]{:S(2)}) collective-permute-start(f32[64,4096]{1,0:T(8,128)} %copy-done.4), channel_id=1, source_target_pairs={{0,1},{1,0},{2,3},{3,2},{4,5},{5,4},{6,7},{7,6},{8,9},{9,8},{10,11... | collective-permute-start | bytes 3145736 | tf_op jit(solution)/shard_map/ppermute | solution.py:32
  102.4 8.6 %collective-permute-start.32 = (f32[128,512]{1,0:T(8,128)S(1)}, f32[128,512]{1,0:T(8,128)S(1)}, u32[]{:S(2)}, u32[]{:S(2)}) collective-permute-start(f32[128,512]{1,0:T(8,128)S(1)} %cut.6), channel_id=1, source_target_pairs={{0,16},{16,32},{32,48},{48,0},{64,80},{80,96},{96,112},{112,64},{1... | collective-permute-start | bytes 786440 | tf_op jit(solution)/shard_map/ppermute | solution.py:36
  104.2 54.6 %collective-permute-start.10 = (f32[192,2048]{1,0:T(8,128)S(1)}, f32[192,2048]{1,0:T(8,128)}, u32[]{:S(2)}, u32[]{:S(2)}) collective-permute-start(f32[192,2048]{1,0:T(8,128)S(1)} %collective-permute-done.9.ref.refs_12_.refs_16_.refs_20_), channel_id=1, source_target_pairs={{0,1},{1,0},{2,3},{3,2},{4,5},{5,4},{6,7},{7,6},{8,9},{9,8},{10,11... | collective-permute-start | bytes 4718600 | tf_op jit(solution)/shard_map/ppermute | solution.py:32
  109.9 49.0 %collective-permute-start.8 = (f32[192,2048]{1,0:T(8,128)S(1)}, f32[192,2048]{1,0:T(8,128)}, u32[]{:S(2)}, u32[]{:S(2)}) collective-permute-start(f32[192,2048]{1,0:T(8,128)S(1)} %collective-permute-done.7.ref.refs_8_.refs_10_.refs_18_), channel_id=1, source_target_pairs={{0,1},{1,0},{2,3},{3,2},{4,5},{5,4},{6,7},{7,6},{8,9},{9,8},{10,11... | collective-permute-start | bytes 4718600 | tf_op jit(solution)/shard_map/ppermute | solution.py:32
  118.6 40.2 %collective-permute-start.6 = (f32[64,4096]{1,0:T(8,128)}, f32[64,4096]{1,0:T(8,128)}, u32[]{:S(2)}, u32[]{:S(2)}) collective-permute-start(f32[64,4096]{1,0:T(8,128)} %collective-permute-done.5.refs_6_), channel_id=1, source_target_pairs={{0,1},{1,0},{2,3},{3,2},{4,5},{5,4},{6,7},{7,6},{8,9},{9,8},{10,11... | collective-permute-start | bytes 3145736 | tf_op jit(solution)/shard_map/ppermute | solution.py:32
  126.1 14.1 %collective-permute-start.13 = (f32[64,2048]{1,0:T(8,128)S(1)}, f32[64,2048]{1,0:T(8,128)}, u32[]{:S(2)}, u32[]{:S(2)}) collective-permute-start(f32[64,2048]{1,0:T(8,128)S(1)} %cut.5), channel_id=1, source_target_pairs={{0,6},{1,7},{2,0},{3,1},{4,2},{5,3},{6,4},{7,5},{8,14},{9,15},{10,... | collective-permute-start | bytes 1572872 | tf_op jit(solution)/shard_map/ppermute | solution.py:32
  129.8 14.5 %collective-permute-start.11 = (f32[64,2048]{1,0:T(8,128)S(1)}, f32[64,2048]{1,0:T(8,128)}, u32[]{:S(2)}, u32[]{:S(2)}) collective-permute-start(f32[64,2048]{1,0:T(8,128)S(1)} %cut.4), channel_id=1, source_target_pairs={{0,2},{1,3},{2,4},{3,5},{4,6},{5,7},{6,0},{7,1},{8,10},{9,11},{10,... | collective-permute-start | bytes 1572872 | tf_op jit(solution)/shard_map/ppermute | solution.py:32
  140.2 18.6 %collective-permute-start.14 = (f32[64,2048]{1,0:T(8,128)}, f32[64,2048]{1,0:T(8,128)}, u32[]{:S(2)}, u32[]{:S(2)}) collective-permute-start(f32[64,2048]{1,0:T(8,128)} %collective-permute-done.13.refs_22_), channel_id=1, source_target_pairs={{0,1},{1,0},{2,3},{3,2},{4,5},{5,4},{6,7},{7,6},{8,9},{9,8},{10,11... | collective-permute-start | bytes 1572872 | tf_op jit(solution)/shard_map/ppermute | solution.py:32
  144.3 14.5 %collective-permute-start.12 = (f32[64,2048]{1,0:T(8,128)}, f32[64,2048]{1,0:T(8,128)}, u32[]{:S(2)}, u32[]{:S(2)}) collective-permute-start(f32[64,2048]{1,0:T(8,128)} %collective-permute-done.11.refs_14_), channel_id=1, source_target_pairs={{0,1},{1,0},{2,3},{3,2},{4,5},{5,4},{6,7},{7,6},{8,9},{9,8},{10,11... | collective-permute-start | bytes 1572872 | tf_op jit(solution)/shard_map/ppermute | solution.py:32
  (39 other events, 349.5 us)

commit v3 on v0

v3 whole, which is shorter than its diff:
```python
import functools

import jax
import jax.numpy as jnp
from jax import lax
from jax.experimental import pallas as pl
from jax.experimental.pallas import tpu as pltpu
from jax.sharding import PartitionSpec as P


NZ, NY, NX, NC = 4, 4, 2, 2


def torus(step):
    pairs = []
    for r in range(NX * NY):
        for q in range(NX * NZ * NC):
            xh, y, xl, z, c = step(r // 4, r % 4, q // 8, (q // 2) % 4, q % 2)
            pairs.append((r * 16 + q, ((xh % 2) * 4 + y % 4) * 16 + (xl % 2) * 8 + (z % 4) * 2 + c % 2))
    return pairs


def send(value, step):
    return lax.ppermute(value, ("row", "col"), torus(step))


def way(c):
    return 1 if c == 0 else -1


def z_way(xh, y, xl, z, c):
    return xh, y, xl, z + way(c), c


def z_back(xh, y, xl, z, c):
    return xh, y, xl, z - way(c), c


def y_way(xh, y, xl, z, c):
    return xh, y + way(c), xl, z, c


def y_back(xh, y, xl, z, c):
    return xh, y - way(c), xl, z, c


def x_lo_swap(xh, y, xl, z, c):
    return xh, y, 1 - xl, z, c


def x_hi_swap(xh, y, xl, z, c):
    return 1 - xh, y, xl, z, c


def core_swap(xh, y, xl, z, c):
    return xh, y, xl, z, 1 - c


def row_pairs(dx, dy, keep=lambda x: True):
    return [(i, ((i // 4 + dx) % 2) * 4 + (i + dy) % 4) for i in range(NX * NY) if keep(i // 4)]


def send_row(value, dx, dy, keep=lambda x: True):
    return lax.ppermute(value, "row", row_pairs(dx, dy, keep))


KP = 64
MB = 512
VMEM = pl.BlockSpec(memory_space=pltpu.VMEM)
ANY = pl.BlockSpec(memory_space=pl.ANY)
SMEM = pl.BlockSpec(memory_space=pltpu.SMEM)


def params(mib):
    return pltpu.CompilerParams(vmem_limit_bytes=mib << 20)


def split(value):
    hi = value.astype(jnp.bfloat16)
    return hi, (value - hi.astype(jnp.float32)).astype(jnp.bfloat16)


def index_body(where, p_ref, index, spare_ref):
    first, root = where[1], where[2]
    p = p_ref[...]
    top = p.shape[1]
    side = 128
    sub = lax.broadcasted_iota(jnp.int32, (side, top), 0)
    lane = lax.broadcasted_iota(jnp.int32, (1, top), 1)

    def column(line, c):
        square = jnp.broadcast_to(line[:, c * side : (c + 1) * side], (side, side)).T
        return jnp.concatenate([square] * (top // side), axis=1)

    def count(hits):
        return jnp.sum(hits, axis=0, keepdims=True)

    chosen = jnp.zeros((1, top), jnp.int32)
    rank = jnp.zeros((1, top), jnp.int32)
    for c in range(top // side):
        pc = column(p, c)
        chosen += count(jnp.where(pc == lane, 1, 0))
        rank += count(jnp.where((pc >= top) & (pc < p), 1, 0))
    free = jnp.where(chosen == 0, 1.0, 0.0)
    before = jnp.zeros((8, top), jnp.float32)
    for c in range(top // side):
        ahead = jnp.where(sub + c * side < lane, 1.0, 0.0).astype(jnp.bfloat16)
        some = jnp.broadcast_to(free[:, c * side : (c + 1) * side], (8, side)).astype(jnp.bfloat16)
        before += jnp.dot(some, ahead, preferred_element_type=jnp.float32)
    place = jnp.where(chosen == 0, before[0:1].astype(jnp.int32), -1)
    spare = jnp.zeros((1, top), jnp.int32)
    for c in range(top // side):
        spare += count(jnp.where(column(place, c) == rank, sub + c * side, 0))
    local = p - first
    owned = (local >= 0) & (local < where[3])
    index[...] = jnp.where(owned, local, jnp.where(root == 1, spare, -1))
    spare_ref[...] = spare


def row_index(where, line):
    shape = jax.ShapeDtypeStruct(line.shape, jnp.int32)
    return pl.pallas_call(
        index_body,
        in_specs=[SMEM, VMEM],
        out_specs=[VMEM] * 2,
        out_shape=[shape] * 2,
        compiler_params=params(6),
        cost_estimate=pl.CostEstimate(flops=0, bytes_accessed=1 << 20, transcendentals=0),
        name="row_index",
    )(where, line)


def gather_body(h, index, where, matrix, *outs):
    y = where[0]
    for out, d in zip(outs, (2, 1, 3, 0)):
        start = lax.rem(y + d, 4) * 256 + h * 128

        def group(g, carry, out=out, start=start):
            rows = []
            for u in range(8):
                i = index[0, start + g * 8 + u]
                row = matrix[pl.ds(jnp.maximum(i, 0), 1), :]
                rows.append(jnp.where(i >= 0, row, 0.0))
            out[pl.ds(pl.multiple_of(g * 8, 8), 8), :] = jnp.concatenate(rows, axis=0)
            return carry

        lax.fori_loop(0, 16, group, 0)


def gather_rows(h, index, where, matrix):
    n = matrix.shape[1]
    return pl.pallas_call(
        functools.partial(gather_body, h),
        in_specs=[SMEM, SMEM, VMEM],
        out_specs=[VMEM] * 4,
        out_shape=[jax.ShapeDtypeStruct((128, n), jnp.float32)] * 4,
        compiler_params=params(4),
        cost_estimate=pl.CostEstimate(flops=0, bytes_accessed=6 << 20, transcendentals=0),
        name="gather_rows",
    )(index, where, matrix)


def dots(bh, bl, ah, al):
    dot = functools.partial(
        lax.dot_general,
        dimension_numbers=(((0,), (0,)), ((), ())),
        preferred_element_type=jnp.float32,
    )
    return dot(ah, bh) + dot(ah, bl) + dot(al, bh)


def prep_body(order, *refs):
    slices, (bh, bl), full = refs[:8], refs[8:10], refs[10]
    y, da = order[16], order[18]
    for s, d in enumerate((0, da, 4 - da, 2)):
        t = lax.rem(y + d, 4)
        for h in range(2):
            full[pl.ds(pl.multiple_of(t * 256 + h * 128, 128), 128), :] = slices[2 * s + h][...]
    for j in range(16):
        rows = full[pl.ds(pl.multiple_of(order[j] * KP, KP), KP), :]
        bh[j * KP : (j + 1) * KP, :], bl[j * KP : (j + 1) * KP, :] = split(rows)


def prep(order, slices):
    n = slices[0].shape[1]
    return pl.pallas_call(
        prep_body,
        in_specs=[SMEM] + [VMEM] * len(slices),
        out_specs=[VMEM] * 2,
        out_shape=[jax.ShapeDtypeStruct((1024, n), jnp.bfloat16)] * 2,
        scratch_shapes=[pltpu.VMEM((1024, n), jnp.float32)],
        compiler_params=params(8),
        cost_estimate=pl.CostEstimate(flops=0, bytes_accessed=4 << 20, transcendentals=0),
        name="prep",
    )(order, *slices)


def load(first, pieces, into=None):
    m = pieces[0].shape[1]
    n = len(pieces)

    def body(*refs):
        ah, al = refs[-2:]

        def block_step(*io):
            at = pl.ds(pl.multiple_of(pl.program_id(0) * MB, MB), MB)
            for j, piece in enumerate(io, first):
                ah[j * KP : (j + 1) * KP, at], al[j * KP : (j + 1) * KP, at] = split(piece[...])

        if into is not None:
            for j, piece in enumerate(refs[:n], first):
                ah[j * KP : (j + 1) * KP, :], al[j * KP : (j + 1) * KP, :] = split(piece[...])
            return
        spec = pl.BlockSpec((KP, MB), lambda i: (0, i))
        pltpu.emit_pipeline(block_step, grid=(m // MB,), in_specs=[spec] * n)(*refs[:n])

    return pl.pallas_call(
        body,
        in_specs=[ANY] * n if into is None else [VMEM] * (n + 2),
        out_specs=[VMEM] * 2,
        out_shape=[jax.ShapeDtypeStruct((16 * KP, m), jnp.bfloat16)] * 2,
        input_output_aliases={} if into is None else {n: 0, n + 1: 1},
        compiler_params=params(12),
        cost_estimate=pl.CostEstimate(flops=0, bytes_accessed=n << 20, transcendentals=0),
    )(*pieces, *([] if into is None else into))


def update(scalars, panel, bh, bl, matrix, parts):
    rows, n = matrix.shape
    nblk = rows // MB

    def body(order, starts, keys, spares, slots, ph, pw, bh, bl, matrix, *refs):
        parts, (out, disp) = refs[:4], refs[4:]
        root = order[17]
        for i, part in enumerate(parts):
            disp[i * 256 : (i + 1) * 256, :] = part[...]

        def block_step(dest):
            block = pl.program_id(0)
            at = pl.ds(pl.multiple_of(block * MB, MB), MB)
            in_top = (root == 1) & (block < 1024 // MB)
            acc = dots(bh[...], bl[...], ph[:, at], pw[:, at])
            dest[...] = jnp.where(in_top, 0.0, matrix[at, :]) + jnp.where(in_top, 1.0, -1.0) * acc

            def patch(source, rows_of):
                def one(k, carry):
                    r = keys[k]
                    dest[pl.ds(r - block * MB, 1), :] += source[pl.ds(rows_of[k], 1), :] - matrix[pl.ds(r, 1), :]
                    return carry

                lax.fori_loop(starts[block], starts[block + 1], one, 0)

            @pl.when(root == 1)
            def _():
                patch(matrix, spares)

            @pl.when(root == 0)
            def _():
                patch(disp, slots)

        pltpu.emit_pipeline(
            block_step, grid=(nblk,), in_specs=[], out_specs=[pl.BlockSpec((MB, n), lambda i: (i, 0))]
        )(out)

    return pl.pallas_call(
        body,
        in_specs=[SMEM] * 5 + [VMEM] * 9,
        out_specs=ANY,
        out_shape=jax.ShapeDtypeStruct(matrix.shape, jnp.float32),
        scratch_shapes=[pltpu.VMEM((1024, n), jnp.float32)],
        compiler_params=params(14),
        cost_estimate=pl.CostEstimate(flops=6 * rows * n * 1024, bytes_accessed=8 << 20, transcendentals=0),
        name="update",
    )(*scalars, *panel, bh, bl, matrix, *parts)


def step(matrix, pivots, lower_panel):
    top = pivots.shape[0]
    local_rows, _ = matrix.shape
    row, col = lax.axis_index("row"), lax.axis_index("col")
    x_hi, y = row // 4, row % 4
    x_lo, z, core = col // 8, (col // 2) % 4, col % 2
    first_row = row * local_rows
    root = row == 0
    quarter, eighth = top // 4, top // 8

    own = lower_panel
    xs = send(own, x_lo_swap)
    za = send(own, z_way)
    zb = send(own, z_back)
    xa = send(xs, z_way)
    xb = send(xs, z_back)
    z2 = send(za, z_way)
    x2 = send(xa, z_way)
    pieces = []
    for piece in (own, xs, za, zb, xa, xb, z2, x2):
        pieces += [piece, send(piece, core_swap)]

    where = jnp.stack([y, first_row, root.astype(jnp.int32), jnp.int32(local_rows)]).astype(jnp.int32)
    index, spare = row_index(where, pivots.reshape(1, top))

    got_a = gather_rows(0, index, where, matrix)
    got_b = gather_rows(1, index, where, matrix)

    def exchange(h, got):
        root_owned = (lax.dynamic_slice(pivots, (y * quarter + h * eighth,), (eighth,)) < local_rows)[:, None]
        m2 = send_row(got[0], 0, 2)
        m1 = send_row(got[1], 0, 1)
        m3 = send_row(got[2], 0, -1)
        pivot_sum, disp = 0.0, 0.0
        for message, source in ((got[3], y), (m1, (y + 3) % 4), (m2, (y + 2) % 4), (m3, (y + 1) % 4)):
            from_root = (x_hi == 0) & (source == 0)
            is_disp = from_root & ~root_owned
            pivot_sum = pivot_sum + jnp.where(is_disp, 0.0, message)
            disp = disp + jnp.where(is_disp, message, 0.0)
        return pivot_sum, disp

    part_a, disp_a = exchange(0, got_a)
    part_b, disp_b = exchange(1, got_b)
    disp = jnp.concatenate([disp_a, disp_b], axis=0)
    full_a = part_a + send(part_a, x_hi_swap)
    full_b = part_b + send(part_b, x_hi_swap)
    cross = send_row(disp, 1, 0, lambda x: x == 0)
    disp = jnp.where(x_hi == 0, disp, cross)
    a_a, b_a = send(full_a, y_way), send(full_a, y_back)
    a_b, b_b = send(full_b, y_way), send(full_b, y_back)
    f_a, f_b = send(a_a, y_way), send(a_b, y_way)
    a_d, b_d = send(disp, y_way), send(disp, y_back)
    f_d = send(a_d, y_way)
    a_off = jnp.where(core == 0, 3, 1)

    dz = jnp.where(core == 0, -1, 1)

    def block(dx, dzs, dc):
        return ((x_lo + dx) % 2) * 8 + ((z + dzs + 4) % 4) * 2 + (core + dc) % 2

    order = []
    for dx, sign in ((0, 0), (1, 0), (0, 1), (0, -1), (1, 1), (1, -1), (0, 2), (1, 2)):
        order += [block(dx, sign * dz, 0), block(dx, -sign * dz, 1)]
    order = jnp.stack(order + [y, root.astype(jnp.int32), a_off]).astype(jnp.int32)

    owned = (pivots >= first_row) & (pivots < first_row + local_rows)
    key = jnp.where(owned & (pivots >= top), pivots - first_row, jnp.int32(2**30))
    slot = jnp.arange(top, dtype=jnp.int32)
    off = (slot // quarter - y + 4) % 4
    part = jnp.where(off == 0, 0, jnp.where(off == 2, 3, jnp.where(off == a_off, 1, 2)))
    keys, slots, spares = lax.sort((key, part * quarter + slot % quarter, spare.reshape(top)), num_keys=1)
    edges = jnp.arange(local_rows // MB + 1, dtype=jnp.int32) * MB
    starts = jnp.sum((key[None, :] < edges[:, None]).astype(jnp.int32), axis=1)

    bh, bl = prep(order, [full_a, full_b, a_a, a_b, b_a, b_b, f_a, f_b])
    panel = load(0, pieces[:14])
    panel = load(14, pieces[14:], panel)
    return update((order, starts, keys, spares, slots), panel, bh, bl, matrix, [disp, a_d, b_d, f_d])


def solution(mesh):
    in_specs = (P("row", "col"), P(), P("col", "row"))
    out_specs = P("row", "col")
    return jax.shard_map(step, mesh=mesh, in_specs=in_specs, out_specs=out_specs, check_vma=False)
```

time: 293 us -> 185 us (0.63)
  waiting for transfers between devices: 179 us -> 58.4 us
  starting transfers between devices: 0.05 us -> 61.5 us
  Pallas kernels: 0 us -> 37 us
  local copies, waits for them, and re-layouts: 53.2 us -> 19.7 us
  matrix products: 31.4 us -> 0 us
  between operations: 14.9 us -> 0.33 us
  other arithmetic: 14.4 us -> 7.53 us
    psum x1 -> x0, waiting for transfers between devices: 178 us -> none  [spread(): return lax.psum(kept, axis)]
    ppermute x0 -> x33, starting transfers between devices: none -> 61.5 us  [the longest x26 48.7 us: send(): return lax.ppermute(value, ('row', 'col'), torus(step))]
    ppermute x0 -> x33, waiting for transfers between devices: none -> 58.4 us  [the longest x26 40.3 us: send(): return lax.ppermute(value, ('row', 'col'), torus(step))]
    pallas_call x0 -> x7, Pallas kernels: none -> 37 us  [the longest x1 19 us: update(): pl.pallas_call(body, in_specs=[SMEM] * 5 + [VMEM] * 9, out_specs=ANY, out...]
    dot_general x1 -> x0, matrix products: 31.4 us -> none  [contract(): lax.dot_general(left_block, right_block, (((0,), (0,)), ((), ())), precis...]
    scatter x2 -> x0, local copies, waits for them, and re-layouts: 29 us -> none  [per_device(): matrix.at[local_target]]
    unnamed x5 -> x60, local copies, waits for them, and re-layouts: 7.78 us -> 19.6 us
    select_n x1 -> x0, local copies, waits for them, and re-layouts: 8.94 us -> none  [per_device(): return jnp.where(global_rows < top, product, swapped - product)]
  transfers between devices with their start and end apart: 2 -> 33, of which waited for: 1 -> 12; matrix products, arithmetic and copies ran while one was open for 13% -> 4% of each run, Pallas kernels for 0% -> 7%
where the time goes in v3:
time: 185 us; the launch traced here: 184 us
  starting transfers between devices  61.5 us (33%)
  waiting for transfers between devices  58.4 us (32%)
  Pallas kernels  37 us (20%)
  local copies, waits for them, and re-layouts  19.7 us (11%)
  other arithmetic  7.53 us (4%)
    ppermute x26, starting transfers between devices, send(): return lax.ppermute(value, ('row', 'col'), torus(step))  48.7 us
    ppermute x26, waiting for transfers between devices, send(): return lax.ppermute(value, ('row', 'col'), torus(step))  40.3 us
    unnamed x60, local copies, waits for them, and re-layouts  19.6 us
    pallas_call x1, Pallas kernels, update(): pl.pallas_call(body, in_specs=[SMEM] * 5 + [VMEM] * 9, out_specs=ANY, out...  19 us
    ppermute x7, waiting for transfers between devices, send_row(): return lax.ppermute(value, 'row', row_pairs(dx, dy, keep))  18 us
    ppermute x7, starting transfers between devices, send_row(): return lax.ppermute(value, 'row', row_pairs(dx, dy, keep))  12.8 us
    pallas_call x2, Pallas kernels, load(): pl.pallas_call(body, in_specs=[ANY] * n if into is None else [VMEM] * (n...  9.18 us
    pallas_call x2, Pallas kernels, gather_rows(): pl.pallas_call(functools.partial(gather_body, h), in_specs=[SMEM, SMEM, V...  5.47 us
  transfers between devices with their start and end apart: 33, of which 12 were waited for; matrix products, arithmetic and copies ran while one was open for 4% of the time, Pallas kernels for 7%

profile of v3, /device:TPU:1, one launch (start us, length us, event | category | flops | bytes accessed | tf_op | source)
XLA Modules:
  0.0 184.4 jit_solution(3572394401824172692)
XLA Ops:
  0.8 2.4 %row_index.1 = (s32[1,1024]{1,0:T(1,128)S(1)}, s32[1,1024]{1,0:T(1,128)S(1)}) custom-call(s32[4]{0:T(128)S(1)} %pad_add_fusion.where, s32[1,1024]{1,0:T(1,128)S(1)} %bitcast.24), custom_call_target="tpu_custom_call" | custom-call | bytes 1048576 | tf_op jit(solution)/shard_map/row_index/pallas_call | solution.py:122
  3.2 3.4 %copy-done = f32[4096,512]{1,0:T(8,128)S(1)} copy-done((f32[4096,512]{1,0:T(8,128)S(1)}, f32[4096,512]{1,0:T(8,128)}, u32[]{:S(2)}) %copy-start) | copy-done | bytes 8388632
  6.6 2.7 %gather_rows.2 = (f32[128,512]{1,0:T(8,128)S(1)}, f32[128,512]{1,0:T(8,128)S(1)}, f32[128,512]{1,0:T(8,128)S(1)}, f32[128,512]{1,0:T(8,128)S(1)}) custom-call(s32[1,1024]{1,0:T(1,128)S(1)} %get-tuple-element.35.index, s32[4]{0:T(128)S(1)} %pad_add_fusion.where, f32[4096,512]{1,0:T(8,128)S(1)} %copy-done), custom_call_target="tpu_custom_call" | custom-call | bytes 6291456 | tf_op jit(solution)/shard_map/gather_rows/pallas_call | solution.py:152
  9.3 3.6 %collective-permute-start.17 = (f32[128,512]{1,0:T(8,128)S(1)}, f32[128,512]{1,0:T(8,128)}, u32[]{:S(2)}, u32[]{:S(2)}) collective-permute-start(f32[128,512]{1,0:T(8,128)S(1)} %get-tuple-element.39), channel_id=1, source_target_pairs={{0,48},{16,0},{32,16},{48,32},{64,112},{80,64},{96,80},{112,96},{1... | collective-permute-start | bytes 786440 | tf_op jit(solution)/shard_map/ppermute | solution.py:64
  14.0 2.7 %gather_rows.3 = (f32[128,512]{1,0:T(8,128)S(1)}, f32[128,512]{1,0:T(8,128)S(1)}, f32[128,512]{1,0:T(8,128)S(1)}, f32[128,512]{1,0:T(8,128)S(1)}) custom-call(s32[1,1024]{1,0:T(1,128)S(1)} %get-tuple-element.35.index, s32[4]{0:T(128)S(1)} %pad_add_fusion.where, f32[4096,512]{1,0:T(8,128)S(1)} %copy-done), custom_call_target="tpu_custom_call" | custom-call | bytes 6291456 | tf_op jit(solution)/shard_map/gather_rows/pallas_call | solution.py:152
  16.7 2.1 %collective-permute-start.21 = (f32[128,512]{1,0:T(8,128)S(1)}, f32[128,512]{1,0:T(8,128)}, u32[]{:S(2)}, u32[]{:S(2)}) collective-permute-start(f32[128,512]{1,0:T(8,128)S(1)} %get-tuple-element.43), channel_id=1, source_target_pairs={{0,48},{16,0},{32,16},{48,32},{64,112},{80,64},{96,80},{112,96},{1... | collective-permute-start | bytes 786440 | tf_op jit(solution)/shard_map/ppermute | solution.py:64
  20.3 2.1 %collective-permute-done.17 = f32[128,512]{1,0:T(8,128)} collective-permute-done((f32[128,512]{1,0:T(8,128)S(1)}, f32[128,512]{1,0:T(8,128)}, u32[]{:S(2)}, u32[]{:S(2)}) %collective-permute-start.17) | collective-permute-done | bytes 262176 | tf_op jit(solution)/shard_map/ppermute | solution.py:64
  22.4 7.3 %collective-permute-done.15 = f32[128,512]{1,0:T(8,128)} collective-permute-done((f32[128,512]{1,0:T(8,128)S(1)}, f32[128,512]{1,0:T(8,128)}, u32[]{:S(2)}, u32[]{:S(2)}) %collective-permute-start.15) | collective-permute-done | bytes 262176 | tf_op jit(solution)/shard_map/ppermute | solution.py:64
  31.0 2.8 %collective-permute-start.18 = (f32[128,512]{1,0:T(8,128)S(1)}, f32[128,512]{1,0:T(8,128)S(1)}, u32[]{:S(2)}, u32[]{:S(2)}) collective-permute-start(f32[128,512]{1,0:T(8,128)S(1)} %get-tuple-element.51), channel_id=1, source_target_pairs={{0,64},{1,65},{2,66},{3,67},{4,68},{5,69},{6,70},{7,71},{8,72},{9,... | collective-permute-start | bytes 786440 | tf_op jit(solution)/shard_map/ppermute | solution.py:24
  34.6 4.8 %collective-permute-done.19 = f32[128,512]{1,0:T(8,128)S(1)} collective-permute-done((f32[128,512]{1,0:T(8,128)S(1)}, f32[128,512]{1,0:T(8,128)S(1)}, u32[]{:S(2)}, u32[]{:S(2)}) %collective-permute-start.19) | collective-permute-done | bytes 262176 | tf_op jit(solution)/shard_map/ppermute | solution.py:64
  40.7 2.8 %collective-permute-start.22 = (f32[128,512]{1,0:T(8,128)S(1)}, f32[128,512]{1,0:T(8,128)S(1)}, u32[]{:S(2)}, u32[]{:S(2)}) collective-permute-start(f32[128,512]{1,0:T(8,128)S(1)} %get-tuple-element.53), channel_id=1, source_target_pairs={{0,64},{1,65},{2,66},{3,67},{4,68},{5,69},{6,70},{7,71},{8,72},{9,... | collective-permute-start | bytes 786440 | tf_op jit(solution)/shard_map/ppermute | solution.py:24
  44.0 5.6 %collective-permute-done.22 = f32[128,512]{1,0:T(8,128)S(1)} collective-permute-done((f32[128,512]{1,0:T(8,128)S(1)}, f32[128,512]{1,0:T(8,128)S(1)}, u32[]{:S(2)}, u32[]{:S(2)}) %collective-permute-start.22) | collective-permute-done | bytes 262176 | tf_op jit(solution)/shard_map/ppermute | solution.py:24
  49.7 1.5 collective-permute-start.25
  51.2 4.2 %collective-permute-start.4 = (f32[64,4096]{1,0:T(8,128)S(1)}, f32[64,4096]{1,0:T(8,128)S(1)}, u32[]{:S(2)}, u32[]{:S(2)}) collective-permute-start(f32[64,4096]{1,0:T(8,128)S(1)} %copy-done.1), channel_id=1, source_target_pairs={{0,1},{1,0},{2,3},{3,2},{4,5},{5,4},{6,7},{7,6},{8,9},{9,8},{10,11... | collective-permute-start | bytes 3145736 | tf_op jit(solution)/shard_map/ppermute | solution.py:24
  55.4 3.8 %collective-permute-start.6 = (f32[64,4096]{1,0:T(8,128)S(1)}, f32[64,4096]{1,0:T(8,128)S(1)}, u32[]{:S(2)}, u32[]{:S(2)}) collective-permute-start(f32[64,4096]{1,0:T(8,128)S(1)} %copy-done.1), channel_id=1, source_target_pairs={{0,2},{1,7},{2,4},{3,1},{4,6},{5,3},{6,0},{7,5},{8,10},{9,15},{10,... | collective-permute-start | bytes 3145736 | tf_op jit(solution)/shard_map/ppermute | solution.py:24
  59.3 6.7 %collective-permute-done.26.refs_5_ = f32[128,512]{1,0:T(8,128)S(1)} collective-permute-done((f32[128,512]{1,0:T(8,128)S(1)}, f32[128,512]{1,0:T(8,128)S(1)}, u32[]{:S(2)}, u32[]{:S(2)}) %collective-permute-start.26) | collective-permute-done | bytes 262176 | tf_op jit(solution)/shard_map/ppermute | solution.py:24
  66.6 4.7 %collective-permute-start.29 = (f32[256,512]{1,0:T(8,128)S(1)}, f32[256,512]{1,0:T(8,128)S(1)}, u32[]{:S(2)}, u32[]{:S(2)}) collective-permute-start(f32[256,512]{1,0:T(8,128)S(1)} %pad_maximum_fusion), channel_id=1, source_target_pairs={{0,64},{16,80},{32,96},{48,112},{1,65},{17,81},{33,97},{49,113},{2... | collective-permute-start | bytes 1572872 | tf_op jit(solution)/shard_map/ppermute | solution.py:64
  72.3 3.8 %collective-permute-start.1 = (f32[64,4096]{1,0:T(8,128)S(1)}, f32[64,4096]{1,0:T(8,128)}, u32[]{:S(2)}, u32[]{:S(2)}) collective-permute-start(f32[64,4096]{1,0:T(8,128)S(1)} %collective-permute-done.refs_2_), channel_id=1, source_target_pairs={{0,2},{1,7},{2,4},{3,1},{4,6},{5,3},{6,0},{7,5},{8,10},{9,15},{10,... | collective-permute-start | bytes 3145736 | tf_op jit(solution)/shard_map/ppermute | solution.py:24
  76.0 3.0 %collective-permute-done.29 = f32[256,512]{1,0:T(8,128)S(1)} collective-permute-done((f32[256,512]{1,0:T(8,128)S(1)}, f32[256,512]{1,0:T(8,128)S(1)}, u32[]{:S(2)}, u32[]{:S(2)}) %collective-permute-start.29) | collective-permute-done | bytes 524320 | tf_op jit(solution)/shard_map/ppermute | solution.py:64
  79.0 4.7 %collective-permute-start.5 = (f32[64,4096]{1,0:T(8,128)S(1)}, f32[64,4096]{1,0:T(8,128)S(1)}, u32[]{:S(2)}, u32[]{:S(2)}) collective-permute-start(f32[64,4096]{1,0:T(8,128)S(1)} %collective-permute-done.refs_2_), channel_id=1, source_target_pairs={{0,1},{1,0},{2,3},{3,2},{4,5},{5,4},{6,7},{7,6},{8,9},{9,8},{10,11... | collective-permute-start | bytes 3145736 | tf_op jit(solution)/shard_map/ppermute | solution.py:24
  84.0 1.6 collective-permute-done.8.refs_6_
  87.9 8.8 %collective-permute-done.28.refs_7_ = f32[128,512]{1,0:T(8,128)S(1)} collective-permute-done((f32[128,512]{1,0:T(8,128)S(1)}, f32[128,512]{1,0:T(8,128)S(1)}, u32[]{:S(2)}, u32[]{:S(2)}) %collective-permute-start.28) | collective-permute-done | bytes 262176 | tf_op jit(solution)/shard_map/ppermute | solution.py:24
  98.6 2.2 %collective-permute-start.13 = (f32[64,4096]{1,0:T(8,128)S(1)}, f32[64,4096]{1,0:T(8,128)}, u32[]{:S(2)}, u32[]{:S(2)}) collective-permute-start(f32[64,4096]{1,0:T(8,128)S(1)} %collective-permute-done.6.refs_4_), channel_id=1, source_target_pairs={{0,2},{1,7},{2,4},{3,1},{4,6},{5,3},{6,0},{7,5},{8,10},{9,15},{10,... | collective-permute-start | bytes 3145736 | tf_op jit(solution)/shard_map/ppermute | solution.py:24
  103.2 3.0 %collective-permute-start.9 = (f32[64,4096]{1,0:T(8,128)}, f32[64,4096]{1,0:T(8,128)}, u32[]{:S(2)}, u32[]{:S(2)}) collective-permute-start(f32[64,4096]{1,0:T(8,128)} %collective-permute-done.8.refs_6_), channel_id=1, source_target_pairs={{0,1},{1,0},{2,3},{3,2},{4,5},{5,4},{6,7},{7,6},{8,9},{9,8},{10,11... | collective-permute-start | bytes 3145736 | tf_op jit(solution)/shard_map/ppermute | solution.py:24
  107.2 9.9 %collective-permute-done.11.refs_10_ = f32[64,4096]{1,0:T(8,128)} collective-permute-done((f32[64,4096]{1,0:T(8,128)S(1)}, f32[64,4096]{1,0:T(8,128)}, u32[]{:S(2)}, u32[]{:S(2)}) %collective-permute-start.11) | collective-permute-done | bytes 1048608 | tf_op jit(solution)/shard_map/ppermute | solution.py:24
  117.2 11.4 %collective-permute-start.12 = (f32[64,4096]{1,0:T(8,128)}, f32[64,4096]{1,0:T(8,128)}, u32[]{:S(2)}, u32[]{:S(2)}) collective-permute-start(f32[64,4096]{1,0:T(8,128)} %collective-permute-done.11.refs_10_), channel_id=1, source_target_pairs={{0,1},{1,0},{2,3},{3,2},{4,5},{5,4},{6,7},{7,6},{8,9},{9,8},{10,11... | collective-permute-start | bytes 3145736 | tf_op jit(solution)/shard_map/ppermute | solution.py:24
  128.7 6.6 %collective-permute-done.2.refs_0_ = f32[64,4096]{1,0:T(8,128)} collective-permute-done((f32[64,4096]{1,0:T(8,128)}, f32[64,4096]{1,0:T(8,128)}, u32[]{:S(2)}, u32[]{:S(2)}) %collective-permute-start.2) | collective-permute-done | bytes 1048608 | tf_op jit(solution)/shard_map/ppermute | solution.py:24
  136.2 2.8 %collective-permute-start.32 = (f32[256,512]{1,0:T(8,128)}, f32[256,512]{1,0:T(8,128)}, u32[]{:S(2)}, u32[]{:S(2)}) collective-permute-start(f32[256,512]{1,0:T(8,128)} %copy-done.26), channel_id=1, source_target_pairs={{0,16},{1,49},{2,18},{3,51},{4,20},{5,53},{6,22},{7,55},{8,24},{9,... | collective-permute-start | bytes 1572872 | tf_op jit(solution)/shard_map/ppermute | solution.py:24
  139.1 4.4 %sort.31 = (s32[1024]{0:T(1024)S(1)}, s32[1024]{0:T(1024)S(1)}, s32[1024]{0:T(1024)S(1)}, s32[1024]{0:T(1024)}) sort(s32[1024]{0:T(1024)S(1)} %subtract_select_fusion, s32[1024]{0:T(1024)S(1)} %fusion.9, s32[1024]{0:T(1024)S(1)} %bitcast.25, s32[1024]{0:T(1024)S(1)} %iota.15), dimensions={0}, to_apply=%region_1.2 | sort | flops 10240 | bytes 32768 | tf_op jit(solution)/shard_map/sort | solution.py:347
  155.1 7.2 %shard_map.37 = (bf16[1024,4096]{1,0:T(8,128)(2,1)S(1)}, bf16[1024,4096]{1,0:T(8,128)(2,1)S(1)}) custom-call(f32[64,4096]{1,0:T(8,128)S(1)} %copy-done.1, f32[64,4096]{1,0:T(8,128)S(1)} %collective-permute-done.4.refs_1_, f32[64,4096]{1,0:T(8,128)S(1)} %collective-permute-done.refs_2_, f32[64,4096]{1,0:T(8,128)S(1)} %copy-done.5, f32[64,4096]{1,0:T(8,128)S(1)} %copy-done.3, ...), custom_call_target="tpu_custom_call" | custom-call | bytes 14680064 | tf_op jit(solution)/shard_map/pallas_call | solution.py:217
  162.4 2.0 %shard_map.38 = (bf16[1024,4096]{1,0:T(8,128)(2,1)S(1)}, bf16[1024,4096]{1,0:T(8,128)(2,1)S(1)}) custom-call(f32[64,4096]{1,0:T(8,128)} %collective-permute-done.2.refs_0_, f32[64,4096]{1,0:T(8,128)} %collective-permute-done.3.refs_1_, bf16[1024,4096]{1,0:T(8,128)(2,1)S(1)} %get-tuple-element.31.refs_2_, ...), custom_call_target="tpu_custom_call", output_to_operand_aliasing={{0}: (2, {}), {1}: (3, {})} | custom-call | bytes 2097152 | tf_op jit(solution)/shard_map/pallas_call | solution.py:217
  165.4 19.0 %update.1 = f32[4096,512]{1,0:T(8,128)} custom-call(s32[19]{0:T(128)S(1)} %stack.91.order, s32[9]{0:T(128)S(1)} %convert_reduce_fusion.starts, s32[1024]{0:T(1024)S(1)} %get-tuple-element.28.keys, s32[1024]{0:T(1024)S(1)} %get-tuple-element.29.spares, s32[1024]{0:T(1024)S(1)} %get-tuple-element.30.slots, bf16[1024,4096]{1,0:T(8,128)(2,1)S(1)} %get-tuple-element.33.ph, ...), custom_call_target="tpu_custom_call" | custom-call | flops 12884901888 | bytes 8388608 | tf_op jit(solution)/shard_map/update/pallas_call | solution.py:265
  (119 shorter events, 30.5 us)
Async XLA Ops:
  9.3 13.1 %collective-permute-start.17 = (f32[128,512]{1,0:T(8,128)S(1)}, f32[128,512]{1,0:T(8,128)}, u32[]{:S(2)}, u32[]{:S(2)}) collective-permute-start(f32[128,512]{1,0:T(8,128)S(1)} %get-tuple-element.39), channel_id=1, source_target_pairs={{0,48},{16,0},{32,16},{48,32},{64,112},{80,64},{96,80},{112,96},{1... | collective-permute-start | bytes 786440 | tf_op jit(solution)/shard_map/ppermute | solution.py:64
  12.9 9.5 %collective-permute-start.16 = (f32[128,512]{1,0:T(8,128)S(1)}, f32[128,512]{1,0:T(8,128)}, u32[]{:S(2)}, u32[]{:S(2)}) collective-permute-start(f32[128,512]{1,0:T(8,128)S(1)} %get-tuple-element.38), channel_id=1, source_target_pairs={{0,32},{16,48},{32,0},{48,16},{64,96},{80,112},{96,64},{112,80},{1... | collective-permute-start | bytes 786440 | tf_op jit(solution)/shard_map/ppermute | solution.py:64
  13.3 16.4 %collective-permute-start.15 = (f32[128,512]{1,0:T(8,128)S(1)}, f32[128,512]{1,0:T(8,128)}, u32[]{:S(2)}, u32[]{:S(2)}) collective-permute-start(f32[128,512]{1,0:T(8,128)S(1)} %get-tuple-element.37), channel_id=1, source_target_pairs={{0,16},{16,32},{32,48},{48,0},{64,80},{80,96},{96,112},{112,64},{1... | collective-permute-start | bytes 786440 | tf_op jit(solution)/shard_map/ppermute | solution.py:64
  16.7 17.9 %collective-permute-start.21 = (f32[128,512]{1,0:T(8,128)S(1)}, f32[128,512]{1,0:T(8,128)}, u32[]{:S(2)}, u32[]{:S(2)}) collective-permute-start(f32[128,512]{1,0:T(8,128)S(1)} %get-tuple-element.43), channel_id=1, source_target_pairs={{0,48},{16,0},{32,16},{48,32},{64,112},{80,64},{96,80},{112,96},{1... | collective-permute-start | bytes 786440 | tf_op jit(solution)/shard_map/ppermute | solution.py:64
  18.8 15.9 %collective-permute-start.20 = (f32[128,512]{1,0:T(8,128)S(1)}, f32[128,512]{1,0:T(8,128)}, u32[]{:S(2)}, u32[]{:S(2)}) collective-permute-start(f32[128,512]{1,0:T(8,128)S(1)} %get-tuple-element.42), channel_id=1, source_target_pairs={{0,32},{16,48},{32,0},{48,16},{64,96},{80,112},{96,64},{112,80},{1... | collective-permute-start | bytes 786440 | tf_op jit(solution)/shard_map/ppermute | solution.py:64
  22.4 17.1 %collective-permute-start.19 = (f32[128,512]{1,0:T(8,128)S(1)}, f32[128,512]{1,0:T(8,128)S(1)}, u32[]{:S(2)}, u32[]{:S(2)}) collective-permute-start(f32[128,512]{1,0:T(8,128)S(1)} %get-tuple-element.41), channel_id=1, source_target_pairs={{0,16},{16,32},{32,48},{48,0},{64,80},{80,96},{96,112},{112,64},{1... | collective-permute-start | bytes 786440 | tf_op jit(solution)/shard_map/ppermute | solution.py:64
  31.0 12.9 %collective-permute-start.18 = (f32[128,512]{1,0:T(8,128)S(1)}, f32[128,512]{1,0:T(8,128)S(1)}, u32[]{:S(2)}, u32[]{:S(2)}) collective-permute-start(f32[128,512]{1,0:T(8,128)S(1)} %get-tuple-element.51), channel_id=1, source_target_pairs={{0,64},{1,65},{2,66},{3,67},{4,68},{5,69},{6,70},{7,71},{8,72},{9,... | collective-permute-start | bytes 786440 | tf_op jit(solution)/shard_map/ppermute | solution.py:24
  40.7 8.9 %collective-permute-start.22 = (f32[128,512]{1,0:T(8,128)S(1)}, f32[128,512]{1,0:T(8,128)S(1)}, u32[]{:S(2)}, u32[]{:S(2)}) collective-permute-start(f32[128,512]{1,0:T(8,128)S(1)} %get-tuple-element.53), channel_id=1, source_target_pairs={{0,64},{1,65},{2,66},{3,67},{4,68},{5,69},{6,70},{7,71},{8,72},{9,... | collective-permute-start | bytes 786440 | tf_op jit(solution)/shard_map/ppermute | solution.py:24
  43.5 28.7 %collective-permute-start = (f32[64,4096]{1,0:T(8,128)S(1)}, f32[64,4096]{1,0:T(8,128)S(1)}, u32[]{:S(2)}, u32[]{:S(2)}) collective-permute-start(f32[64,4096]{1,0:T(8,128)S(1)} %copy-done.1), channel_id=1, source_target_pairs={{0,8},{1,9},{2,10},{3,11},{4,12},{5,13},{6,14},{7,15},{8,0},{9,1},... | collective-permute-start | bytes 3145736 | tf_op jit(solution)/shard_map/ppermute | solution.py:24
  43.9 11.5 %collective-permute-start.23 = (f32[128,512]{1,0:T(8,128)S(1)}, f32[128,512]{1,0:T(8,128)S(1)}, u32[]{:S(2)}, u32[]{:S(2)}) collective-permute-start(f32[128,512]{1,0:T(8,128)S(1)} %add.394.refs_0_), channel_id=1, source_target_pairs={{0,16},{1,49},{2,18},{3,51},{4,20},{5,53},{6,22},{7,55},{8,24},{9,... | collective-permute-start | bytes 786440 | tf_op jit(solution)/shard_map/ppermute | solution.py:24
  49.7 9.5 %collective-permute-start.24 = (f32[128,512]{1,0:T(8,128)S(1)}, f32[128,512]{1,0:T(8,128)S(1)}, u32[]{:S(2)}, u32[]{:S(2)}) collective-permute-start(f32[128,512]{1,0:T(8,128)S(1)} %add.400.refs_1_), channel_id=1, source_target_pairs={{0,16},{1,49},{2,18},{3,51},{4,20},{5,53},{6,22},{7,55},{8,24},{9,... | collective-permute-start | bytes 786440 | tf_op jit(solution)/shard_map/ppermute | solution.py:24
  49.7 9.4 %collective-permute-start.25 = (f32[128,512]{1,0:T(8,128)S(1)}, f32[128,512]{1,0:T(8,128)S(1)}, u32[]{:S(2)}, u32[]{:S(2)}) collective-permute-start(f32[128,512]{1,0:T(8,128)S(1)} %add.394.refs_0_), channel_id=1, source_target_pairs={{0,48},{1,17},{2,50},{3,19},{4,52},{5,21},{6,54},{7,23},{8,56},{9,... | collective-permute-start | bytes 786440 | tf_op jit(solution)/shard_map/ppermute | solution.py:24
  51.2 27.8 %collective-permute-start.4 = (f32[64,4096]{1,0:T(8,128)S(1)}, f32[64,4096]{1,0:T(8,128)S(1)}, u32[]{:S(2)}, u32[]{:S(2)}) collective-permute-start(f32[64,4096]{1,0:T(8,128)S(1)} %copy-done.1), channel_id=1, source_target_pairs={{0,1},{1,0},{2,3},{3,2},{4,5},{5,4},{6,7},{7,6},{8,9},{9,8},{10,11... | collective-permute-start | bytes 3145736 | tf_op jit(solution)/shard_map/ppermute | solution.py:24
  55.4 28.4 %collective-permute-start.6 = (f32[64,4096]{1,0:T(8,128)S(1)}, f32[64,4096]{1,0:T(8,128)S(1)}, u32[]{:S(2)}, u32[]{:S(2)}) collective-permute-start(f32[64,4096]{1,0:T(8,128)S(1)} %copy-done.1), channel_id=1, source_target_pairs={{0,2},{1,7},{2,4},{3,1},{4,6},{5,3},{6,0},{7,5},{8,10},{9,15},{10,... | collective-permute-start | bytes 3145736 | tf_op jit(solution)/shard_map/ppermute | solution.py:24
  59.1 26.5 %collective-permute-start.8 = (f32[64,4096]{1,0:T(8,128)S(1)}, f32[64,4096]{1,0:T(8,128)}, u32[]{:S(2)}, u32[]{:S(2)}) collective-permute-start(f32[64,4096]{1,0:T(8,128)S(1)} %copy-done.1), channel_id=1, source_target_pairs={{0,6},{1,3},{2,0},{3,5},{4,2},{5,7},{6,4},{7,1},{8,14},{9,11},{10,... | collective-permute-start | bytes 3145736 | tf_op jit(solution)/shard_map/ppermute | solution.py:24
  66.6 12.4 %collective-permute-start.29 = (f32[256,512]{1,0:T(8,128)S(1)}, f32[256,512]{1,0:T(8,128)S(1)}, u32[]{:S(2)}, u32[]{:S(2)}) collective-permute-start(f32[256,512]{1,0:T(8,128)S(1)} %pad_maximum_fusion), channel_id=1, source_target_pairs={{0,64},{16,80},{32,96},{48,112},{1,65},{17,81},{33,97},{49,113},{2... | collective-permute-start | bytes 1572872 | tf_op jit(solution)/shard_map/ppermute | solution.py:64
  72.3 28.6 %collective-permute-start.1 = (f32[64,4096]{1,0:T(8,128)S(1)}, f32[64,4096]{1,0:T(8,128)}, u32[]{:S(2)}, u32[]{:S(2)}) collective-permute-start(f32[64,4096]{1,0:T(8,128)S(1)} %collective-permute-done.refs_2_), channel_id=1, source_target_pairs={{0,2},{1,7},{2,4},{3,1},{4,6},{5,3},{6,0},{7,5},{8,10},{9,15},{10,... | collective-permute-start | bytes 3145736 | tf_op jit(solution)/shard_map/ppermute | solution.py:24
  79.0 8.0 %collective-permute-start.27 = (f32[128,512]{1,0:T(8,128)S(1)}, f32[128,512]{1,0:T(8,128)S(1)}, u32[]{:S(2)}, u32[]{:S(2)}) collective-permute-start(f32[128,512]{1,0:T(8,128)S(1)} %collective-permute-done.23.refs_2_), channel_id=1, source_target_pairs={{0,16},{1,49},{2,18},{3,51},{4,20},{5,53},{6,22},{7,55},{8,24},{9,... | collective-permute-start | bytes 786440 | tf_op jit(solution)/shard_map/ppermute | solution.py:24
  79.0 23.2 %collective-permute-start.5 = (f32[64,4096]{1,0:T(8,128)S(1)}, f32[64,4096]{1,0:T(8,128)S(1)}, u32[]{:S(2)}, u32[]{:S(2)}) collective-permute-start(f32[64,4096]{1,0:T(8,128)S(1)} %collective-permute-done.refs_2_), channel_id=1, source_target_pairs={{0,1},{1,0},{2,3},{3,2},{4,5},{5,4},{6,7},{7,6},{8,9},{9,8},{10,11... | collective-permute-start | bytes 3145736 | tf_op jit(solution)/shard_map/ppermute | solution.py:24
  83.8 22.4 %collective-permute-start.7 = (f32[64,4096]{1,0:T(8,128)S(1)}, f32[64,4096]{1,0:T(8,128)S(1)}, u32[]{:S(2)}, u32[]{:S(2)}) collective-permute-start(f32[64,4096]{1,0:T(8,128)S(1)} %collective-permute-done.6.refs_4_), channel_id=1, source_target_pairs={{0,1},{1,0},{2,3},{3,2},{4,5},{5,4},{6,7},{7,6},{8,9},{9,8},{10,11... | collective-permute-start | bytes 3145736 | tf_op jit(solution)/shard_map/ppermute | solution.py:24
  85.6 13.0 %collective-permute-start.30 = (f32[256,512]{1,0:T(8,128)S(1)}, f32[256,512]{1,0:T(8,128)S(1)}, u32[]{:S(2)}, u32[]{:S(2)}) collective-permute-start(f32[256,512]{1,0:T(8,128)S(1)} %broadcast_select_fusion.refs_0_), channel_id=1, source_target_pairs={{0,16},{1,49},{2,18},{3,51},{4,20},{5,53},{6,22},{7,55},{8,24},{9,... | collective-permute-start | bytes 1572872 | tf_op jit(solution)/shard_map/ppermute | solution.py:24
  87.7 9.1 %collective-permute-start.28 = (f32[128,512]{1,0:T(8,128)S(1)}, f32[128,512]{1,0:T(8,128)S(1)}, u32[]{:S(2)}, u32[]{:S(2)}) collective-permute-start(f32[128,512]{1,0:T(8,128)S(1)} %collective-permute-done.24.refs_3_), channel_id=1, source_target_pairs={{0,16},{1,49},{2,18},{3,51},{4,20},{5,53},{6,22},{7,55},{8,24},{9,... | collective-permute-start | bytes 786440 | tf_op jit(solution)/shard_map/ppermute | solution.py:24
  97.4 19.7 %collective-permute-start.11 = (f32[64,4096]{1,0:T(8,128)S(1)}, f32[64,4096]{1,0:T(8,128)}, u32[]{:S(2)}, u32[]{:S(2)}) collective-permute-start(f32[64,4096]{1,0:T(8,128)S(1)} %collective-permute-done.refs_2_), channel_id=1, source_target_pairs={{0,6},{1,3},{2,0},{3,5},{4,2},{5,7},{6,4},{7,1},{8,14},{9,11},{10,... | collective-permute-start | bytes 3145736 | tf_op jit(solution)/shard_map/ppermute | solution.py:24
  98.6 30.0 %collective-permute-start.13 = (f32[64,4096]{1,0:T(8,128)S(1)}, f32[64,4096]{1,0:T(8,128)}, u32[]{:S(2)}, u32[]{:S(2)}) collective-permute-start(f32[64,4096]{1,0:T(8,128)S(1)} %collective-permute-done.6.refs_4_), channel_id=1, source_target_pairs={{0,2},{1,7},{2,4},{3,1},{4,6},{5,3},{6,0},{7,5},{8,10},{9,15},{10,... | collective-permute-start | bytes 3145736 | tf_op jit(solution)/shard_map/ppermute | solution.py:24
  100.8 34.5 %collective-permute-start.2 = (f32[64,4096]{1,0:T(8,128)}, f32[64,4096]{1,0:T(8,128)}, u32[]{:S(2)}, u32[]{:S(2)}) collective-permute-start(f32[64,4096]{1,0:T(8,128)} %collective-permute-done.1.refs_8_), channel_id=1, source_target_pairs={{0,2},{1,7},{2,4},{3,1},{4,6},{5,3},{6,0},{7,5},{8,10},{9,15},{10,... | collective-permute-start | bytes 3145736 | tf_op jit(solution)/shard_map/ppermute | solution.py:24
  103.2 33.0 %collective-permute-start.9 = (f32[64,4096]{1,0:T(8,128)}, f32[64,4096]{1,0:T(8,128)}, u32[]{:S(2)}, u32[]{:S(2)}) collective-permute-start(f32[64,4096]{1,0:T(8,128)} %collective-permute-done.8.refs_6_), channel_id=1, source_target_pairs={{0,1},{1,0},{2,3},{3,2},{4,5},{5,4},{6,7},{7,6},{8,9},{9,8},{10,11... | collective-permute-start | bytes 3145736 | tf_op jit(solution)/shard_map/ppermute | solution.py:24
  107.2 29.0 %collective-permute-start.10 = (f32[64,4096]{1,0:T(8,128)}, f32[64,4096]{1,0:T(8,128)}, u32[]{:S(2)}, u32[]{:S(2)}) collective-permute-start(f32[64,4096]{1,0:T(8,128)} %collective-permute-done.1.refs_8_), channel_id=1, source_target_pairs={{0,1},{1,0},{2,3},{3,2},{4,5},{5,4},{6,7},{7,6},{8,9},{9,8},{10,11... | collective-permute-start | bytes 3145736 | tf_op jit(solution)/shard_map/ppermute | solution.py:24
  117.2 34.3 %collective-permute-start.12 = (f32[64,4096]{1,0:T(8,128)}, f32[64,4096]{1,0:T(8,128)}, u32[]{:S(2)}, u32[]{:S(2)}) collective-permute-start(f32[64,4096]{1,0:T(8,128)} %collective-permute-done.11.refs_10_), channel_id=1, source_target_pairs={{0,1},{1,0},{2,3},{3,2},{4,5},{5,4},{6,7},{7,6},{8,9},{9,8},{10,11... | collective-permute-start | bytes 3145736 | tf_op jit(solution)/shard_map/ppermute | solution.py:24
  128.6 22.9 %collective-permute-start.14 = (f32[64,4096]{1,0:T(8,128)}, f32[64,4096]{1,0:T(8,128)}, u32[]{:S(2)}, u32[]{:S(2)}) collective-permute-start(f32[64,4096]{1,0:T(8,128)} %collective-permute-done.13.refs_12_), channel_id=1, source_target_pairs={{0,1},{1,0},{2,3},{3,2},{4,5},{5,4},{6,7},{7,6},{8,9},{9,8},{10,11... | collective-permute-start | bytes 3145736 | tf_op jit(solution)/shard_map/ppermute | solution.py:24
  135.3 27.0 %collective-permute-start.3 = (f32[64,4096]{1,0:T(8,128)}, f32[64,4096]{1,0:T(8,128)}, u32[]{:S(2)}, u32[]{:S(2)}) collective-permute-start(f32[64,4096]{1,0:T(8,128)} %collective-permute-done.2.refs_0_), channel_id=1, source_target_pairs={{0,1},{1,0},{2,3},{3,2},{4,5},{5,4},{6,7},{7,6},{8,9},{9,8},{10,11... | collective-permute-start | bytes 3145736 | tf_op jit(solution)/shard_map/ppermute | solution.py:24
  136.2 28.1 %collective-permute-start.31 = (f32[256,512]{1,0:T(8,128)}, f32[256,512]{1,0:T(8,128)}, u32[]{:S(2)}, u32[]{:S(2)}) collective-permute-start(f32[256,512]{1,0:T(8,128)} %copy-done.10), channel_id=1, source_target_pairs={{0,48},{1,17},{2,50},{3,19},{4,52},{5,21},{6,54},{7,23},{8,56},{9,... | collective-permute-start | bytes 1572872 | tf_op jit(solution)/shard_map/ppermute | solution.py:24
  136.2 28.2 %collective-permute-start.32 = (f32[256,512]{1,0:T(8,128)}, f32[256,512]{1,0:T(8,128)}, u32[]{:S(2)}, u32[]{:S(2)}) collective-permute-start(f32[256,512]{1,0:T(8,128)} %copy-done.26), channel_id=1, source_target_pairs={{0,16},{1,49},{2,18},{3,51},{4,20},{5,53},{6,22},{7,55},{8,24},{9,... | collective-permute-start | bytes 1572872 | tf_op jit(solution)/shard_map/ppermute | solution.py:24
  (31 other events, 417.0 us)

commit v4 on v3

--- a/solution.py
+++ b/solution.py
@@ -69,6 +69,7 @@
 VMEM = pl.BlockSpec(memory_space=pltpu.VMEM)
 ANY = pl.BlockSpec(memory_space=pl.ANY)
 SMEM = pl.BlockSpec(memory_space=pltpu.SMEM)
+HBM = pl.BlockSpec(memory_space=pltpu.HBM)
 
 
 def params(mib):
@@ -125,7 +126,7 @@
         out_specs=[VMEM] * 2,
         out_shape=[shape] * 2,
         compiler_params=params(6),
-        cost_estimate=pl.CostEstimate(flops=0, bytes_accessed=1 << 20, transcendentals=0),
+        cost_estimate=pl.CostEstimate(flops=6 << 30, bytes_accessed=1 << 20, transcendentals=0),
         name="row_index",
     )(where, line)
 
@@ -216,7 +217,7 @@
 
     return pl.pallas_call(
         body,
-        in_specs=[ANY] * n if into is None else [VMEM] * (n + 2),
+        in_specs=[HBM] + [ANY] * (n - 1) if into is None else [VMEM] * (n + 2),
         out_specs=[VMEM] * 2,
         out_shape=[jax.ShapeDtypeStruct((16 * KP, m), jnp.bfloat16)] * 2,
         input_output_aliases={} if into is None else {n: 0, n + 1: 1},
@@ -225,22 +226,66 @@
     )(*pieces, *([] if into is None else into))
 
 
-def update(scalars, panel, bh, bl, matrix, parts):
+def update_left(scalars, panel, bh, bl, matrix):
     rows, n = matrix.shape
-    nblk = rows // MB
-
-    def body(order, starts, keys, spares, slots, ph, pw, bh, bl, matrix, *refs):
-        parts, (out, disp) = refs[:4], refs[4:]
+    half = rows // 2
+
+    def body(order, starts, keys, spares, ph, pw, bh, bl, matrix, out):
+        root = order[17]
+
+        def block_step(block, carry):
+            at = pl.ds(pl.multiple_of(block * MB, MB), MB)
+            in_top = (root == 1) & (block < 1024 // MB)
+            acc = dots(bh[...], bl[...], ph[:, at], pw[:, at])
+            out[at, :] = jnp.where(in_top, 0.0, matrix[at, :]) + jnp.where(in_top, 1.0, -1.0) * acc
+            return carry
+
+        lax.fori_loop(0, half // MB, block_step, 0)
+
+        def patch(k, carry):
+            r = pl.ds(keys[k], 1)
+            line = jnp.where(root == 1, matrix[pl.ds(spares[k], 1), :], 0.0)
+            out[r, :] += line - matrix[r, :]
+            return carry
+
+        lax.fori_loop(0, starts[half // MB], patch, 0)
+
+    return pl.pallas_call(
+        body,
+        in_specs=[SMEM] * 4 + [VMEM] * 5,
+        out_specs=VMEM,
+        out_shape=jax.ShapeDtypeStruct((half, n), jnp.float32),
+        compiler_params=params(14),
+        cost_estimate=pl.CostEstimate(flops=3 * rows * n * 1024, bytes_accessed=1 << 20, transcendentals=0),
+        name="update_left",
+    )(*scalars, *panel, bh, bl, matrix)
+
+
+def update_right(scalars, panel, bh, bl, matrix, left, parts):
+    rows, n = matrix.shape
+    first = rows // 2 // MB
+
+    def body(order, starts, keys, spares, slots, ph, pw, bh, bl, matrix, _, *refs):
+        parts, (out, left, disp, sem) = refs[:4], refs[4:]
         root = order[17]
         for i, part in enumerate(parts):
             disp[i * 256 : (i + 1) * 256, :] = part[...]
 
+        @pl.when(root == 0)
+        def _():
+            def one(k, carry):
+                left[pl.ds(keys[k], 1), :] += disp[pl.ds(slots[k], 1), :]
+                return carry
+
+            lax.fori_loop(0, starts[first], one, 0)
+
+        away = pltpu.make_async_copy(left, out.at[pl.ds(0, first * MB), :], sem)
+        away.start()
+
         def block_step(dest):
-            block = pl.program_id(0)
+            block = pl.program_id(0) + first
             at = pl.ds(pl.multiple_of(block * MB, MB), MB)
-            in_top = (root == 1) & (block < 1024 // MB)
-            acc = dots(bh[...], bl[...], ph[:, at], pw[:, at])
-            dest[...] = jnp.where(in_top, 0.0, matrix[at, :]) + jnp.where(in_top, 1.0, -1.0) * acc
+            dest[...] = matrix[at, :] - dots(bh[...], bl[...], ph[:, at], pw[:, at])
 
             def patch(source, rows_of):
                 def one(k, carry):
@@ -259,19 +304,21 @@
                 patch(disp, slots)
 
         pltpu.emit_pipeline(
-            block_step, grid=(nblk,), in_specs=[], out_specs=[pl.BlockSpec((MB, n), lambda i: (i, 0))]
+            block_step, grid=(first,), in_specs=[], out_specs=[pl.BlockSpec((MB, n), lambda i: (i + first, 0))]
         )(out)
+        away.wait()
 
     return pl.pallas_call(
         body,
-        in_specs=[SMEM] * 5 + [VMEM] * 9,
-        out_specs=ANY,
-        out_shape=jax.ShapeDtypeStruct(matrix.shape, jnp.float32),
-        scratch_shapes=[pltpu.VMEM((1024, n), jnp.float32)],
+        in_specs=[SMEM] * 5 + [VMEM] * 10,
+        out_specs=[ANY, VMEM],
+        out_shape=[jax.ShapeDtypeStruct(matrix.shape, jnp.float32), jax.ShapeDtypeStruct(left.shape, jnp.float32)],
+        scratch_shapes=[pltpu.VMEM((1024, n), jnp.float32), pltpu.SemaphoreType.DMA],
+        input_output_aliases={10: 1},
         compiler_params=params(14),
-        cost_estimate=pl.CostEstimate(flops=6 * rows * n * 1024, bytes_accessed=8 << 20, transcendentals=0),
-        name="update",
-    )(*scalars, *panel, bh, bl, matrix, *parts)
+        cost_estimate=pl.CostEstimate(flops=3 * rows * n * 1024, bytes_accessed=8 << 20, transcendentals=0),
+        name="update_right",
+    )(*scalars, *panel, bh, bl, matrix, left, *parts)[0]
 
 
 def step(matrix, pivots, lower_panel):
@@ -351,7 +398,8 @@
     bh, bl = prep(order, [full_a, full_b, a_a, a_b, b_a, b_b, f_a, f_b])
     panel = load(0, pieces[:14])
     panel = load(14, pieces[14:], panel)
-    return update((order, starts, keys, spares, slots), panel, bh, bl, matrix, [disp, a_d, b_d, f_d])
+    left = update_left((order, starts, keys, spares), panel, bh, bl, matrix)
+    return update_right((order, starts, keys, spares, slots), panel, bh, bl, matrix, left, [disp, a_d, b_d, f_d])
 
 
 def solution(mesh):

time: 185 us -> 185 us (level)
  waiting for transfers between devices: 58.4 us -> 56 us
    ppermute x7, waiting for transfers between devices: 18 us -> 11.9 us  [send_row(): return lax.ppermute(value, 'row', row_pairs(dx, dy, keep))]
    ppermute x26, waiting for transfers between devices: 40.3 us -> 44.1 us  [send(): return lax.ppermute(value, ('row', 'col'), torus(step))]
    ppermute x7, starting transfers between devices: 12.8 us -> 16.4 us  [send_row(): return lax.ppermute(value, 'row', row_pairs(dx, dy, keep))]
    ppermute x26, starting transfers between devices: 48.7 us -> 45.4 us  [send(): return lax.ppermute(value, ('row', 'col'), torus(step))]
    unnamed x60 -> x56, local copies, waits for them, and re-layouts: 19.6 us -> 20.2 us
    pallas_call x3 -> x4, Pallas kernels: 28.1 us -> 28.2 us  [the longest x1 10.4 us: update_right(): pl.pallas_call(body, in_specs=[SMEM] * 5 + [VMEM] * 10, out_specs=[ANY, V...]
  transfers between devices with their start and end apart: 33 -> 33, of which waited for: 12 -> 12; matrix products, arithmetic and copies ran while one was open for 4% -> 4% of each run, Pallas kernels for 7% -> 15%
where the time goes in v4:
time: 185 us; the launch traced here: 184 us
  starting transfers between devices  61.8 us (33%)
  waiting for transfers between devices  56 us (30%)
  Pallas kernels  37.9 us (20%)
  local copies, waits for them, and re-layouts  20.3 us (11%)
  other arithmetic  7.44 us (4%)
    ppermute x26, starting transfers between devices, send(): return lax.ppermute(value, ('row', 'col'), torus(step))  45.4 us
    ppermute x26, waiting for transfers between devices, send(): return lax.ppermute(value, ('row', 'col'), torus(step))  44.1 us
    unnamed x56, local copies, waits for them, and re-layouts  20.2 us
    ppermute x7, starting transfers between devices, send_row(): return lax.ppermute(value, 'row', row_pairs(dx, dy, keep))  16.4 us
    ppermute x7, waiting for transfers between devices, send_row(): return lax.ppermute(value, 'row', row_pairs(dx, dy, keep))  11.9 us
    pallas_call x1, Pallas kernels, update_right(): pl.pallas_call(body, in_specs=[SMEM] * 5 + [VMEM] * 10, out_specs=[ANY, V...  10.4 us
    pallas_call x2, Pallas kernels, load(): pl.pallas_call(body, in_specs=[HBM] + [ANY] * (n - 1) if into is None els...  9.18 us
    pallas_call x1, Pallas kernels, update_left(): pl.pallas_call(body, in_specs=[SMEM] * 4 + [VMEM] * 5, out_specs=VMEM, ou...  8.59 us
  transfers between devices with their start and end apart: 33, of which 12 were waited for; matrix products, arithmetic and copies ran while one was open for 4% of the time, Pallas kernels for 15%

profile of v4, /device:TPU:1, one launch (start us, length us, event | category | flops | bytes accessed | tf_op | source)
XLA Modules:
  0.0 183.9 jit_solution(4813898054188632828)
XLA Ops:
  0.0 2.0 %collective-permute-start = (f32[64,4096]{1,0:T(8,128)}, f32[64,4096]{1,0:T(8,128)S(1)}, u32[]{:S(2)}, u32[]{:S(2)}) collective-permute-start(f32[64,4096]{1,0:T(8,128)} %refs_0_.1), channel_id=1, source_target_pairs={{0,8},{1,9},{2,10},{3,11},{4,12},{5,13},{6,14},{7,15},{8,0},{9,1},... | collective-permute-start | bytes 3145736 | tf_op jit(solution)/shard_map/ppermute | solution.py:24
  2.8 2.4 %row_index.1 = (s32[1,1024]{1,0:T(1,128)S(1)}, s32[1,1024]{1,0:T(1,128)S(1)}) custom-call(s32[4]{0:T(128)S(1)} %pad_add_fusion.where, s32[1,1024]{1,0:T(1,128)S(1)} %bitcast.24), custom_call_target="tpu_custom_call" | custom-call | flops 6442450944 | bytes 1048576 | tf_op jit(solution)/shard_map/row_index/pallas_call | solution.py:123
  6.2 3.6 %gather_rows.2 = (f32[128,512]{1,0:T(8,128)}, f32[128,512]{1,0:T(8,128)}, f32[128,512]{1,0:T(8,128)}, f32[128,512]{1,0:T(8,128)S(1)}) custom-call(s32[1,1024]{1,0:T(1,128)S(1)} %get-tuple-element.36.index, s32[4]{0:T(128)S(1)} %pad_add_fusion.where, f32[4096,512]{1,0:T(8,128)S(1)} %copy-done), custom_call_target="tpu_custom_call" | custom-call | bytes 6291456 | tf_op jit(solution)/shard_map/gather_rows/pallas_call | solution.py:153
  9.8 2.7 %collective-permute-start.17 = (f32[128,512]{1,0:T(8,128)}, f32[128,512]{1,0:T(8,128)}, u32[]{:S(2)}, u32[]{:S(2)}) collective-permute-start(f32[128,512]{1,0:T(8,128)} %get-tuple-element.40), channel_id=1, source_target_pairs={{0,48},{16,0},{32,16},{48,32},{64,112},{80,64},{96,80},{112,96},{1... | collective-permute-start | bytes 786440 | tf_op jit(solution)/shard_map/ppermute | solution.py:64
  13.6 2.7 %gather_rows.3 = (f32[128,512]{1,0:T(8,128)S(1)}, f32[128,512]{1,0:T(8,128)S(1)}, f32[128,512]{1,0:T(8,128)S(1)}, f32[128,512]{1,0:T(8,128)S(1)}) custom-call(s32[1,1024]{1,0:T(1,128)S(1)} %get-tuple-element.36.index, s32[4]{0:T(128)S(1)} %pad_add_fusion.where, f32[4096,512]{1,0:T(8,128)S(1)} %copy-done), custom_call_target="tpu_custom_call" | custom-call | bytes 6291456 | tf_op jit(solution)/shard_map/gather_rows/pallas_call | solution.py:153
  16.3 2.1 %collective-permute-start.21 = (f32[128,512]{1,0:T(8,128)S(1)}, f32[128,512]{1,0:T(8,128)}, u32[]{:S(2)}, u32[]{:S(2)}) collective-permute-start(f32[128,512]{1,0:T(8,128)S(1)} %get-tuple-element.44), channel_id=1, source_target_pairs={{0,48},{16,0},{32,16},{48,32},{64,112},{80,64},{96,80},{112,96},{1... | collective-permute-start | bytes 786440 | tf_op jit(solution)/shard_map/ppermute | solution.py:64
  21.1 4.8 %collective-permute-start.19 = (f32[128,512]{1,0:T(8,128)S(1)}, f32[128,512]{1,0:T(8,128)S(1)}, u32[]{:S(2)}, u32[]{:S(2)}) collective-permute-start(f32[128,512]{1,0:T(8,128)S(1)} %get-tuple-element.42), channel_id=1, source_target_pairs={{0,16},{16,32},{32,48},{48,0},{64,80},{80,96},{96,112},{112,64},{1... | collective-permute-start | bytes 786440 | tf_op jit(solution)/shard_map/ppermute | solution.py:64
  25.9 3.9 %collective-permute-done.15 = f32[128,512]{1,0:T(8,128)} collective-permute-done((f32[128,512]{1,0:T(8,128)}, f32[128,512]{1,0:T(8,128)}, u32[]{:S(2)}, u32[]{:S(2)}) %collective-permute-start.15) | collective-permute-done | bytes 262176 | tf_op jit(solution)/shard_map/ppermute | solution.py:64
  31.1 2.5 %collective-permute-start.18 = (f32[128,512]{1,0:T(8,128)S(1)}, f32[128,512]{1,0:T(8,128)S(1)}, u32[]{:S(2)}, u32[]{:S(2)}) collective-permute-start(f32[128,512]{1,0:T(8,128)S(1)} %get-tuple-element.53), channel_id=1, source_target_pairs={{0,64},{1,65},{2,66},{3,67},{4,68},{5,69},{6,70},{7,71},{8,72},{9,... | collective-permute-start | bytes 786440 | tf_op jit(solution)/shard_map/ppermute | solution.py:24
  33.6 5.7 %collective-permute-done.19 = f32[128,512]{1,0:T(8,128)S(1)} collective-permute-done((f32[128,512]{1,0:T(8,128)S(1)}, f32[128,512]{1,0:T(8,128)S(1)}, u32[]{:S(2)}, u32[]{:S(2)}) %collective-permute-start.19) | collective-permute-done | bytes 262176 | tf_op jit(solution)/shard_map/ppermute | solution.py:64
  40.4 2.5 %collective-permute-start.22 = (f32[128,512]{1,0:T(8,128)S(1)}, f32[128,512]{1,0:T(8,128)S(1)}, u32[]{:S(2)}, u32[]{:S(2)}) collective-permute-start(f32[128,512]{1,0:T(8,128)S(1)} %get-tuple-element.55), channel_id=1, source_target_pairs={{0,64},{1,65},{2,66},{3,67},{4,68},{5,69},{6,70},{7,71},{8,72},{9,... | collective-permute-start | bytes 786440 | tf_op jit(solution)/shard_map/ppermute | solution.py:24
  43.1 6.2 %collective-permute-done.22 = f32[128,512]{1,0:T(8,128)S(1)} collective-permute-done((f32[128,512]{1,0:T(8,128)S(1)}, f32[128,512]{1,0:T(8,128)S(1)}, u32[]{:S(2)}, u32[]{:S(2)}) %collective-permute-start.22) | collective-permute-done | bytes 262176 | tf_op jit(solution)/shard_map/ppermute | solution.py:24
  49.5 1.5 collective-permute-start.4
  51.0 3.8 %collective-permute-start.6 = (f32[64,4096]{1,0:T(8,128)S(1)}, f32[64,4096]{1,0:T(8,128)S(1)}, u32[]{:S(2)}, u32[]{:S(2)}) collective-permute-start(f32[64,4096]{1,0:T(8,128)S(1)} %copy-done.1), channel_id=1, source_target_pairs={{0,2},{1,7},{2,4},{3,1},{4,6},{5,3},{6,0},{7,5},{8,10},{9,15},{10,... | collective-permute-start | bytes 3145736 | tf_op jit(solution)/shard_map/ppermute | solution.py:24
  55.7 4.4 %collective-permute-start.29 = (f32[256,512]{1,0:T(8,128)S(1)}, f32[256,512]{1,0:T(8,128)S(1)}, u32[]{:S(2)}, u32[]{:S(2)}) collective-permute-start(f32[256,512]{1,0:T(8,128)S(1)} %pad_maximum_fusion), channel_id=1, source_target_pairs={{0,64},{16,80},{32,96},{48,112},{1,65},{17,81},{33,97},{49,113},{2... | collective-permute-start | bytes 1572872 | tf_op jit(solution)/shard_map/ppermute | solution.py:64
  61.2 1.6 collective-permute-start.8
  62.9 2.2 %collective-permute-start.1 = (f32[64,4096]{1,0:T(8,128)S(1)}, f32[64,4096]{1,0:T(8,128)}, u32[]{:S(2)}, u32[]{:S(2)}) collective-permute-start(f32[64,4096]{1,0:T(8,128)S(1)} %collective-permute-done.refs_2_), channel_id=1, source_target_pairs={{0,2},{1,7},{2,4},{3,1},{4,6},{5,3},{6,0},{7,5},{8,10},{9,15},{10,... | collective-permute-start | bytes 3145736 | tf_op jit(solution)/shard_map/ppermute | solution.py:24
  66.3 8.4 %collective-permute-done.26.refs_5_ = f32[128,512]{1,0:T(8,128)S(1)} collective-permute-done((f32[128,512]{1,0:T(8,128)S(1)}, f32[128,512]{1,0:T(8,128)S(1)}, u32[]{:S(2)}, u32[]{:S(2)}) %collective-permute-start.26) | collective-permute-done | bytes 262176 | tf_op jit(solution)/shard_map/ppermute | solution.py:24
  75.4 4.3 %collective-permute-start.30 = (f32[256,512]{1,0:T(8,128)S(1)}, f32[256,512]{1,0:T(8,128)S(1)}, u32[]{:S(2)}, u32[]{:S(2)}) collective-permute-start(f32[256,512]{1,0:T(8,128)S(1)} %broadcast_select_fusion.refs_0_), channel_id=1, source_target_pairs={{0,16},{1,49},{2,18},{3,51},{4,20},{5,53},{6,22},{7,55},{8,24},{9,... | collective-permute-start | bytes 1572872 | tf_op jit(solution)/shard_map/ppermute | solution.py:24
  82.2 6.6 %collective-permute-done.8.refs_6_ = f32[64,4096]{1,0:T(8,128)} collective-permute-done((f32[64,4096]{1,0:T(8,128)S(1)}, f32[64,4096]{1,0:T(8,128)}, u32[]{:S(2)}, u32[]{:S(2)}) %collective-permute-start.8) | collective-permute-done | bytes 1048608 | tf_op jit(solution)/shard_map/ppermute | solution.py:24
  90.2 3.3 %collective-permute-start.7 = (f32[64,4096]{1,0:T(8,128)S(1)}, f32[64,4096]{1,0:T(8,128)S(1)}, u32[]{:S(2)}, u32[]{:S(2)}) collective-permute-start(f32[64,4096]{1,0:T(8,128)S(1)} %collective-permute-done.6.refs_4_), channel_id=1, source_target_pairs={{0,1},{1,0},{2,3},{3,2},{4,5},{5,4},{6,7},{7,6},{8,9},{9,8},{10,11... | collective-permute-start | bytes 3145736 | tf_op jit(solution)/shard_map/ppermute | solution.py:24
  94.1 3.9 %collective-permute-start.11 = (f32[64,4096]{1,0:T(8,128)S(1)}, f32[64,4096]{1,0:T(8,128)}, u32[]{:S(2)}, u32[]{:S(2)}) collective-permute-start(f32[64,4096]{1,0:T(8,128)S(1)} %collective-permute-done.refs_2_), channel_id=1, source_target_pairs={{0,6},{1,3},{2,0},{3,5},{4,2},{5,7},{6,4},{7,1},{8,14},{9,11},{10,... | collective-permute-start | bytes 3145736 | tf_op jit(solution)/shard_map/ppermute | solution.py:24
  98.1 1.8 collective-permute-start.13
  105.5 12.6 %collective-permute-done.11.refs_10_ = f32[64,4096]{1,0:T(8,128)} collective-permute-done((f32[64,4096]{1,0:T(8,128)S(1)}, f32[64,4096]{1,0:T(8,128)}, u32[]{:S(2)}, u32[]{:S(2)}) %collective-permute-start.11) | collective-permute-done | bytes 1048608 | tf_op jit(solution)/shard_map/ppermute | solution.py:24
  118.1 7.6 %collective-permute-start.12 = (f32[64,4096]{1,0:T(8,128)}, f32[64,4096]{1,0:T(8,128)}, u32[]{:S(2)}, u32[]{:S(2)}) collective-permute-start(f32[64,4096]{1,0:T(8,128)} %collective-permute-done.11.refs_10_), channel_id=1, source_target_pairs={{0,1},{1,0},{2,3},{3,2},{4,5},{5,4},{6,7},{7,6},{8,9},{9,8},{10,11... | collective-permute-start | bytes 3145736 | tf_op jit(solution)/shard_map/ppermute | solution.py:24
  125.8 9.0 %collective-permute-done.2.refs_0_ = f32[64,4096]{1,0:T(8,128)} collective-permute-done((f32[64,4096]{1,0:T(8,128)}, f32[64,4096]{1,0:T(8,128)}, u32[]{:S(2)}, u32[]{:S(2)}) %collective-permute-start.2) | collective-permute-done | bytes 1048608 | tf_op jit(solution)/shard_map/ppermute | solution.py:24
  135.3 4.4 %sort.31 = (s32[1024]{0:T(1024)S(1)}, s32[1024]{0:T(1024)S(1)}, s32[1024]{0:T(1024)S(1)}, s32[1024]{0:T(1024)}) sort(s32[1024]{0:T(1024)S(1)} %subtract_select_fusion, s32[1024]{0:T(1024)S(1)} %fusion.9, s32[1024]{0:T(1024)S(1)} %bitcast.25, s32[1024]{0:T(1024)S(1)} %iota.15), dimensions={0}, to_apply=%region_1.2 | sort | flops 10240 | bytes 32768 | tf_op jit(solution)/shard_map/sort | solution.py:394
  145.8 2.7 %collective-permute-start.32 = (f32[256,512]{1,0:T(8,128)}, f32[256,512]{1,0:T(8,128)S(1)}, u32[]{:S(2)}, u32[]{:S(2)}) collective-permute-start(f32[256,512]{1,0:T(8,128)} %copy-done.12), channel_id=1, source_target_pairs={{0,16},{1,49},{2,18},{3,51},{4,20},{5,53},{6,22},{7,55},{8,24},{9,... | collective-permute-start | bytes 1572872 | tf_op jit(solution)/shard_map/ppermute | solution.py:24
  154.6 7.2 %shard_map.37 = (bf16[1024,4096]{1,0:T(8,128)(2,1)S(1)}, bf16[1024,4096]{1,0:T(8,128)(2,1)S(1)}) custom-call(f32[64,4096]{1,0:T(8,128)S(1)} %copy-done.1, f32[64,4096]{1,0:T(8,128)S(1)} %copy-done.5, f32[64,4096]{1,0:T(8,128)S(1)} %copy-done.3, f32[64,4096]{1,0:T(8,128)S(1)} %copy-done.9, f32[64,4096]{1,0:T(8,128)S(1)} %copy-done.7, ...), custom_call_target="tpu_custom_call" | custom-call | bytes 14680064 | tf_op jit(solution)/shard_map/pallas_call | solution.py:218
  161.8 2.0 %shard_map.38 = (bf16[1024,4096]{1,0:T(8,128)(2,1)S(1)}, bf16[1024,4096]{1,0:T(8,128)(2,1)S(1)}) custom-call(f32[64,4096]{1,0:T(8,128)} %collective-permute-done.2.refs_0_, f32[64,4096]{1,0:T(8,128)} %collective-permute-done.3.refs_1_, bf16[1024,4096]{1,0:T(8,128)(2,1)S(1)} %get-tuple-element.32.refs_2_, ...), custom_call_target="tpu_custom_call", output_to_operand_aliasing={{0}: (2, {}), {1}: (3, {})} | custom-call | bytes 2097152 | tf_op jit(solution)/shard_map/pallas_call | solution.py:218
  164.7 8.6 %update_left.1._ = f32[2048,512]{1,0:T(8,128)S(1)} custom-call(s32[19]{0:T(128)S(1)} %stack.91.order, s32[9]{0:T(128)S(1)} %convert_reduce_fusion.starts, s32[1024]{0:T(1024)S(1)} %get-tuple-element.29.keys, s32[1024]{0:T(1024)S(1)} %get-tuple-element.30.spares, bf16[1024,4096]{1,0:T(8,128)(2,1)S(1)} %get-tuple-element.34.ph, ...), custom_call_target="tpu_custom_call" | custom-call | flops 6442450944 | bytes 1048576 | tf_op jit(solution)/shard_map/update_left/pallas_call | solution.py:253
  173.3 10.4 %update_right.1 = (f32[4096,512]{1,0:T(8,128)}, f32[2048,512]{1,0:T(8,128)S(1)}) custom-call(s32[19]{0:T(128)S(1)} %stack.91.order, s32[9]{0:T(128)S(1)} %convert_reduce_fusion.starts, s32[1024]{0:T(1024)S(1)} %get-tuple-element.29.keys, s32[1024]{0:T(1024)S(1)} %get-tuple-element.30.spares, ...), custom_call_target="tpu_custom_call", output_to_operand_aliasing={{1}: (10, {})} | custom-call | flops 6442450944 | bytes 8388608 | tf_op jit(solution)/shard_map/update_right/pallas_call | solution.py:311
  (116 shorter events, 35.9 us)
Async XLA Ops:
  0.0 62.9 %collective-permute-start = (f32[64,4096]{1,0:T(8,128)}, f32[64,4096]{1,0:T(8,128)S(1)}, u32[]{:S(2)}, u32[]{:S(2)}) collective-permute-start(f32[64,4096]{1,0:T(8,128)} %refs_0_.1), channel_id=1, source_target_pairs={{0,8},{1,9},{2,10},{3,11},{4,12},{5,13},{6,14},{7,15},{8,0},{9,1},... | collective-permute-start | bytes 3145736 | tf_op jit(solution)/shard_map/ppermute | solution.py:24
  9.8 8.8 %collective-permute-start.17 = (f32[128,512]{1,0:T(8,128)}, f32[128,512]{1,0:T(8,128)}, u32[]{:S(2)}, u32[]{:S(2)}) collective-permute-start(f32[128,512]{1,0:T(8,128)} %get-tuple-element.40), channel_id=1, source_target_pairs={{0,48},{16,0},{32,16},{48,32},{64,112},{80,64},{96,80},{112,96},{1... | collective-permute-start | bytes 786440 | tf_op jit(solution)/shard_map/ppermute | solution.py:64
  12.6 8.5 %collective-permute-start.16 = (f32[128,512]{1,0:T(8,128)}, f32[128,512]{1,0:T(8,128)}, u32[]{:S(2)}, u32[]{:S(2)}) collective-permute-start(f32[128,512]{1,0:T(8,128)} %get-tuple-element.39), channel_id=1, source_target_pairs={{0,32},{16,48},{32,0},{48,16},{64,96},{80,112},{96,64},{112,80},{1... | collective-permute-start | bytes 786440 | tf_op jit(solution)/shard_map/ppermute | solution.py:64
  12.9 16.9 %collective-permute-start.15 = (f32[128,512]{1,0:T(8,128)}, f32[128,512]{1,0:T(8,128)}, u32[]{:S(2)}, u32[]{:S(2)}) collective-permute-start(f32[128,512]{1,0:T(8,128)} %get-tuple-element.38), channel_id=1, source_target_pairs={{0,16},{16,32},{32,48},{48,0},{64,80},{80,96},{96,112},{112,64},{1... | collective-permute-start | bytes 786440 | tf_op jit(solution)/shard_map/ppermute | solution.py:64
  16.3 17.3 %collective-permute-start.21 = (f32[128,512]{1,0:T(8,128)S(1)}, f32[128,512]{1,0:T(8,128)}, u32[]{:S(2)}, u32[]{:S(2)}) collective-permute-start(f32[128,512]{1,0:T(8,128)S(1)} %get-tuple-element.44), channel_id=1, source_target_pairs={{0,48},{16,0},{32,16},{48,32},{64,112},{80,64},{96,80},{112,96},{1... | collective-permute-start | bytes 786440 | tf_op jit(solution)/shard_map/ppermute | solution.py:64
  18.6 15.0 %collective-permute-start.20 = (f32[128,512]{1,0:T(8,128)S(1)}, f32[128,512]{1,0:T(8,128)S(1)}, u32[]{:S(2)}, u32[]{:S(2)}) collective-permute-start(f32[128,512]{1,0:T(8,128)S(1)} %get-tuple-element.43), channel_id=1, source_target_pairs={{0,32},{16,48},{32,0},{48,16},{64,96},{80,112},{96,64},{112,80},{1... | collective-permute-start | bytes 786440 | tf_op jit(solution)/shard_map/ppermute | solution.py:64
  21.1 18.2 %collective-permute-start.19 = (f32[128,512]{1,0:T(8,128)S(1)}, f32[128,512]{1,0:T(8,128)S(1)}, u32[]{:S(2)}, u32[]{:S(2)}) collective-permute-start(f32[128,512]{1,0:T(8,128)S(1)} %get-tuple-element.42), channel_id=1, source_target_pairs={{0,16},{16,32},{32,48},{48,0},{64,80},{80,96},{96,112},{112,64},{1... | collective-permute-start | bytes 786440 | tf_op jit(solution)/shard_map/ppermute | solution.py:64
  31.1 11.9 %collective-permute-start.18 = (f32[128,512]{1,0:T(8,128)S(1)}, f32[128,512]{1,0:T(8,128)S(1)}, u32[]{:S(2)}, u32[]{:S(2)}) collective-permute-start(f32[128,512]{1,0:T(8,128)S(1)} %get-tuple-element.53), channel_id=1, source_target_pairs={{0,64},{1,65},{2,66},{3,67},{4,68},{5,69},{6,70},{7,71},{8,72},{9,... | collective-permute-start | bytes 786440 | tf_op jit(solution)/shard_map/ppermute | solution.py:24
  40.4 8.9 %collective-permute-start.22 = (f32[128,512]{1,0:T(8,128)S(1)}, f32[128,512]{1,0:T(8,128)S(1)}, u32[]{:S(2)}, u32[]{:S(2)}) collective-permute-start(f32[128,512]{1,0:T(8,128)S(1)} %get-tuple-element.55), channel_id=1, source_target_pairs={{0,64},{1,65},{2,66},{3,67},{4,68},{5,69},{6,70},{7,71},{8,72},{9,... | collective-permute-start | bytes 786440 | tf_op jit(solution)/shard_map/ppermute | solution.py:24
  43.0 8.0 %collective-permute-start.23 = (f32[128,512]{1,0:T(8,128)S(1)}, f32[128,512]{1,0:T(8,128)S(1)}, u32[]{:S(2)}, u32[]{:S(2)}) collective-permute-start(f32[128,512]{1,0:T(8,128)S(1)} %add.394.refs_0_), channel_id=1, source_target_pairs={{0,16},{1,49},{2,18},{3,51},{4,20},{5,53},{6,22},{7,55},{8,24},{9,... | collective-permute-start | bytes 786440 | tf_op jit(solution)/shard_map/ppermute | solution.py:24
  49.5 30.3 %collective-permute-start.4 = (f32[64,4096]{1,0:T(8,128)S(1)}, f32[64,4096]{1,0:T(8,128)S(1)}, u32[]{:S(2)}, u32[]{:S(2)}) collective-permute-start(f32[64,4096]{1,0:T(8,128)S(1)} %copy-done.1), channel_id=1, source_target_pairs={{0,1},{1,0},{2,3},{3,2},{4,5},{5,4},{6,7},{7,6},{8,9},{9,8},{10,11... | collective-permute-start | bytes 3145736 | tf_op jit(solution)/shard_map/ppermute | solution.py:24
  51.0 9.5 %collective-permute-start.25 = (f32[128,512]{1,0:T(8,128)S(1)}, f32[128,512]{1,0:T(8,128)S(1)}, u32[]{:S(2)}, u32[]{:S(2)}) collective-permute-start(f32[128,512]{1,0:T(8,128)S(1)} %add.394.refs_0_), channel_id=1, source_target_pairs={{0,48},{1,17},{2,50},{3,19},{4,52},{5,21},{6,54},{7,23},{8,56},{9,... | collective-permute-start | bytes 786440 | tf_op jit(solution)/shard_map/ppermute | solution.py:24
  51.0 31.2 %collective-permute-start.6 = (f32[64,4096]{1,0:T(8,128)S(1)}, f32[64,4096]{1,0:T(8,128)S(1)}, u32[]{:S(2)}, u32[]{:S(2)}) collective-permute-start(f32[64,4096]{1,0:T(8,128)S(1)} %copy-done.1), channel_id=1, source_target_pairs={{0,2},{1,7},{2,4},{3,1},{4,6},{5,3},{6,0},{7,5},{8,10},{9,15},{10,... | collective-permute-start | bytes 3145736 | tf_op jit(solution)/shard_map/ppermute | solution.py:24
  55.7 10.5 %collective-permute-start.29 = (f32[256,512]{1,0:T(8,128)S(1)}, f32[256,512]{1,0:T(8,128)S(1)}, u32[]{:S(2)}, u32[]{:S(2)}) collective-permute-start(f32[256,512]{1,0:T(8,128)S(1)} %pad_maximum_fusion), channel_id=1, source_target_pairs={{0,64},{16,80},{32,96},{48,112},{1,65},{17,81},{33,97},{49,113},{2... | collective-permute-start | bytes 1572872 | tf_op jit(solution)/shard_map/ppermute | solution.py:64
  61.2 27.6 %collective-permute-start.8 = (f32[64,4096]{1,0:T(8,128)S(1)}, f32[64,4096]{1,0:T(8,128)}, u32[]{:S(2)}, u32[]{:S(2)}) collective-permute-start(f32[64,4096]{1,0:T(8,128)S(1)} %copy-done.1), channel_id=1, source_target_pairs={{0,6},{1,3},{2,0},{3,5},{4,2},{5,7},{6,4},{7,1},{8,14},{9,11},{10,... | collective-permute-start | bytes 3145736 | tf_op jit(solution)/shard_map/ppermute | solution.py:24
  62.9 38.1 %collective-permute-start.1 = (f32[64,4096]{1,0:T(8,128)S(1)}, f32[64,4096]{1,0:T(8,128)}, u32[]{:S(2)}, u32[]{:S(2)}) collective-permute-start(f32[64,4096]{1,0:T(8,128)S(1)} %collective-permute-done.refs_2_), channel_id=1, source_target_pairs={{0,2},{1,7},{2,4},{3,1},{4,6},{5,3},{6,0},{7,5},{8,10},{9,15},{10,... | collective-permute-start | bytes 3145736 | tf_op jit(solution)/shard_map/ppermute | solution.py:24
  66.2 8.5 %collective-permute-start.26 = (f32[128,512]{1,0:T(8,128)S(1)}, f32[128,512]{1,0:T(8,128)S(1)}, u32[]{:S(2)}, u32[]{:S(2)}) collective-permute-start(f32[128,512]{1,0:T(8,128)S(1)} %add.400.refs_1_), channel_id=1, source_target_pairs={{0,48},{1,17},{2,50},{3,19},{4,52},{5,21},{6,54},{7,23},{8,56},{9,... | collective-permute-start | bytes 786440 | tf_op jit(solution)/shard_map/ppermute | solution.py:24
  75.4 22.6 %collective-permute-start.30 = (f32[256,512]{1,0:T(8,128)S(1)}, f32[256,512]{1,0:T(8,128)S(1)}, u32[]{:S(2)}, u32[]{:S(2)}) collective-permute-start(f32[256,512]{1,0:T(8,128)S(1)} %broadcast_select_fusion.refs_0_), channel_id=1, source_target_pairs={{0,16},{1,49},{2,18},{3,51},{4,20},{5,53},{6,22},{7,55},{8,24},{9,... | collective-permute-start | bytes 1572872 | tf_op jit(solution)/shard_map/ppermute | solution.py:24
  80.7 8.7 %collective-permute-start.27 = (f32[128,512]{1,0:T(8,128)S(1)}, f32[128,512]{1,0:T(8,128)S(1)}, u32[]{:S(2)}, u32[]{:S(2)}) collective-permute-start(f32[128,512]{1,0:T(8,128)S(1)} %collective-permute-done.23.refs_2_), channel_id=1, source_target_pairs={{0,16},{1,49},{2,18},{3,51},{4,20},{5,53},{6,22},{7,55},{8,24},{9,... | collective-permute-start | bytes 786440 | tf_op jit(solution)/shard_map/ppermute | solution.py:24
  82.2 11.2 %collective-permute-start.28 = (f32[128,512]{1,0:T(8,128)S(1)}, f32[128,512]{1,0:T(8,128)S(1)}, u32[]{:S(2)}, u32[]{:S(2)}) collective-permute-start(f32[128,512]{1,0:T(8,128)S(1)} %collective-permute-done.24.refs_3_), channel_id=1, source_target_pairs={{0,16},{1,49},{2,18},{3,51},{4,20},{5,53},{6,22},{7,55},{8,24},{9,... | collective-permute-start | bytes 786440 | tf_op jit(solution)/shard_map/ppermute | solution.py:24
  88.8 13.5 %collective-permute-start.5 = (f32[64,4096]{1,0:T(8,128)S(1)}, f32[64,4096]{1,0:T(8,128)S(1)}, u32[]{:S(2)}, u32[]{:S(2)}) collective-permute-start(f32[64,4096]{1,0:T(8,128)S(1)} %collective-permute-done.refs_2_), channel_id=1, source_target_pairs={{0,1},{1,0},{2,3},{3,2},{4,5},{5,4},{6,7},{7,6},{8,9},{9,8},{10,11... | collective-permute-start | bytes 3145736 | tf_op jit(solution)/shard_map/ppermute | solution.py:24
  90.2 14.3 %collective-permute-start.7 = (f32[64,4096]{1,0:T(8,128)S(1)}, f32[64,4096]{1,0:T(8,128)S(1)}, u32[]{:S(2)}, u32[]{:S(2)}) collective-permute-start(f32[64,4096]{1,0:T(8,128)S(1)} %collective-permute-done.6.refs_4_), channel_id=1, source_target_pairs={{0,1},{1,0},{2,3},{3,2},{4,5},{5,4},{6,7},{7,6},{8,9},{9,8},{10,11... | collective-permute-start | bytes 3145736 | tf_op jit(solution)/shard_map/ppermute | solution.py:24
  94.1 24.0 %collective-permute-start.11 = (f32[64,4096]{1,0:T(8,128)S(1)}, f32[64,4096]{1,0:T(8,128)}, u32[]{:S(2)}, u32[]{:S(2)}) collective-permute-start(f32[64,4096]{1,0:T(8,128)S(1)} %collective-permute-done.refs_2_), channel_id=1, source_target_pairs={{0,6},{1,3},{2,0},{3,5},{4,2},{5,7},{6,4},{7,1},{8,14},{9,11},{10,... | collective-permute-start | bytes 3145736 | tf_op jit(solution)/shard_map/ppermute | solution.py:24
  98.1 27.6 %collective-permute-start.13 = (f32[64,4096]{1,0:T(8,128)S(1)}, f32[64,4096]{1,0:T(8,128)}, u32[]{:S(2)}, u32[]{:S(2)}) collective-permute-start(f32[64,4096]{1,0:T(8,128)S(1)} %collective-permute-done.6.refs_4_), channel_id=1, source_target_pairs={{0,2},{1,7},{2,4},{3,1},{4,6},{5,3},{6,0},{7,5},{8,10},{9,15},{10,... | collective-permute-start | bytes 3145736 | tf_op jit(solution)/shard_map/ppermute | solution.py:24
  100.9 33.9 %collective-permute-start.2 = (f32[64,4096]{1,0:T(8,128)}, f32[64,4096]{1,0:T(8,128)}, u32[]{:S(2)}, u32[]{:S(2)}) collective-permute-start(f32[64,4096]{1,0:T(8,128)} %collective-permute-done.1.refs_8_), channel_id=1, source_target_pairs={{0,2},{1,7},{2,4},{3,1},{4,6},{5,3},{6,0},{7,5},{8,10},{9,15},{10,... | collective-permute-start | bytes 3145736 | tf_op jit(solution)/shard_map/ppermute | solution.py:24
  103.3 42.4 %collective-permute-start.9 = (f32[64,4096]{1,0:T(8,128)}, f32[64,4096]{1,0:T(8,128)}, u32[]{:S(2)}, u32[]{:S(2)}) collective-permute-start(f32[64,4096]{1,0:T(8,128)} %collective-permute-done.8.refs_6_), channel_id=1, source_target_pairs={{0,1},{1,0},{2,3},{3,2},{4,5},{5,4},{6,7},{7,6},{8,9},{9,8},{10,11... | collective-permute-start | bytes 3145736 | tf_op jit(solution)/shard_map/ppermute | solution.py:24
  105.5 40.3 %collective-permute-start.10 = (f32[64,4096]{1,0:T(8,128)}, f32[64,4096]{1,0:T(8,128)}, u32[]{:S(2)}, u32[]{:S(2)}) collective-permute-start(f32[64,4096]{1,0:T(8,128)} %collective-permute-done.1.refs_8_), channel_id=1, source_target_pairs={{0,1},{1,0},{2,3},{3,2},{4,5},{5,4},{6,7},{7,6},{8,9},{9,8},{10,11... | collective-permute-start | bytes 3145736 | tf_op jit(solution)/shard_map/ppermute | solution.py:24
  118.1 30.4 %collective-permute-start.12 = (f32[64,4096]{1,0:T(8,128)}, f32[64,4096]{1,0:T(8,128)}, u32[]{:S(2)}, u32[]{:S(2)}) collective-permute-start(f32[64,4096]{1,0:T(8,128)} %collective-permute-done.11.refs_10_), channel_id=1, source_target_pairs={{0,1},{1,0},{2,3},{3,2},{4,5},{5,4},{6,7},{7,6},{8,9},{9,8},{10,11... | collective-permute-start | bytes 3145736 | tf_op jit(solution)/shard_map/ppermute | solution.py:24
  125.7 22.8 %collective-permute-start.14 = (f32[64,4096]{1,0:T(8,128)}, f32[64,4096]{1,0:T(8,128)}, u32[]{:S(2)}, u32[]{:S(2)}) collective-permute-start(f32[64,4096]{1,0:T(8,128)} %collective-permute-done.13.refs_12_), channel_id=1, source_target_pairs={{0,1},{1,0},{2,3},{3,2},{4,5},{5,4},{6,7},{7,6},{8,9},{9,8},{10,11... | collective-permute-start | bytes 3145736 | tf_op jit(solution)/shard_map/ppermute | solution.py:24
  134.8 27.0 %collective-permute-start.3 = (f32[64,4096]{1,0:T(8,128)}, f32[64,4096]{1,0:T(8,128)}, u32[]{:S(2)}, u32[]{:S(2)}) collective-permute-start(f32[64,4096]{1,0:T(8,128)} %collective-permute-done.2.refs_0_), channel_id=1, source_target_pairs={{0,1},{1,0},{2,3},{3,2},{4,5},{5,4},{6,7},{7,6},{8,9},{9,8},{10,11... | collective-permute-start | bytes 3145736 | tf_op jit(solution)/shard_map/ppermute | solution.py:24
  145.7 27.5 %collective-permute-start.31 = (f32[256,512]{1,0:T(8,128)S(1)}, f32[256,512]{1,0:T(8,128)S(1)}, u32[]{:S(2)}, u32[]{:S(2)}) collective-permute-start(f32[256,512]{1,0:T(8,128)S(1)} %broadcast_select_fusion.refs_0_), channel_id=1, source_target_pairs={{0,48},{1,17},{2,50},{3,19},{4,52},{5,21},{6,54},{7,23},{8,56},{9,... | collective-permute-start | bytes 1572872 | tf_op jit(solution)/shard_map/ppermute | solution.py:24
  145.8 27.4 %collective-permute-start.32 = (f32[256,512]{1,0:T(8,128)}, f32[256,512]{1,0:T(8,128)S(1)}, u32[]{:S(2)}, u32[]{:S(2)}) collective-permute-start(f32[256,512]{1,0:T(8,128)} %copy-done.12), channel_id=1, source_target_pairs={{0,16},{1,49},{2,18},{3,51},{4,20},{5,53},{6,22},{7,55},{8,24},{9,... | collective-permute-start | bytes 1572872 | tf_op jit(solution)/shard_map/ppermute | solution.py:24
  (29 other events, 284.0 us)

commit v5 on v4

--- a/solution.py
+++ b/solution.py
@@ -221,9 +221,30 @@
         out_specs=[VMEM] * 2,
         out_shape=[jax.ShapeDtypeStruct((16 * KP, m), jnp.bfloat16)] * 2,
         input_output_aliases={} if into is None else {n: 0, n + 1: 1},
-        compiler_params=params(12),
-        cost_estimate=pl.CostEstimate(flops=0, bytes_accessed=n << 20, transcendentals=0),
+        compiler_params=params(6),
+        cost_estimate=pl.CostEstimate(flops=(n << 30) if into is None else 0, bytes_accessed=n << 20, transcendentals=0),
     )(*pieces, *([] if into is None else into))
+
+
+def patch_rows(lo, hi, ref, row, change):
+    fours = lax.div(hi - lo, 4)
+
+    def put(ks):
+        rows = [pl.ds(row(k), 1) for k in ks]
+        values = [ref[r, :] + change(k) for r, k in zip(rows, ks)]
+        for r, value in zip(rows, values):
+            ref[r, :] = value
+
+    def four(i, carry):
+        put([lo + 4 * i + u for u in range(4)])
+        return carry
+
+    def one(k, carry):
+        put([k])
+        return carry
+
+    lax.fori_loop(0, fours, four, 0)
+    lax.fori_loop(lo + 4 * fours, hi, one, 0)
 
 
 def update_left(scalars, panel, bh, bl, matrix):
@@ -234,21 +255,26 @@
         root = order[17]
 
         def block_step(block, carry):
-            at = pl.ds(pl.multiple_of(block * MB, MB), MB)
-            in_top = (root == 1) & (block < 1024 // MB)
+            at = pl.ds(pl.multiple_of(block * 2 * MB, 2 * MB), 2 * MB)
+            in_top = (root == 1) & (block < 512 // MB)
             acc = dots(bh[...], bl[...], ph[:, at], pw[:, at])
             out[at, :] = jnp.where(in_top, 0.0, matrix[at, :]) + jnp.where(in_top, 1.0, -1.0) * acc
             return carry
 
-        lax.fori_loop(0, half // MB, block_step, 0)
-
-        def patch(k, carry):
-            r = pl.ds(keys[k], 1)
-            line = jnp.where(root == 1, matrix[pl.ds(spares[k], 1), :], 0.0)
-            out[r, :] += line - matrix[r, :]
-            return carry
-
-        lax.fori_loop(0, starts[half // MB], patch, 0)
+        lax.fori_loop(0, half // MB // 2, block_step, 0)
+
+        end = starts[half // MB]
+
+        @pl.when(root == 1)
+        def _():
+            patch_rows(
+                0, end, out, lambda k: keys[k],
+                lambda k: matrix[pl.ds(spares[k], 1), :] - matrix[pl.ds(keys[k], 1), :],
+            )
+
+        @pl.when(root == 0)
+        def _():
+            patch_rows(0, end, out, lambda k: keys[k], lambda k: -matrix[pl.ds(keys[k], 1), :])
 
     return pl.pallas_call(
         body,
@@ -273,11 +299,7 @@
 
         @pl.when(root == 0)
         def _():
-            def one(k, carry):
-                left[pl.ds(keys[k], 1), :] += disp[pl.ds(slots[k], 1), :]
-                return carry
-
-            lax.fori_loop(0, starts[first], one, 0)
+            patch_rows(0, starts[first], left, lambda k: keys[k], lambda k: disp[pl.ds(slots[k], 1), :])
 
         away = pltpu.make_async_copy(left, out.at[pl.ds(0, first * MB), :], sem)
         away.start()
@@ -288,12 +310,10 @@
             dest[...] = matrix[at, :] - dots(bh[...], bl[...], ph[:, at], pw[:, at])
 
             def patch(source, rows_of):
-                def one(k, carry):
-                    r = keys[k]
-                    dest[pl.ds(r - block * MB, 1), :] += source[pl.ds(rows_of[k], 1), :] - matrix[pl.ds(r, 1), :]
-                    return carry
-
-                lax.fori_loop(starts[block], starts[block + 1], one, 0)
+                patch_rows(
+                    starts[block], starts[block + 1], dest, lambda k: keys[k] - block * MB,
+                    lambda k: source[pl.ds(rows_of[k], 1), :] - matrix[pl.ds(keys[k], 1), :],
+                )
 
             @pl.when(root == 1)
             def _():
@@ -396,7 +416,8 @@
     starts = jnp.sum((key[None, :] < edges[:, None]).astype(jnp.int32), axis=1)
 
     bh, bl = prep(order, [full_a, full_b, a_a, a_b, b_a, b_b, f_a, f_b])
-    panel = load(0, pieces[:14])
+    panel = load(0, pieces[:10])
+    panel = load(10, pieces[10:14], panel)
     panel = load(14, pieces[14:], panel)
     left = update_left((order, starts, keys, spares), panel, bh, bl, matrix)
     return update_right((order, starts, keys, spares, slots), panel, bh, bl, matrix, left, [disp, a_d, b_d, f_d])

time: 185 us -> 164 us (0.89)
  local copies, waits for them, and re-layouts: 20.3 us -> 7.29 us
  starting transfers between devices: 61.8 us -> 54.2 us
    unnamed x56 -> x22, local copies, waits for them, and re-layouts: 20.2 us -> 7.19 us
    ppermute x7, waiting for transfers between devices: 11.9 us -> 21.2 us  [send_row(): return lax.ppermute(value, 'row', row_pairs(dx, dy, keep))]
    ppermute x26, waiting for transfers between devices: 44.1 us -> 35.7 us  [send(): return lax.ppermute(value, ('row', 'col'), torus(step))]
    ppermute x26, starting transfers between devices: 45.4 us -> 41.5 us  [send(): return lax.ppermute(value, ('row', 'col'), torus(step))]
    ppermute x7, starting transfers between devices: 16.4 us -> 12.8 us  [send_row(): return lax.ppermute(value, 'row', row_pairs(dx, dy, keep))]
    pallas_call x2 -> x3, Pallas kernels: 9.18 us -> 10.9 us  [load(): pl.pallas_call(body, in_specs=[HBM] + [ANY] * (n - 1) if into is None els...]
  transfers between devices with their start and end apart: 33 -> 33, of which waited for: 12 -> 13; matrix products, arithmetic and copies ran while one was open for 4% -> 4% of each run, Pallas kernels for 15% -> 14%
where the time goes in v5:
time: 164 us
  waiting for transfers between devices  56.9 us (35%)
  starting transfers between devices  54.2 us (33%)
  Pallas kernels  38.3 us (23%)
  local copies, waits for them, and re-layouts  7.29 us (4%)
  other arithmetic  6.34 us (4%)
    ppermute x26, starting transfers between devices, send(): return lax.ppermute(value, ('row', 'col'), torus(step))  41.5 us
    ppermute x26, waiting for transfers between devices, send(): return lax.ppermute(value, ('row', 'col'), torus(step))  35.7 us
    ppermute x7, waiting for transfers between devices, send_row(): return lax.ppermute(value, 'row', row_pairs(dx, dy, keep))  21.2 us
    ppermute x7, starting transfers between devices, send_row(): return lax.ppermute(value, 'row', row_pairs(dx, dy, keep))  12.8 us
    pallas_call x3, Pallas kernels, load(): pl.pallas_call(body, in_specs=[HBM] + [ANY] * (n - 1) if into is None els...  10.9 us
    pallas_call x1, Pallas kernels, update_right(): pl.pallas_call(body, in_specs=[SMEM] * 5 + [VMEM] * 10, out_specs=[ANY, V...  10.5 us
    pallas_call x1, Pallas kernels, update_left(): pl.pallas_call(body, in_specs=[SMEM] * 4 + [VMEM] * 5, out_specs=VMEM, ou...  7.99 us
    unnamed x22, local copies, waits for them, and re-layouts  7.19 us
  transfers between devices with their start and end apart: 33, of which 13 were waited for; matrix products, arithmetic and copies ran while one was open for 4% of the time, Pallas kernels for 14%

profile of v5, /device:TPU:1, one launch (start us, length us, event | category | flops | bytes accessed | tf_op | source)
XLA Modules:
  0.0 163.7 jit_solution(16789404544329888609)
XLA Ops:
  0.8 2.4 %row_index.1 = (s32[1,1024]{1,0:T(1,128)S(1)}, s32[1,1024]{1,0:T(1,128)S(1)}) custom-call(s32[4]{0:T(128)S(1)} %pad_add_fusion.where, s32[1,1024]{1,0:T(1,128)S(1)} %bitcast.24), custom_call_target="tpu_custom_call" | custom-call | flops 6442450944 | bytes 1048576 | tf_op jit(solution)/shard_map/row_index/pallas_call | solution.py:123
  4.2 2.7 %gather_rows.2 = (f32[128,512]{1,0:T(8,128)S(1)}, f32[128,512]{1,0:T(8,128)S(1)}, f32[128,512]{1,0:T(8,128)S(1)}, f32[128,512]{1,0:T(8,128)S(1)}) custom-call(s32[1,1024]{1,0:T(1,128)S(1)} %get-tuple-element.40.index, s32[4]{0:T(128)S(1)} %pad_add_fusion.where, f32[4096,512]{1,0:T(8,128)S(1)} %copy-done), custom_call_target="tpu_custom_call" | custom-call | bytes 6291456 | tf_op jit(solution)/shard_map/gather_rows/pallas_call | solution.py:153
  6.9 3.6 %collective-permute-start.17 = (f32[128,512]{1,0:T(8,128)S(1)}, f32[128,512]{1,0:T(8,128)S(1)}, u32[]{:S(2)}, u32[]{:S(2)}) collective-permute-start(f32[128,512]{1,0:T(8,128)S(1)} %get-tuple-element.44), channel_id=1, source_target_pairs={{0,48},{16,0},{32,16},{48,32},{64,112},{80,64},{96,80},{112,96},{1... | collective-permute-start | bytes 786440 | tf_op jit(solution)/shard_map/ppermute | solution.py:64
  11.6 2.7 %gather_rows.3 = (f32[128,512]{1,0:T(8,128)S(1)}, f32[128,512]{1,0:T(8,128)S(1)}, f32[128,512]{1,0:T(8,128)S(1)}, f32[128,512]{1,0:T(8,128)S(1)}) custom-call(s32[1,1024]{1,0:T(1,128)S(1)} %get-tuple-element.40.index, s32[4]{0:T(128)S(1)} %pad_add_fusion.where, f32[4096,512]{1,0:T(8,128)S(1)} %copy-done), custom_call_target="tpu_custom_call" | custom-call | bytes 6291456 | tf_op jit(solution)/shard_map/gather_rows/pallas_call | solution.py:153
  17.9 2.1 %collective-permute-done.17 = f32[128,512]{1,0:T(8,128)S(1)} collective-permute-done((f32[128,512]{1,0:T(8,128)S(1)}, f32[128,512]{1,0:T(8,128)S(1)}, u32[]{:S(2)}, u32[]{:S(2)}) %collective-permute-start.17) | collective-permute-done | bytes 262176 | tf_op jit(solution)/shard_map/ppermute | solution.py:64
  20.0 7.3 %collective-permute-done.15 = f32[128,512]{1,0:T(8,128)} collective-permute-done((f32[128,512]{1,0:T(8,128)S(1)}, f32[128,512]{1,0:T(8,128)}, u32[]{:S(2)}, u32[]{:S(2)}) %collective-permute-start.15) | collective-permute-done | bytes 262176 | tf_op jit(solution)/shard_map/ppermute | solution.py:64
  28.4 2.8 %collective-permute-start.18 = (f32[128,512]{1,0:T(8,128)S(1)}, f32[128,512]{1,0:T(8,128)S(1)}, u32[]{:S(2)}, u32[]{:S(2)}) collective-permute-start(f32[128,512]{1,0:T(8,128)S(1)} %get-tuple-element.57), channel_id=1, source_target_pairs={{0,64},{1,65},{2,66},{3,67},{4,68},{5,69},{6,70},{7,71},{8,72},{9,... | collective-permute-start | bytes 786440 | tf_op jit(solution)/shard_map/ppermute | solution.py:24
  32.2 4.8 %collective-permute-done.19 = f32[128,512]{1,0:T(8,128)S(1)} collective-permute-done((f32[128,512]{1,0:T(8,128)S(1)}, f32[128,512]{1,0:T(8,128)S(1)}, u32[]{:S(2)}, u32[]{:S(2)}) %collective-permute-start.19) | collective-permute-done | bytes 262176 | tf_op jit(solution)/shard_map/ppermute | solution.py:64
  37.3 2.8 %collective-permute-start.22 = (f32[128,512]{1,0:T(8,128)S(1)}, f32[128,512]{1,0:T(8,128)S(1)}, u32[]{:S(2)}, u32[]{:S(2)}) collective-permute-start(f32[128,512]{1,0:T(8,128)S(1)} %get-tuple-element.59), channel_id=1, source_target_pairs={{0,64},{1,65},{2,66},{3,67},{4,68},{5,69},{6,70},{7,71},{8,72},{9,... | collective-permute-start | bytes 786440 | tf_op jit(solution)/shard_map/ppermute | solution.py:24
  40.5 5.7 %collective-permute-done.22 = f32[128,512]{1,0:T(8,128)S(1)} collective-permute-done((f32[128,512]{1,0:T(8,128)S(1)}, f32[128,512]{1,0:T(8,128)S(1)}, u32[]{:S(2)}, u32[]{:S(2)}) %collective-permute-start.22) | collective-permute-done | bytes 262176 | tf_op jit(solution)/shard_map/ppermute | solution.py:24
  46.3 3.8 %collective-permute-start.6 = (f32[64,4096]{1,0:T(8,128)}, f32[64,4096]{1,0:T(8,128)}, u32[]{:S(2)}, u32[]{:S(2)}) collective-permute-start(f32[64,4096]{1,0:T(8,128)} %refs_0_.1), channel_id=1, source_target_pairs={{0,2},{1,7},{2,4},{3,1},{4,6},{5,3},{6,0},{7,5},{8,10},{9,15},{10,... | collective-permute-start | bytes 3145736 | tf_op jit(solution)/shard_map/ppermute | solution.py:24
  51.5 2.3 %collective-permute-start.9 = (f32[64,4096]{1,0:T(8,128)}, f32[64,4096]{1,0:T(8,128)S(1)}, u32[]{:S(2)}, u32[]{:S(2)}) collective-permute-start(f32[64,4096]{1,0:T(8,128)} %refs_0_.1), channel_id=1, source_target_pairs={{0,1},{1,0},{2,3},{3,2},{4,5},{5,4},{6,7},{7,6},{8,9},{9,8},{10,11... | collective-permute-start | bytes 3145736 | tf_op jit(solution)/shard_map/ppermute | solution.py:24
  53.8 4.9 %collective-permute-done.25.refs_4_ = f32[128,512]{1,0:T(8,128)S(1)} collective-permute-done((f32[128,512]{1,0:T(8,128)S(1)}, f32[128,512]{1,0:T(8,128)S(1)}, u32[]{:S(2)}, u32[]{:S(2)}) %collective-permute-start.25) | collective-permute-done | bytes 262176 | tf_op jit(solution)/shard_map/ppermute | solution.py:24
  58.8 2.8 %collective-permute-done.26.refs_5_ = f32[128,512]{1,0:T(8,128)S(1)} collective-permute-done((f32[128,512]{1,0:T(8,128)S(1)}, f32[128,512]{1,0:T(8,128)S(1)}, u32[]{:S(2)}, u32[]{:S(2)}) %collective-permute-start.26) | collective-permute-done | bytes 262176 | tf_op jit(solution)/shard_map/ppermute | solution.py:24
  61.6 4.7 %collective-permute-start.29 = (f32[256,512]{1,0:T(8,128)S(1)}, f32[256,512]{1,0:T(8,128)S(1)}, u32[]{:S(2)}, u32[]{:S(2)}) collective-permute-start(f32[256,512]{1,0:T(8,128)S(1)} %pad_maximum_fusion), channel_id=1, source_target_pairs={{0,64},{16,80},{32,96},{48,112},{1,65},{17,81},{33,97},{49,113},{2... | collective-permute-start | bytes 1572872 | tf_op jit(solution)/shard_map/ppermute | solution.py:64
  66.3 2.6 %collective-permute-done.refs_2_ = f32[64,4096]{1,0:T(8,128)} collective-permute-done((f32[64,4096]{1,0:T(8,128)}, f32[64,4096]{1,0:T(8,128)}, u32[]{:S(2)}, u32[]{:S(2)}) %collective-permute-start) | collective-permute-done | bytes 1048608 | tf_op jit(solution)/shard_map/ppermute | solution.py:24
  68.8 3.8 %collective-permute-start.1 = (f32[64,4096]{1,0:T(8,128)}, f32[64,4096]{1,0:T(8,128)}, u32[]{:S(2)}, u32[]{:S(2)}) collective-permute-start(f32[64,4096]{1,0:T(8,128)} %collective-permute-done.refs_2_), channel_id=1, source_target_pairs={{0,2},{1,7},{2,4},{3,1},{4,6},{5,3},{6,0},{7,5},{8,10},{9,15},{10,... | collective-permute-start | bytes 3145736 | tf_op jit(solution)/shard_map/ppermute | solution.py:24
  72.6 6.0 %collective-permute-done.29 = f32[256,512]{1,0:T(8,128)S(1)} collective-permute-done((f32[256,512]{1,0:T(8,128)S(1)}, f32[256,512]{1,0:T(8,128)S(1)}, u32[]{:S(2)}, u32[]{:S(2)}) %collective-permute-start.29) | collective-permute-done | bytes 524320 | tf_op jit(solution)/shard_map/ppermute | solution.py:64
  80.6 2.1 %collective-permute-start.7 = (f32[64,4096]{1,0:T(8,128)}, f32[64,4096]{1,0:T(8,128)}, u32[]{:S(2)}, u32[]{:S(2)}) collective-permute-start(f32[64,4096]{1,0:T(8,128)} %collective-permute-done.6.refs_4_), channel_id=1, source_target_pairs={{0,2},{1,7},{2,4},{3,1},{4,6},{5,3},{6,0},{7,5},{8,10},{9,15},{10,... | collective-permute-start | bytes 3145736 | tf_op jit(solution)/shard_map/ppermute | solution.py:24
  84.4 4.9 %collective-permute-done.27.refs_6_ = f32[128,512]{1,0:T(8,128)S(1)} collective-permute-done((f32[128,512]{1,0:T(8,128)S(1)}, f32[128,512]{1,0:T(8,128)S(1)}, u32[]{:S(2)}, u32[]{:S(2)}) %collective-permute-start.27) | collective-permute-done | bytes 262176 | tf_op jit(solution)/shard_map/ppermute | solution.py:24
  91.2 6.5 %collective-permute-done.28.refs_7_ = f32[128,512]{1,0:T(8,128)S(1)} collective-permute-done((f32[128,512]{1,0:T(8,128)S(1)}, f32[128,512]{1,0:T(8,128)S(1)}, u32[]{:S(2)}, u32[]{:S(2)}) %collective-permute-start.28) | collective-permute-done | bytes 262176 | tf_op jit(solution)/shard_map/ppermute | solution.py:24
  98.4 3.6 %collective-permute-start.10 = (f32[64,4096]{1,0:T(8,128)}, f32[64,4096]{1,0:T(8,128)}, u32[]{:S(2)}, u32[]{:S(2)}) collective-permute-start(f32[64,4096]{1,0:T(8,128)} %collective-permute-done.refs_2_), channel_id=1, source_target_pairs={{0,1},{1,0},{2,3},{3,2},{4,5},{5,4},{6,7},{7,6},{8,9},{9,8},{10,11... | collective-permute-start | bytes 3145736 | tf_op jit(solution)/shard_map/ppermute | solution.py:24
  102.1 3.0 %collective-permute-start.2 = (f32[64,4096]{1,0:T(8,128)}, f32[64,4096]{1,0:T(8,128)}, u32[]{:S(2)}, u32[]{:S(2)}) collective-permute-start(f32[64,4096]{1,0:T(8,128)} %collective-permute-done.1.refs_8_), channel_id=1, source_target_pairs={{0,2},{1,7},{2,4},{3,1},{4,6},{5,3},{6,0},{7,5},{8,10},{9,15},{10,... | collective-permute-start | bytes 3145736 | tf_op jit(solution)/shard_map/ppermute | solution.py:24
  108.2 2.6 %collective-permute-start.14 = (f32[64,4096]{1,0:T(8,128)}, f32[64,4096]{1,0:T(8,128)}, u32[]{:S(2)}, u32[]{:S(2)}) collective-permute-start(f32[64,4096]{1,0:T(8,128)} %collective-permute-done.1.refs_8_), channel_id=1, source_target_pairs={{0,1},{1,0},{2,3},{3,2},{4,5},{5,4},{6,7},{7,6},{8,9},{9,8},{10,11... | collective-permute-start | bytes 3145736 | tf_op jit(solution)/shard_map/ppermute | solution.py:24
  111.6 6.7 %collective-permute-done.2.refs_0_ = f32[64,4096]{1,0:T(8,128)} collective-permute-done((f32[64,4096]{1,0:T(8,128)}, f32[64,4096]{1,0:T(8,128)}, u32[]{:S(2)}, u32[]{:S(2)}) %collective-permute-start.2) | collective-permute-done | bytes 1048608 | tf_op jit(solution)/shard_map/ppermute | solution.py:24
  118.4 3.7 %collective-permute-start.3 = (f32[64,4096]{1,0:T(8,128)}, f32[64,4096]{1,0:T(8,128)}, u32[]{:S(2)}, u32[]{:S(2)}) collective-permute-start(f32[64,4096]{1,0:T(8,128)} %collective-permute-done.2.refs_0_), channel_id=1, source_target_pairs={{0,1},{1,0},{2,3},{3,2},{4,5},{5,4},{6,7},{7,6},{8,9},{9,8},{10,11... | collective-permute-start | bytes 3145736 | tf_op jit(solution)/shard_map/ppermute | solution.py:24
  122.3 4.4 %sort.31 = (s32[1024]{0:T(1024)S(1)}, s32[1024]{0:T(1024)S(1)}, s32[1024]{0:T(1024)S(1)}, s32[1024]{0:T(1024)}) sort(s32[1024]{0:T(1024)S(1)} %subtract_select_fusion, s32[1024]{0:T(1024)S(1)} %fusion.9, s32[1024]{0:T(1024)S(1)} %bitcast.25, s32[1024]{0:T(1024)S(1)} %iota.15), dimensions={0}, to_apply=%region_1.2 | sort | flops 10240 | bytes 32768 | tf_op jit(solution)/shard_map/sort | solution.py:414
  130.0 2.7 %collective-permute-start.32 = (f32[256,512]{1,0:T(8,128)}, f32[256,512]{1,0:T(8,128)S(1)}, u32[]{:S(2)}, u32[]{:S(2)}) collective-permute-start(f32[256,512]{1,0:T(8,128)} %collective-permute-done.30.refs_1_), channel_id=1, source_target_pairs={{0,16},{1,49},{2,18},{3,51},{4,20},{5,53},{6,22},{7,55},{8,24},{9,... | collective-permute-start | bytes 1572872 | tf_op jit(solution)/shard_map/ppermute | solution.py:24
  133.9 6.5 %shard_map.37 = (bf16[1024,4096]{1,0:T(8,128)(2,1)S(1)}, bf16[1024,4096]{1,0:T(8,128)(2,1)S(1)}) custom-call(f32[64,4096]{1,0:T(8,128)} %refs_0_.1, f32[64,4096]{1,0:T(8,128)S(1)} %copy-done.8, f32[64,4096]{1,0:T(8,128)} %collective-permute-done.refs_2_, f32[64,4096]{1,0:T(8,128)} %collective-permute-done.10.refs_3_, ...), custom_call_target="tpu_custom_call" | custom-call | flops 10737418240 | bytes 10485760 | tf_op jit(solution)/shard_map/pallas_call | solution.py:218
  140.5 2.6 %shard_map.38 = (bf16[1024,4096]{1,0:T(8,128)(2,1)S(1)}, bf16[1024,4096]{1,0:T(8,128)(2,1)S(1)}) custom-call(f32[64,4096]{1,0:T(8,128)S(1)} %collective-permute-done.4.refs_0_, f32[64,4096]{1,0:T(8,128)} %collective-permute-done.5.refs_1_, f32[64,4096]{1,0:T(8,128)} %collective-permute-done.7.refs_2_, ...), custom_call_target="tpu_custom_call", output_to_operand_aliasing={{0}: (4, {}), {1}: (5, {})} | custom-call | bytes 4194304 | tf_op jit(solution)/shard_map/pallas_call | solution.py:218
  145.0 8.0 %update_left.1._ = f32[2048,512]{1,0:T(8,128)S(1)} custom-call(s32[19]{0:T(128)S(1)} %stack.91.order, s32[9]{0:T(128)S(1)} %convert_reduce_fusion.starts, s32[1024]{0:T(1024)S(1)} %get-tuple-element.31.keys, s32[1024]{0:T(1024)S(1)} %get-tuple-element.32.spares, bf16[1024,4096]{1,0:T(8,128)(2,1)S(1)} %get-tuple-element.38.ph, ...), custom_call_target="tpu_custom_call" | custom-call | flops 6442450944 | bytes 1048576 | tf_op jit(solution)/shard_map/update_left/pallas_call | solution.py:279
  153.0 10.5 %update_right.1 = (f32[4096,512]{1,0:T(8,128)}, f32[2048,512]{1,0:T(8,128)S(1)}) custom-call(s32[19]{0:T(128)S(1)} %stack.91.order, s32[9]{0:T(128)S(1)} %convert_reduce_fusion.starts, s32[1024]{0:T(1024)S(1)} %get-tuple-element.31.keys, s32[1024]{0:T(1024)S(1)} %get-tuple-element.32.spares, ...), custom_call_target="tpu_custom_call", output_to_operand_aliasing={{1}: (10, {})} | custom-call | flops 6442450944 | bytes 8388608 | tf_op jit(solution)/shard_map/update_right/pallas_call | solution.py:331
  (83 shorter events, 27.3 us)
Async XLA Ops:
  6.9 13.1 %collective-permute-start.17 = (f32[128,512]{1,0:T(8,128)S(1)}, f32[128,512]{1,0:T(8,128)S(1)}, u32[]{:S(2)}, u32[]{:S(2)}) collective-permute-start(f32[128,512]{1,0:T(8,128)S(1)} %get-tuple-element.44), channel_id=1, source_target_pairs={{0,48},{16,0},{32,16},{48,32},{64,112},{80,64},{96,80},{112,96},{1... | collective-permute-start | bytes 786440 | tf_op jit(solution)/shard_map/ppermute | solution.py:64
  10.5 9.5 %collective-permute-start.16 = (f32[128,512]{1,0:T(8,128)S(1)}, f32[128,512]{1,0:T(8,128)S(1)}, u32[]{:S(2)}, u32[]{:S(2)}) collective-permute-start(f32[128,512]{1,0:T(8,128)S(1)} %get-tuple-element.43), channel_id=1, source_target_pairs={{0,32},{16,48},{32,0},{48,16},{64,96},{80,112},{96,64},{112,80},{1... | collective-permute-start | bytes 786440 | tf_op jit(solution)/shard_map/ppermute | solution.py:64
  10.9 16.4 %collective-permute-start.15 = (f32[128,512]{1,0:T(8,128)S(1)}, f32[128,512]{1,0:T(8,128)}, u32[]{:S(2)}, u32[]{:S(2)}) collective-permute-start(f32[128,512]{1,0:T(8,128)S(1)} %get-tuple-element.42), channel_id=1, source_target_pairs={{0,16},{16,32},{32,48},{48,0},{64,80},{80,96},{96,112},{112,64},{1... | collective-permute-start | bytes 786440 | tf_op jit(solution)/shard_map/ppermute | solution.py:64
  14.3 17.9 %collective-permute-start.21 = (f32[128,512]{1,0:T(8,128)S(1)}, f32[128,512]{1,0:T(8,128)S(1)}, u32[]{:S(2)}, u32[]{:S(2)}) collective-permute-start(f32[128,512]{1,0:T(8,128)S(1)} %get-tuple-element.48), channel_id=1, source_target_pairs={{0,48},{16,0},{32,16},{48,32},{64,112},{80,64},{96,80},{112,96},{1... | collective-permute-start | bytes 786440 | tf_op jit(solution)/shard_map/ppermute | solution.py:64
  16.4 15.9 %collective-permute-start.20 = (f32[128,512]{1,0:T(8,128)S(1)}, f32[128,512]{1,0:T(8,128)S(1)}, u32[]{:S(2)}, u32[]{:S(2)}) collective-permute-start(f32[128,512]{1,0:T(8,128)S(1)} %get-tuple-element.47), channel_id=1, source_target_pairs={{0,32},{16,48},{32,0},{48,16},{64,96},{80,112},{96,64},{112,80},{1... | collective-permute-start | bytes 786440 | tf_op jit(solution)/shard_map/ppermute | solution.py:64
  20.0 17.1 %collective-permute-start.19 = (f32[128,512]{1,0:T(8,128)S(1)}, f32[128,512]{1,0:T(8,128)S(1)}, u32[]{:S(2)}, u32[]{:S(2)}) collective-permute-start(f32[128,512]{1,0:T(8,128)S(1)} %get-tuple-element.46), channel_id=1, source_target_pairs={{0,16},{16,32},{32,48},{48,0},{64,80},{80,96},{96,112},{112,64},{1... | collective-permute-start | bytes 786440 | tf_op jit(solution)/shard_map/ppermute | solution.py:64
  28.4 12.0 %collective-permute-start.18 = (f32[128,512]{1,0:T(8,128)S(1)}, f32[128,512]{1,0:T(8,128)S(1)}, u32[]{:S(2)}, u32[]{:S(2)}) collective-permute-start(f32[128,512]{1,0:T(8,128)S(1)} %get-tuple-element.57), channel_id=1, source_target_pairs={{0,64},{1,65},{2,66},{3,67},{4,68},{5,69},{6,70},{7,71},{8,72},{9,... | collective-permute-start | bytes 786440 | tf_op jit(solution)/shard_map/ppermute | solution.py:24
  37.3 8.9 %collective-permute-start.22 = (f32[128,512]{1,0:T(8,128)S(1)}, f32[128,512]{1,0:T(8,128)S(1)}, u32[]{:S(2)}, u32[]{:S(2)}) collective-permute-start(f32[128,512]{1,0:T(8,128)S(1)} %get-tuple-element.59), channel_id=1, source_target_pairs={{0,64},{1,65},{2,66},{3,67},{4,68},{5,69},{6,70},{7,71},{8,72},{9,... | collective-permute-start | bytes 786440 | tf_op jit(solution)/shard_map/ppermute | solution.py:24
  40.1 28.8 %collective-permute-start = (f32[64,4096]{1,0:T(8,128)}, f32[64,4096]{1,0:T(8,128)}, u32[]{:S(2)}, u32[]{:S(2)}) collective-permute-start(f32[64,4096]{1,0:T(8,128)} %refs_0_.1), channel_id=1, source_target_pairs={{0,8},{1,9},{2,10},{3,11},{4,12},{5,13},{6,14},{7,15},{8,0},{9,1},... | collective-permute-start | bytes 3145736 | tf_op jit(solution)/shard_map/ppermute | solution.py:24
  40.4 11.1 %collective-permute-start.23 = (f32[128,512]{1,0:T(8,128)S(1)}, f32[128,512]{1,0:T(8,128)S(1)}, u32[]{:S(2)}, u32[]{:S(2)}) collective-permute-start(f32[128,512]{1,0:T(8,128)S(1)} %add.394.refs_0_), channel_id=1, source_target_pairs={{0,16},{1,49},{2,18},{3,51},{4,20},{5,53},{6,22},{7,55},{8,24},{9,... | collective-permute-start | bytes 786440 | tf_op jit(solution)/shard_map/ppermute | solution.py:24
  46.2 7.6 %collective-permute-start.24 = (f32[128,512]{1,0:T(8,128)S(1)}, f32[128,512]{1,0:T(8,128)S(1)}, u32[]{:S(2)}, u32[]{:S(2)}) collective-permute-start(f32[128,512]{1,0:T(8,128)S(1)} %add.400.refs_1_), channel_id=1, source_target_pairs={{0,16},{1,49},{2,18},{3,51},{4,20},{5,53},{6,22},{7,55},{8,24},{9,... | collective-permute-start | bytes 786440 | tf_op jit(solution)/shard_map/ppermute | solution.py:24
  46.3 34.3 %collective-permute-start.6 = (f32[64,4096]{1,0:T(8,128)}, f32[64,4096]{1,0:T(8,128)}, u32[]{:S(2)}, u32[]{:S(2)}) collective-permute-start(f32[64,4096]{1,0:T(8,128)} %refs_0_.1), channel_id=1, source_target_pairs={{0,2},{1,7},{2,4},{3,1},{4,6},{5,3},{6,0},{7,5},{8,10},{9,15},{10,... | collective-permute-start | bytes 3145736 | tf_op jit(solution)/shard_map/ppermute | solution.py:24
  50.1 8.6 %collective-permute-start.25 = (f32[128,512]{1,0:T(8,128)S(1)}, f32[128,512]{1,0:T(8,128)S(1)}, u32[]{:S(2)}, u32[]{:S(2)}) collective-permute-start(f32[128,512]{1,0:T(8,128)S(1)} %add.394.refs_0_), channel_id=1, source_target_pairs={{0,48},{1,17},{2,50},{3,19},{4,52},{5,21},{6,54},{7,23},{8,56},{9,... | collective-permute-start | bytes 786440 | tf_op jit(solution)/shard_map/ppermute | solution.py:24
  51.5 31.2 %collective-permute-start.9 = (f32[64,4096]{1,0:T(8,128)}, f32[64,4096]{1,0:T(8,128)S(1)}, u32[]{:S(2)}, u32[]{:S(2)}) collective-permute-start(f32[64,4096]{1,0:T(8,128)} %refs_0_.1), channel_id=1, source_target_pairs={{0,1},{1,0},{2,3},{3,2},{4,5},{5,4},{6,7},{7,6},{8,9},{9,8},{10,11... | collective-permute-start | bytes 3145736 | tf_op jit(solution)/shard_map/ppermute | solution.py:24
  53.8 7.7 %collective-permute-start.26 = (f32[128,512]{1,0:T(8,128)S(1)}, f32[128,512]{1,0:T(8,128)S(1)}, u32[]{:S(2)}, u32[]{:S(2)}) collective-permute-start(f32[128,512]{1,0:T(8,128)S(1)} %add.400.refs_1_), channel_id=1, source_target_pairs={{0,48},{1,17},{2,50},{3,19},{4,52},{5,21},{6,54},{7,23},{8,56},{9,... | collective-permute-start | bytes 786440 | tf_op jit(solution)/shard_map/ppermute | solution.py:24
  58.8 25.0 %collective-permute-start.12 = (f32[64,4096]{1,0:T(8,128)}, f32[64,4096]{1,0:T(8,128)}, u32[]{:S(2)}, u32[]{:S(2)}) collective-permute-start(f32[64,4096]{1,0:T(8,128)} %refs_0_.1), channel_id=1, source_target_pairs={{0,6},{1,3},{2,0},{3,5},{4,2},{5,7},{6,4},{7,1},{8,14},{9,11},{10,... | collective-permute-start | bytes 3145736 | tf_op jit(solution)/shard_map/ppermute | solution.py:24
  61.6 17.0 %collective-permute-start.29 = (f32[256,512]{1,0:T(8,128)S(1)}, f32[256,512]{1,0:T(8,128)S(1)}, u32[]{:S(2)}, u32[]{:S(2)}) collective-permute-start(f32[256,512]{1,0:T(8,128)S(1)} %pad_maximum_fusion), channel_id=1, source_target_pairs={{0,64},{16,80},{32,96},{48,112},{1,65},{17,81},{33,97},{49,113},{2... | collective-permute-start | bytes 1572872 | tf_op jit(solution)/shard_map/ppermute | solution.py:64
  68.8 33.2 %collective-permute-start.1 = (f32[64,4096]{1,0:T(8,128)}, f32[64,4096]{1,0:T(8,128)}, u32[]{:S(2)}, u32[]{:S(2)}) collective-permute-start(f32[64,4096]{1,0:T(8,128)} %collective-permute-done.refs_2_), channel_id=1, source_target_pairs={{0,2},{1,7},{2,4},{3,1},{4,6},{5,3},{6,0},{7,5},{8,10},{9,15},{10,... | collective-permute-start | bytes 3145736 | tf_op jit(solution)/shard_map/ppermute | solution.py:24
  78.6 28.1 %collective-permute-start.4 = (f32[64,4096]{1,0:T(8,128)}, f32[64,4096]{1,0:T(8,128)S(1)}, u32[]{:S(2)}, u32[]{:S(2)}) collective-permute-start(f32[64,4096]{1,0:T(8,128)} %collective-permute-done.refs_2_), channel_id=1, source_target_pairs={{0,6},{1,3},{2,0},{3,5},{4,2},{5,7},{6,4},{7,1},{8,14},{9,11},{10,... | collective-permute-start | bytes 3145736 | tf_op jit(solution)/shard_map/ppermute | solution.py:24
  80.6 27.7 %collective-permute-start.7 = (f32[64,4096]{1,0:T(8,128)}, f32[64,4096]{1,0:T(8,128)}, u32[]{:S(2)}, u32[]{:S(2)}) collective-permute-start(f32[64,4096]{1,0:T(8,128)} %collective-permute-done.6.refs_4_), channel_id=1, source_target_pairs={{0,2},{1,7},{2,4},{3,1},{4,6},{5,3},{6,0},{7,5},{8,10},{9,15},{10,... | collective-permute-start | bytes 3145736 | tf_op jit(solution)/shard_map/ppermute | solution.py:24
  83.8 18.3 %collective-permute-start.30 = (f32[256,512]{1,0:T(8,128)S(1)}, f32[256,512]{1,0:T(8,128)}, u32[]{:S(2)}, u32[]{:S(2)}) collective-permute-start(f32[256,512]{1,0:T(8,128)S(1)} %broadcast_select_fusion.refs_0_), channel_id=1, source_target_pairs={{0,16},{1,49},{2,18},{3,51},{4,20},{5,53},{6,22},{7,55},{8,24},{9,... | collective-permute-start | bytes 1572872 | tf_op jit(solution)/shard_map/ppermute | solution.py:24
  90.0 7.7 %collective-permute-start.28 = (f32[128,512]{1,0:T(8,128)S(1)}, f32[128,512]{1,0:T(8,128)S(1)}, u32[]{:S(2)}, u32[]{:S(2)}) collective-permute-start(f32[128,512]{1,0:T(8,128)S(1)} %collective-permute-done.24.refs_3_), channel_id=1, source_target_pairs={{0,16},{1,49},{2,18},{3,51},{4,20},{5,53},{6,22},{7,55},{8,24},{9,... | collective-permute-start | bytes 786440 | tf_op jit(solution)/shard_map/ppermute | solution.py:24
  98.4 12.6 %collective-permute-start.10 = (f32[64,4096]{1,0:T(8,128)}, f32[64,4096]{1,0:T(8,128)}, u32[]{:S(2)}, u32[]{:S(2)}) collective-permute-start(f32[64,4096]{1,0:T(8,128)} %collective-permute-done.refs_2_), channel_id=1, source_target_pairs={{0,1},{1,0},{2,3},{3,2},{4,5},{5,4},{6,7},{7,6},{8,9},{9,8},{10,11... | collective-permute-start | bytes 3145736 | tf_op jit(solution)/shard_map/ppermute | solution.py:24
  102.1 9.1 %collective-permute-start.11 = (f32[64,4096]{1,0:T(8,128)}, f32[64,4096]{1,0:T(8,128)}, u32[]{:S(2)}, u32[]{:S(2)}) collective-permute-start(f32[64,4096]{1,0:T(8,128)} %collective-permute-done.6.refs_4_), channel_id=1, source_target_pairs={{0,1},{1,0},{2,3},{3,2},{4,5},{5,4},{6,7},{7,6},{8,9},{9,8},{10,11... | collective-permute-start | bytes 3145736 | tf_op jit(solution)/shard_map/ppermute | solution.py:24
  102.1 16.3 %collective-permute-start.2 = (f32[64,4096]{1,0:T(8,128)}, f32[64,4096]{1,0:T(8,128)}, u32[]{:S(2)}, u32[]{:S(2)}) collective-permute-start(f32[64,4096]{1,0:T(8,128)} %collective-permute-done.1.refs_8_), channel_id=1, source_target_pairs={{0,2},{1,7},{2,4},{3,1},{4,6},{5,3},{6,0},{7,5},{8,10},{9,15},{10,... | collective-permute-start | bytes 3145736 | tf_op jit(solution)/shard_map/ppermute | solution.py:24
  106.7 22.9 %collective-permute-start.13 = (f32[64,4096]{1,0:T(8,128)}, f32[64,4096]{1,0:T(8,128)}, u32[]{:S(2)}, u32[]{:S(2)}) collective-permute-start(f32[64,4096]{1,0:T(8,128)} %collective-permute-done.12.refs_6_), channel_id=1, source_target_pairs={{0,1},{1,0},{2,3},{3,2},{4,5},{5,4},{6,7},{7,6},{8,9},{9,8},{10,11... | collective-permute-start | bytes 3145736 | tf_op jit(solution)/shard_map/ppermute | solution.py:24
  108.2 21.7 %collective-permute-start.14 = (f32[64,4096]{1,0:T(8,128)}, f32[64,4096]{1,0:T(8,128)}, u32[]{:S(2)}, u32[]{:S(2)}) collective-permute-start(f32[64,4096]{1,0:T(8,128)} %collective-permute-done.1.refs_8_), channel_id=1, source_target_pairs={{0,1},{1,0},{2,3},{3,2},{4,5},{5,4},{6,7},{7,6},{8,9},{9,8},{10,11... | collective-permute-start | bytes 3145736 | tf_op jit(solution)/shard_map/ppermute | solution.py:24
  111.0 29.4 %collective-permute-start.5 = (f32[64,4096]{1,0:T(8,128)S(1)}, f32[64,4096]{1,0:T(8,128)}, u32[]{:S(2)}, u32[]{:S(2)}) collective-permute-start(f32[64,4096]{1,0:T(8,128)S(1)} %collective-permute-done.4.refs_0_), channel_id=1, source_target_pairs={{0,1},{1,0},{2,3},{3,2},{4,5},{5,4},{6,7},{7,6},{8,9},{9,8},{10,11... | collective-permute-start | bytes 3145736 | tf_op jit(solution)/shard_map/ppermute | solution.py:24
  111.1 29.3 %collective-permute-start.8 = (f32[64,4096]{1,0:T(8,128)}, f32[64,4096]{1,0:T(8,128)}, u32[]{:S(2)}, u32[]{:S(2)}) collective-permute-start(f32[64,4096]{1,0:T(8,128)} %collective-permute-done.7.refs_2_), channel_id=1, source_target_pairs={{0,1},{1,0},{2,3},{3,2},{4,5},{5,4},{6,7},{7,6},{8,9},{9,8},{10,11... | collective-permute-start | bytes 3145736 | tf_op jit(solution)/shard_map/ppermute | solution.py:24
  118.4 24.7 %collective-permute-start.3 = (f32[64,4096]{1,0:T(8,128)}, f32[64,4096]{1,0:T(8,128)}, u32[]{:S(2)}, u32[]{:S(2)}) collective-permute-start(f32[64,4096]{1,0:T(8,128)} %collective-permute-done.2.refs_0_), channel_id=1, source_target_pairs={{0,1},{1,0},{2,3},{3,2},{4,5},{5,4},{6,7},{7,6},{8,9},{9,8},{10,11... | collective-permute-start | bytes 3145736 | tf_op jit(solution)/shard_map/ppermute | solution.py:24
  129.7 23.3 %collective-permute-start.31 = (f32[256,512]{1,0:T(8,128)S(1)}, f32[256,512]{1,0:T(8,128)S(1)}, u32[]{:S(2)}, u32[]{:S(2)}) collective-permute-start(f32[256,512]{1,0:T(8,128)S(1)} %broadcast_select_fusion.refs_0_), channel_id=1, source_target_pairs={{0,48},{1,17},{2,50},{3,19},{4,52},{5,21},{6,54},{7,23},{8,56},{9,... | collective-permute-start | bytes 1572872 | tf_op jit(solution)/shard_map/ppermute | solution.py:24
  130.0 23.0 %collective-permute-start.32 = (f32[256,512]{1,0:T(8,128)}, f32[256,512]{1,0:T(8,128)S(1)}, u32[]{:S(2)}, u32[]{:S(2)}) collective-permute-start(f32[256,512]{1,0:T(8,128)} %collective-permute-done.30.refs_1_), channel_id=1, source_target_pairs={{0,16},{1,49},{2,18},{3,51},{4,20},{5,53},{6,22},{7,55},{8,24},{9,... | collective-permute-start | bytes 1572872 | tf_op jit(solution)/shard_map/ppermute | solution.py:24
  (12 other events, 44.3 us)
